TPU v7x, 512 devices: a whole 4x4x16 slice. The times are simulated.
512 devices in a mesh: dp: 32 (over z, core), expert: 16 (over x, y).
Axes of the slice: x: 4, y: 4, z: 16, core: 2. Of those that a mesh axis runs over, the one named last changes fastest.
Arguments:
- cached_hidden: bfloat16 [65536, 1536], P(('dp', 'expert')), may hold values from -6 to 6
- direction: bfloat16 [16, 2880, 1536], P('expert', 'dp'), may hold values from -1 to 1
- expert_ids: int32 [65536, 4], P(('dp', 'expert')), may hold values from 0 to 127, as said below
- gate_weights: float32 [65536, 4], P(('dp', 'expert')), may hold values from 0.05 to 1
Outputs:
- curvature_product: float32 [16, 2880, 1536], P('expert', 'dp')
Inputs may be any that keep to these rules, and one draw needn't show every extreme that they name: `expert_ids`: each row names 4 different experts, at most two of them below 16. Among the 128 rows of one device no expert below 16 is named more than 8 times; for every dp index, some expert below 16 is named exactly 8 times by the rows of each device with that dp index.
All inputs are finite; a program needn't handle non-finite values.
Results may differ from a plain program's by a relative error of at most 0.0034.
Values may be sent and summed in bfloat16 or wider, within the bound.
No kernel may reach another device: no remote copies, remote signals or barrier semaphores. Data moves between devices by JAX's collectives and lax.ppermute only.
A program may use at most 128 MiB of HBM per device.

v0:
```python
import functools
import math

import jax
import jax.numpy as jnp
from jax import lax
from jax.experimental import pallas as pl
from jax.experimental.pallas import tpu as pltpu
from jax.sharding import PartitionSpec as P


VMEM = pltpu.VMEM
FEATS = 96
TAB = 8
LANES = 128
LIMIT = 24 * 2**20


def whole():
    return pl.BlockSpec(memory_space=VMEM)


def full(x):
    return pl.BlockSpec(x.shape, lambda i: (0,) * x.ndim)


def params():
    return pltpu.CompilerParams(vmem_limit_bytes=LIMIT)


def cost(flops, nbytes):
    return pl.CostEstimate(flops=flops, bytes_accessed=nbytes, transcendentals=0)


def table_kernel(capacity, experts, ids_ref, gates_ref, out_ref):
    topk, tokens = ids_ref.shape
    slots = experts * capacity
    slot = lax.broadcasted_iota(jnp.int32, (slots, tokens), 0)
    expert = slot // capacity
    place = (slot % capacity).astype(jnp.float32)
    named = [ids_ref[k : k + 1, :] == expert for k in range(topk)]
    any_named = functools.reduce(jnp.logical_or, named)
    first = lax.broadcasted_iota(jnp.int32, (tokens, tokens), 0)
    second = lax.broadcasted_iota(jnp.int32, (tokens, tokens), 1)
    earlier = (first < second).astype(jnp.float32).astype(jnp.bfloat16)
    before = jnp.dot(
        any_named.astype(jnp.float32).astype(jnp.bfloat16),
        earlier,
        preferred_element_type=jnp.float32,
    )
    here = before == place
    token = lax.broadcasted_iota(jnp.int32, (1, tokens), 1).astype(jnp.float32)
    total = jnp.zeros((8, slots), jnp.float32)
    for k in range(topk):
        gate = gates_ref[k : k + 1, :]
        high = gate.astype(jnp.bfloat16).astype(jnp.float32)
        middle = (gate - high).astype(jnp.bfloat16).astype(jnp.float32)
        low = gate - high - middle
        rows = jnp.concatenate(
            [token, high, middle, low, jnp.zeros((4, tokens), jnp.float32)], axis=0
        ).astype(jnp.bfloat16)
        holds = jnp.logical_and(named[k], here).astype(jnp.float32).astype(jnp.bfloat16)
        total += lax.dot_general(
            rows, holds, (((1,), (1,)), ((), ())), preferred_element_type=jnp.float32
        )
    out_ref[...] = total.astype(out_ref.dtype)


def slot_table(ids, gates, experts, capacity):
    return pl.pallas_call(
        functools.partial(table_kernel, capacity, experts),
        out_shape=jax.ShapeDtypeStruct((TAB, experts * capacity), jnp.bfloat16),
        in_specs=[whole(), whole()],
        out_specs=whole(),
        compiler_params=params(),
        cost_estimate=cost(10**7, 10**5),
        name="slot_table",
    )(ids.T, gates.T)


def mix_of(table, scale):
    rows = table.astype(jnp.float32)
    slots = rows.shape[1]
    gate = rows[1:2] + rows[2:3] + rows[3:4]
    both = jnp.concatenate([rows[0:1], gate, jnp.zeros((6, slots), jnp.float32)], axis=0)
    columns = both.T
    mix = jnp.where(columns[:, 0:1] == both[0:1], (scale * columns[:, 1:2]) * both[1:2], 0.0)
    high = mix.astype(jnp.bfloat16)
    low = (mix - high.astype(jnp.float32)).astype(jnp.bfloat16)
    return jnp.concatenate([high, low], axis=1)


def project(rows, dirs):
    return lax.dot_general(
        rows, dirs, (((1,), (1,)), ((), ())), preferred_element_type=jnp.float32
    )


def pack(out_ref, values):
    sources = out_ref.shape[0]
    tail = jnp.concatenate([value[:, LANES:] for value in values], axis=1)
    for i, value in enumerate([value[:, :LANES] for value in values] + [tail]):
        out_ref[:, i] = value.reshape(sources, -1, LANES).astype(jnp.bfloat16)


def tangents(pair, pieces, dirs, kept, shape, mix_shape, scale):
    sources, _, capacity, _ = shape
    span = sources * capacity
    spare = pieces[-1].shape[0] - TAB
    n = len(pieces)
    args = list(pieces) + [pieces[-1], dirs] + list(kept)

    def kernel(*refs):
        table_ref, dir_ref = refs[n], refs[n + 1]
        out_ref, mix_ref = refs[-2], refs[-1]
        parts = [refs[i][...] for i in range(n - 1)] + [refs[n - 1][:spare, :]]
        value = project(jnp.concatenate(parts, axis=0), dir_ref[...])
        pack(out_ref, [value[:span], value[span:]])
        for i in range(2):
            mix_ref[i] = mix_of(table_ref[:, i * LANES : (i + 1) * LANES], scale)

    return pl.pallas_call(
        kernel,
        grid=(1,),
        out_shape=[
            jax.ShapeDtypeStruct(shape, jnp.bfloat16),
            jax.ShapeDtypeStruct(mix_shape, jnp.bfloat16),
        ],
        in_specs=[full(x) for x in pieces]
        + [pl.BlockSpec((TAB, 2 * LANES), lambda i: (spare // TAB, 0)), full(dirs)]
        + [pl.BlockSpec(memory_space=pl.ANY)] * len(kept),
        out_specs=[
            pl.BlockSpec((sources, 3, capacity, LANES), lambda i: (0, pair, 0, 0)),
            pl.BlockSpec((2,) + mix_shape[1:], lambda i: (pair, 0, 0)),
        ],
        input_output_aliases={n + 2 + i: i for i in range(len(kept))},
        compiler_params=params(),
        cost_estimate=cost(4 * span * dirs.size, 2 * 2 * span * dirs.shape[1] + 2 * dirs.size),
        name="tangents",
    )(*args)


def own_tangents(rows, dirs):
    def kernel(rows_ref, dir_ref, out_ref):
        out_ref[...] = project(rows_ref[...], dir_ref[...])

    return pl.pallas_call(
        kernel,
        out_shape=jax.ShapeDtypeStruct((rows.shape[0], dirs.shape[0]), jnp.float32),
        in_specs=[whole(), whole()],
        out_specs=whole(),
        compiler_params=params(),
        cost_estimate=cost(2 * rows.shape[0] * dirs.size, 2 * rows.size + 2 * dirs.size),
        name="own_tangents",
    )(rows, dirs)


def last_tangents(pair, own, rows, dirs, packed):
    sources, _, capacity, _ = packed.shape

    def kernel(own_ref, rows_ref, dir_ref, _, out_ref):
        pack(out_ref, [own_ref[...], project(rows_ref[...], dir_ref[...])])

    return pl.pallas_call(
        kernel,
        grid=(1,),
        out_shape=jax.ShapeDtypeStruct(packed.shape, packed.dtype),
        in_specs=[full(x) for x in (own, rows, dirs)] + [pl.BlockSpec(memory_space=pl.ANY)],
        out_specs=pl.BlockSpec((sources, 3, capacity, LANES), lambda i: (0, pair, 0, 0)),
        input_output_aliases={3: 0},
        compiler_params=params(),
        cost_estimate=cost(2 * own.shape[0] * dirs.size, 2 * dirs.size),
        name="last_tangents",
    )(own, rows, dirs, packed)


def combine(packed, mixes, tables, scale):
    experts, slabs, capacity, _ = packed.shape
    slots = experts * capacity

    def kernel(in_ref, mix_ref, *refs):
        out_ref = refs[-1]
        lane = lax.broadcasted_iota(jnp.int32, (slots, LANES), 1)

        def load(slab):
            return in_ref[:, slab].astype(jnp.float32).reshape(slots, LANES).astype(jnp.bfloat16)

        for pair in range(slabs // 3):
            tail = load(3 * pair + 2)
            tails = []
            for i in range(2):
                x = jnp.concatenate([load(3 * pair + i), tail], axis=1)
                here = 2 * pair + i
                if here < mixes.shape[0]:
                    mix = mix_ref[here]
                else:
                    mix = mix_of(refs[i][...], scale)
                y = jnp.dot(
                    mix, jnp.concatenate([x, x], axis=0), preferred_element_type=jnp.float32
                )
                tails.append(y[:, LANES:])
                out_ref[:, 3 * pair + i] = (
                    y[:, :LANES].reshape(experts, capacity, LANES).astype(jnp.bfloat16)
                )
            both = jnp.where(lane < LANES // 2, tails[0], tails[1])
            out_ref[:, 3 * pair + 2] = both.reshape(experts, capacity, LANES).astype(jnp.bfloat16)

    return pl.pallas_call(
        kernel,
        out_shape=jax.ShapeDtypeStruct(packed.shape, packed.dtype),
        in_specs=[whole()] * (2 + len(tables)),
        out_specs=whole(),
        compiler_params=params(),
        cost_estimate=cost(10**9, 4 * packed.size),
        name="combine",
    )(packed, mixes, *tables)


def gradients(packed, groups, feats):
    sources, slabs, capacity, _ = packed.shape
    span = sources * capacity
    pairs = slabs // 3
    width = groups[0][0].shape[1]
    tiles = width // LANES
    step = 2 * LANES
    pieces = [x for group in groups for x in group]

    def kernel(in_ref, *refs):
        own_ref, other_ref, lhs_ref = refs[-3:]
        column = pl.program_id(0)

        @pl.when(column == 0)
        def _():
            def load(slab):
                return in_ref[:, slab].astype(jnp.float32).reshape(span, LANES)

            for pair in range(pairs):
                main = jnp.concatenate([load(3 * pair).T, load(3 * pair + 1).T], axis=1)
                tail = load(3 * pair + 2).T
                tail = jnp.concatenate([tail[: LANES // 2], tail[LANES // 2 :]], axis=1)
                lhs_ref[pair] = jnp.concatenate([main, tail], axis=0).astype(jnp.bfloat16)

        total = None
        at = 0
        for pair, group in enumerate(groups):
            parts = []
            left = 2 * span
            for piece in group:
                rows = min(left, piece.shape[0])
                parts.append(refs[at][:rows, :])
                left -= rows
                at += 1
            term = jnp.dot(
                lhs_ref[pair], jnp.concatenate(parts, axis=0), preferred_element_type=jnp.float32
            )
            total = term if total is None else total + term
        for i in range(2):
            lanes = slice(i * LANES, (i + 1) * LANES)
            rows = pl.ds(2 * column + i, feats, stride=tiles)
            own_ref[rows, :] = total[:feats, lanes]
            other_ref[rows, :] = total[FEATS : FEATS + feats, lanes]

    shape = jax.ShapeDtypeStruct((feats * tiles, LANES), jnp.float32)
    return pl.pallas_call(
        kernel,
        grid=(width // step,),
        out_shape=[shape, shape],
        in_specs=[full(packed)]
        + [pl.BlockSpec((x.shape[0], step), lambda i: (0, i)) for x in pieces],
        out_specs=[pl.BlockSpec(shape.shape, lambda i: (0, 0))] * 2,
        scratch_shapes=[pltpu.VMEM((pairs, 2 * FEATS, 2 * span), jnp.bfloat16)],
        compiler_params=params(),
        cost_estimate=cost(4 * FEATS * 2 * span * pairs * width, 2 * 2 * span * pairs * width),
        name="gradients",
    )(packed, *pieces)


def body(cached_hidden, direction, expert_ids, gate_weights):
    rows = lax.axis_size("dp")
    experts = lax.axis_size("expert")
    span, width = cached_hidden.shape
    capacity = span // experts
    feats = direction.shape[1]
    scale = 1.0 / math.sqrt(expert_ids.shape[0] * rows * experts)
    steps = rows // 4
    ring = [(i, (i + 2) % rows if i % 2 == 0 else (i - 2) % rows) for i in range(rows)]
    partner = [(i, i ^ 1) for i in range(rows)]

    def shift(x):
        return lax.ppermute(x, "dp", ring)

    def swap(x):
        return lax.ppermute(x, "dp", partner)

    chain_a = [shift(cached_hidden)]
    other = swap(cached_hidden)
    table = slot_table(expert_ids, gate_weights, experts, capacity)
    other_table = swap(table)
    chip_table = jnp.concatenate(
        [table, other_table, jnp.zeros((TAB, width - 2 * span), jnp.bfloat16)], axis=1
    )
    chain_b = [shift(jnp.concatenate([other, chip_table], axis=0))]
    other_dir = swap(direction[0])
    pad = jnp.zeros((FEATS - feats, width), jnp.bfloat16)
    dirs = jnp.concatenate([direction[0], pad, other_dir, pad], axis=0)
    for _ in range(2, steps):
        chain_a.append(shift(chain_a[-1]))
        chain_b.append(shift(chain_b[-1]))
    last = shift(chain_a[-1])
    last_table = shift(chain_b[-1][span:, :LANES])
    shape = (experts, 3 * steps, capacity, LANES)
    mix_shape = (2 * (steps - 1), span, 2 * span)
    kept = ()
    groups = []
    for s in range(1, steps):
        pieces = [chain_a[s - 1], chain_b[s - 1]]
        kept = tangents(s - 1, pieces, dirs, kept, shape, mix_shape, scale)
        groups.append(pieces)
    packed, mixes = kept
    own = own_tangents(cached_hidden, dirs)
    packed = last_tangents(steps - 1, own, last, dirs, packed)
    groups.append([cached_hidden, last])
    arrived = lax.all_to_all(packed, "expert", split_axis=0, concat_axis=0, tiled=True)
    adjoint = combine(arrived, mixes, [table, last_table], scale)
    back = lax.all_to_all(adjoint, "expert", split_axis=0, concat_axis=0, tiled=True)
    mine, theirs = gradients(back, groups, feats)
    theirs = swap(theirs)
    return (mine + theirs).reshape(1, feats, width)


def solution(mesh):
    return jax.shard_map(
        body,
        mesh=mesh,
        in_specs=(
            P(("dp", "expert"), None),
            P("expert", "dp", None),
            P(("dp", "expert"), None),
            P(("dp", "expert"), None),
        ),
        out_specs=P("expert", "dp", None),
        check_vma=False,
    )
```

profile of v0, /device:TPU:1, one launch (start us, length us, event | category | flops | bytes accessed | tf_op | source)
XLA Modules:
  0.0 146.9 jit_solution(12073586243003945748)
XLA Ops:
  0.0 8.7 %collective-permute-start.9 = (bf16[128,1536]{1,0:T(8,128)(2,1)}, bf16[128,1536]{1,0:T(8,128)(2,1)S(1)}, u32[]{:S(2)}, u32[]{:S(2)}) collective-permute-start(bf16[128,1536]{1,0:T(8,128)(2,1)} %refs_14_.1), channel_id=1, source_target_pairs={{0,16},{16,0},{32,48},{48,32},{64,80},{80,64},{96,112},{112,96},{1... | collective-permute-start | bytes 1179656 | tf_op jit(solution)/shard_map/ppermute | solution.py:293
  8.8 0.7 copy-done.20
  9.4 0.7 copy-done.21
  10.1 0.3 slot_table.1.refs_0_
  10.4 1.9 %collective-permute-start.10 = (bf16[8,128]{1,0:T(8,128)(2,1)S(1)}, bf16[8,128]{1,0:T(8,128)(2,1)S(1)}, u32[]{:S(2)}, u32[]{:S(2)}) collective-permute-start(bf16[8,128]{1,0:T(8,128)(2,1)S(1)} %slot_table.1.refs_0_), channel_id=1, source_target_pairs={{0,16},{16,0},{32,48},{48,32},{64,80},{80,64},{96,112},{112,96},{1... | collective-permute-start | bytes 6152 | tf_op jit(solution)/shard_map/ppermute | solution.py:293
  12.4 5.8 %collective-permute-start.1 = (bf16[128,1536]{1,0:T(8,128)(2,1)}, bf16[128,1536]{1,0:T(8,128)(2,1)S(1)}, u32[]{:S(2)}, u32[]{:S(2)}) collective-permute-start(bf16[128,1536]{1,0:T(8,128)(2,1)} %refs_14_.1), channel_id=1, source_target_pairs={{0,32},{16,496},{32,64},{48,16},{64,96},{80,48},{96,128},{112,80},... | collective-permute-start | bytes 1179656 | tf_op jit(solution)/shard_map/ppermute | solution.py:290
  18.2 0.0 copy-start.16
  18.2 2.8 %collective-permute-start.11 = (bf16[136,1536]{1,0:T(8,128)(2,1)S(1)}, bf16[136,1536]{1,0:T(8,128)(2,1)S(1)}, u32[]{:S(2)}, u32[]{:S(2)}) collective-permute-start(bf16[136,1536]{1,0:T(8,128)(2,1)S(1)} %maximum_maximum_fusion), channel_id=1, source_target_pairs={{0,32},{16,496},{32,64},{48,16},{64,96},{80,48},{96,128},{112,80},... | collective-permute-start | bytes 1253384 | tf_op jit(solution)/shard_map/ppermute | solution.py:290
  21.0 2.2 %collective-permute-done.1.refs_0_ = bf16[128,1536]{1,0:T(8,128)(2,1)S(1)} collective-permute-done((bf16[128,1536]{1,0:T(8,128)(2,1)}, bf16[128,1536]{1,0:T(8,128)(2,1)S(1)}, u32[]{:S(2)}, u32[]{:S(2)}) %collective-permute-start.1) | collective-permute-done | bytes 393248 | tf_op jit(solution)/shard_map/ppermute | solution.py:290
  23.2 4.9 %collective-permute-start.2 = (bf16[128,1536]{1,0:T(8,128)(2,1)S(1)}, bf16[128,1536]{1,0:T(8,128)(2,1)S(1)}, u32[]{:S(2)}, u32[]{:S(2)}) collective-permute-start(bf16[128,1536]{1,0:T(8,128)(2,1)S(1)} %collective-permute-done.1.refs_0_), channel_id=1, source_target_pairs={{0,32},{16,496},{32,64},{48,16},{64,96},{80,48},{96,128},{112,80},... | collective-permute-start | bytes 1179656 | tf_op jit(solution)/shard_map/ppermute | solution.py:290
  28.1 4.5 %collective-permute-start.12 = (bf16[136,1536]{1,0:T(8,128)(2,1)S(1)}, bf16[136,1536]{1,0:T(8,128)(2,1)S(1)}, u32[]{:S(2)}, u32[]{:S(2)}) collective-permute-start(bf16[136,1536]{1,0:T(8,128)(2,1)S(1)} %collective-permute-done.11.refs_1_.refs_2_), channel_id=1, source_target_pairs={{0,32},{16,496},{32,64},{48,16},{64,96},{80,48},{96,128},{112,80},... | collective-permute-start | bytes 1253384 | tf_op jit(solution)/shard_map/ppermute | solution.py:290
  32.5 0.2 collective-permute-done.2.refs_0_.refs_2_
  32.8 5.0 %collective-permute-start.3 = (bf16[128,1536]{1,0:T(8,128)(2,1)S(1)}, bf16[128,1536]{1,0:T(8,128)(2,1)S(1)}, u32[]{:S(2)}, u32[]{:S(2)}) collective-permute-start(bf16[128,1536]{1,0:T(8,128)(2,1)S(1)} %collective-permute-done.2.refs_0_.refs_2_), channel_id=1, source_target_pairs={{0,32},{16,496},{32,64},{48,16},{64,96},{80,48},{96,128},{112,80},... | collective-permute-start | bytes 1179656 | tf_op jit(solution)/shard_map/ppermute | solution.py:290
  37.8 4.7 %collective-permute-start.13 = (bf16[136,1536]{1,0:T(8,128)(2,1)S(1)}, bf16[136,1536]{1,0:T(8,128)(2,1)S(1)}, u32[]{:S(2)}, u32[]{:S(2)}) collective-permute-start(bf16[136,1536]{1,0:T(8,128)(2,1)S(1)} %collective-permute-done.12.refs_1_.refs_2_.refs_3_), channel_id=1, source_target_pairs={{0,32},{16,496},{32,64},{48,16},{64,96},{80,48},{96,128},{112,80},... | collective-permute-start | bytes 1253384 | tf_op jit(solution)/shard_map/ppermute | solution.py:290
  42.6 5.0 %collective-permute-start.4 = (bf16[128,1536]{1,0:T(8,128)(2,1)S(1)}, bf16[128,1536]{1,0:T(8,128)(2,1)S(1)}, u32[]{:S(2)}, u32[]{:S(2)}) collective-permute-start(bf16[128,1536]{1,0:T(8,128)(2,1)S(1)} %collective-permute-done.3.refs_0_.refs_4_), channel_id=1, source_target_pairs={{0,32},{16,496},{32,64},{48,16},{64,96},{80,48},{96,128},{112,80},... | collective-permute-start | bytes 1179656 | tf_op jit(solution)/shard_map/ppermute | solution.py:290
  47.5 5.0 %collective-permute-start.14 = (bf16[136,1536]{1,0:T(8,128)(2,1)S(1)}, bf16[136,1536]{1,0:T(8,128)(2,1)S(1)}, u32[]{:S(2)}, u32[]{:S(2)}) collective-permute-start(bf16[136,1536]{1,0:T(8,128)(2,1)S(1)} %collective-permute-done.13.refs_1_.refs_2_.refs_5_), channel_id=1, source_target_pairs={{0,32},{16,496},{32,64},{48,16},{64,96},{80,48},{96,128},{112,80},... | collective-permute-start | bytes 1253384 | tf_op jit(solution)/shard_map/ppermute | solution.py:290
  52.5 4.7 %collective-permute-start.5 = (bf16[128,1536]{1,0:T(8,128)(2,1)S(1)}, bf16[128,1536]{1,0:T(8,128)(2,1)S(1)}, u32[]{:S(2)}, u32[]{:S(2)}) collective-permute-start(bf16[128,1536]{1,0:T(8,128)(2,1)S(1)} %collective-permute-done.4.refs_0_.refs_6_), channel_id=1, source_target_pairs={{0,32},{16,496},{32,64},{48,16},{64,96},{80,48},{96,128},{112,80},... | collective-permute-start | bytes 1179656 | tf_op jit(solution)/shard_map/ppermute | solution.py:290
  57.2 0.2 collective-permute-done.14.refs_1_.refs_2_.refs_7_
  57.5 5.0 %collective-permute-start.15 = (bf16[136,1536]{1,0:T(8,128)(2,1)S(1)}, bf16[136,1536]{1,0:T(8,128)(2,1)S(1)}, u32[]{:S(2)}, u32[]{:S(2)}) collective-permute-start(bf16[136,1536]{1,0:T(8,128)(2,1)S(1)} %collective-permute-done.14.refs_1_.refs_2_.refs_7_), channel_id=1, source_target_pairs={{0,32},{16,496},{32,64},{48,16},{64,96},{80,48},{96,128},{112,80},... | collective-permute-start | bytes 1253384 | tf_op jit(solution)/shard_map/ppermute | solution.py:290
  62.5 4.4 %collective-permute-start.6 = (bf16[128,1536]{1,0:T(8,128)(2,1)S(1)}, bf16[128,1536]{1,0:T(8,128)(2,1)S(1)}, u32[]{:S(2)}, u32[]{:S(2)}) collective-permute-start(bf16[128,1536]{1,0:T(8,128)(2,1)S(1)} %collective-permute-done.5.refs_0_.refs_8_), channel_id=1, source_target_pairs={{0,32},{16,496},{32,64},{48,16},{64,96},{80,48},{96,128},{112,80},... | collective-permute-start | bytes 1179656 | tf_op jit(solution)/shard_map/ppermute | solution.py:290
  67.0 0.5 collective-permute-done.15.refs_1_.refs_2_.refs_9_
  67.5 5.0 %collective-permute-start.16 = (bf16[136,1536]{1,0:T(8,128)(2,1)S(1)}, bf16[136,1536]{1,0:T(8,128)(2,1)S(1)}, u32[]{:S(2)}, u32[]{:S(2)}) collective-permute-start(bf16[136,1536]{1,0:T(8,128)(2,1)S(1)} %collective-permute-done.15.refs_1_.refs_2_.refs_9_), channel_id=1, source_target_pairs={{0,32},{16,496},{32,64},{48,16},{64,96},{80,48},{96,128},{112,80},... | collective-permute-start | bytes 1253384 | tf_op jit(solution)/shard_map/ppermute | solution.py:290
  72.5 4.2 %collective-permute-start.7 = (bf16[128,1536]{1,0:T(8,128)(2,1)S(1)}, bf16[128,1536]{1,0:T(8,128)(2,1)S(1)}, u32[]{:S(2)}, u32[]{:S(2)}) collective-permute-start(bf16[128,1536]{1,0:T(8,128)(2,1)S(1)} %collective-permute-done.6.refs_0_.refs_10_), channel_id=1, source_target_pairs={{0,32},{16,496},{32,64},{48,16},{64,96},{80,48},{96,128},{112,80},... | collective-permute-start | bytes 1179656 | tf_op jit(solution)/shard_map/ppermute | solution.py:290
  76.7 6.4 %collective-permute-start = (bf16[90,1536]{1,0:T(8,128)(2,1)}, bf16[90,1536]{1,0:T(8,128)(2,1)S(1)}, u32[]{:S(2)}, u32[]{:S(2)}) collective-permute-start(bf16[90,1536]{1,0:T(8,128)(2,1)} %bitcast.6), channel_id=1, source_target_pairs={{0,16},{16,0},{32,48},{48,32},{64,80},{80,64},{96,112},{112,96},{1... | collective-permute-start | bytes 829448 | tf_op jit(solution)/shard_map/ppermute | solution.py:293
  83.1 0.0 copy-start
  83.1 4.9 %collective-permute-start.17 = (bf16[136,1536]{1,0:T(8,128)(2,1)S(1)}, bf16[136,1536]{1,0:T(8,128)(2,1)S(1)}, u32[]{:S(2)}, u32[]{:S(2)}) collective-permute-start(bf16[136,1536]{1,0:T(8,128)(2,1)S(1)} %collective-permute-done.16.refs_1_.refs_2_.refs_11_), channel_id=1, source_target_pairs={{0,32},{16,496},{32,64},{48,16},{64,96},{80,48},{96,128},{112,80},... | collective-permute-start | bytes 1253384 | tf_op jit(solution)/shard_map/ppermute | solution.py:290
  88.0 1.9 %collective-permute-start.8 = (bf16[128,1536]{1,0:T(8,128)(2,1)S(1)}, bf16[128,1536]{1,0:T(8,128)(2,1)S(1)}, u32[]{:S(2)}, u32[]{:S(2)}) collective-permute-start(bf16[128,1536]{1,0:T(8,128)(2,1)S(1)} %collective-permute-done.7.refs_0_.refs_12_), channel_id=1, source_target_pairs={{0,32},{16,496},{32,64},{48,16},{64,96},{80,48},{96,128},{112,80},... | collective-permute-start | bytes 1179656 | tf_op jit(solution)/shard_map/ppermute | solution.py:290
  90.0 0.3 own_tangents.1.own_ref
  90.3 1.1 tangents.7
  91.5 1.1 tangents.8
  92.6 1.2 tangents.9
  93.7 1.1 tangents.10
  94.9 1.1 tangents.11
  96.0 1.1 tangents.12
  97.1 1.1 tangents.13
  98.2 1.1 last_tangents.1
  99.3 0.8 copy-done.18
  100.0 6.8 %all-to-all-start = ((bf16[16,24,8,128]{3,2,1,0:T(8,128)(2,1)}), bf16[16,24,8,128]{3,2,1,0:T(8,128)(2,1)}, u32[]{:S(2)}, u32[]{:S(2)}) async-start(bf16[16,24,8,128]{3,2,1,0:T(8,128)(2,1)} %last_tangents.1), calls=%async_computation | async-start | bytes 1572864 | tf_op jit(solution)/shard_map/all_to_all | solution.py:323
  106.9 3.9 %collective-permute-start.18 = (bf16[8,128]{1,0:T(8,128)(2,1)S(1)}, bf16[8,128]{1,0:T(8,128)(2,1)S(1)}, u32[]{:S(2)}, u32[]{:S(2)}) collective-permute-start(bf16[8,128]{1,0:T(8,128)(2,1)S(1)} %slice.4), channel_id=1, source_target_pairs={{0,32},{16,496},{32,64},{48,16},{64,96},{80,48},{96,128},{112,80},... | collective-permute-start | bytes 6152 | tf_op jit(solution)/shard_map/ppermute | solution.py:290
  110.8 0.7 collective-permute-done.18.refs_1_
  111.5 6.3 %all-to-all-done.in_ref = bf16[16,24,8,128]{3,2,1,0:T(8,128)(2,1)} async-done(((bf16[16,24,8,128]{3,2,1,0:T(8,128)(2,1)}), bf16[16,24,8,128]{3,2,1,0:T(8,128)(2,1)}, u32[]{:S(2)}, u32[]{:S(2)}) %all-to-all-start) | async-done | bytes 786464 | tf_op jit(solution)/shard_map/all_to_all | solution.py:323
  117.8 0.0 copy-start.17
  117.8 1.8 %combine.1 = bf16[16,24,8,128]{3,2,1,0:T(8,128)(2,1)S(1)} custom-call(bf16[16,24,8,128]{3,2,1,0:T(8,128)(2,1)} %all-to-all-done.in_ref, bf16[14,128,256]{2,1,0:T(8,128)(2,1)S(1)} %get-tuple-element.34.mix_ref, bf16[8,128]{1,0:T(8,128)(2,1)S(1)} %slot_table.1.refs_0_, bf16[8,128]{1,0:T(8,128)(2,1)S(1)} %collective-permute-done.18.refs_1_), custom_call_target="tpu_custom_call" | custom-call | flops 1000000000 | bytes 1572864 | tf_op jit(solution)/shard_map/combine/pallas_call | solution.py:208
  119.6 13.9 %all_to_all.10.in_ref = bf16[16,24,8,128]{3,2,1,0:T(8,128)(2,1)S(1)} all-to-all(bf16[16,24,8,128]{3,2,1,0:T(8,128)(2,1)S(1)} %combine.1), channel_id=1, replica_groups=mesh['dp'=32,'expert'=16] {'expert'}, dimensions={0} | all-to-all | bytes 1572864 | tf_op jit(solution)/shard_map/all_to_all | solution.py:325
  133.7 3.6 %gradients.1 = (f32[1080,128]{1,0:T(8,128)S(1)}, f32[1080,128]{1,0:T(8,128)S(1)}) custom-call(bf16[16,24,8,128]{3,2,1,0:T(8,128)(2,1)S(1)} %all_to_all.10.in_ref, bf16[128,1536]{1,0:T(8,128)(2,1)S(1)} %copy-done.3, bf16[136,1536]{1,0:T(8,128)(2,1)S(1)} %collective-permute-done.11.refs_1_.refs_2_, bf16[128,1536]{1,0:T(8,128)(2,1)S(1)} %copy-done.5, ...), custom_call_target="tpu_custom_call" | custom-call | flops 1207959552 | bytes 6291456 | tf_op jit(solution)/shard_map/gradients/pallas_call | solution.py:264
  137.3 7.2 %collective-permute-start.19 = (f32[1080,128]{1,0:T(8,128)S(1)}, f32[1080,128]{1,0:T(8,128)S(1)}, u32[]{:S(2)}, u32[]{:S(2)}) collective-permute-start(f32[1080,128]{1,0:T(8,128)S(1)} %get-tuple-element.36), channel_id=1, source_target_pairs={{0,16},{16,0},{32,48},{48,32},{64,80},{80,64},{96,112},{112,96},{1... | collective-permute-start | bytes 1658888 | tf_op jit(solution)/shard_map/ppermute | solution.py:293
  144.5 1.6 %collective-permute-done.19 = f32[1080,128]{1,0:T(8,128)S(1)} collective-permute-done((f32[1080,128]{1,0:T(8,128)S(1)}, f32[1080,128]{1,0:T(8,128)S(1)}, u32[]{:S(2)}, u32[]{:S(2)}) %collective-permute-start.19) | collective-permute-done | bytes 552992 | tf_op jit(solution)/shard_map/ppermute | solution.py:293
  146.1 0.9 add.3
  (59 shorter events, 0.2 us)
Async XLA Ops:
  0.0 18.2 %collective-permute-start.9 = (bf16[128,1536]{1,0:T(8,128)(2,1)}, bf16[128,1536]{1,0:T(8,128)(2,1)S(1)}, u32[]{:S(2)}, u32[]{:S(2)}) collective-permute-start(bf16[128,1536]{1,0:T(8,128)(2,1)} %refs_14_.1), channel_id=1, source_target_pairs={{0,16},{16,0},{32,48},{48,32},{64,80},{80,64},{96,112},{112,96},{1... | collective-permute-start | bytes 1179656 | tf_op jit(solution)/shard_map/ppermute | solution.py:293
  8.7 0.7 copy-start.20
  9.4 0.7 copy-start.21
  10.1 79.8 %copy-start.22 = (bf16[1,90,1536]{2,1,0:T(8,128)(2,1)S(1)}, bf16[1,90,1536]{2,1,0:T(8,128)(2,1)}, u32[]{:S(2)}) copy-start(bf16[1,90,1536]{2,1,0:T(8,128)(2,1)} %param.5) | copy-start | bytes 829444
  10.4 7.7 %collective-permute-start.10 = (bf16[8,128]{1,0:T(8,128)(2,1)S(1)}, bf16[8,128]{1,0:T(8,128)(2,1)S(1)}, u32[]{:S(2)}, u32[]{:S(2)}) collective-permute-start(bf16[8,128]{1,0:T(8,128)(2,1)S(1)} %slot_table.1.refs_0_), channel_id=1, source_target_pairs={{0,16},{16,0},{32,48},{48,32},{64,80},{80,64},{96,112},{112,96},{1... | collective-permute-start | bytes 6152 | tf_op jit(solution)/shard_map/ppermute | solution.py:293
  12.4 10.8 %collective-permute-start.1 = (bf16[128,1536]{1,0:T(8,128)(2,1)}, bf16[128,1536]{1,0:T(8,128)(2,1)S(1)}, u32[]{:S(2)}, u32[]{:S(2)}) collective-permute-start(bf16[128,1536]{1,0:T(8,128)(2,1)} %refs_14_.1), channel_id=1, source_target_pairs={{0,32},{16,496},{32,64},{48,16},{64,96},{80,48},{96,128},{112,80},... | collective-permute-start | bytes 1179656 | tf_op jit(solution)/shard_map/ppermute | solution.py:290
  18.2 71.8 %copy-start.16 = (bf16[128,1536]{1,0:T(8,128)(2,1)S(1)}, bf16[128,1536]{1,0:T(8,128)(2,1)}, u32[]{:S(2)}) copy-start(bf16[128,1536]{1,0:T(8,128)(2,1)} %refs_14_.1) | copy-start | bytes 1179652
  18.2 9.9 %collective-permute-start.11 = (bf16[136,1536]{1,0:T(8,128)(2,1)S(1)}, bf16[136,1536]{1,0:T(8,128)(2,1)S(1)}, u32[]{:S(2)}, u32[]{:S(2)}) collective-permute-start(bf16[136,1536]{1,0:T(8,128)(2,1)S(1)} %maximum_maximum_fusion), channel_id=1, source_target_pairs={{0,32},{16,496},{32,64},{48,16},{64,96},{80,48},{96,128},{112,80},... | collective-permute-start | bytes 1253384 | tf_op jit(solution)/shard_map/ppermute | solution.py:290
  23.2 67.2 %copy-start.2 = (bf16[128,1536]{1,0:T(8,128)(2,1)}, bf16[128,1536]{1,0:T(8,128)(2,1)S(1)}, u32[]{:S(2)}) copy-start(bf16[128,1536]{1,0:T(8,128)(2,1)S(1)} %collective-permute-done.1.refs_0_) | copy-start | bytes 1179652
  23.2 9.6 %collective-permute-start.2 = (bf16[128,1536]{1,0:T(8,128)(2,1)S(1)}, bf16[128,1536]{1,0:T(8,128)(2,1)S(1)}, u32[]{:S(2)}, u32[]{:S(2)}) collective-permute-start(bf16[128,1536]{1,0:T(8,128)(2,1)S(1)} %collective-permute-done.1.refs_0_), channel_id=1, source_target_pairs={{0,32},{16,496},{32,64},{48,16},{64,96},{80,48},{96,128},{112,80},... | collective-permute-start | bytes 1179656 | tf_op jit(solution)/shard_map/ppermute | solution.py:290
  28.1 9.7 %collective-permute-start.12 = (bf16[136,1536]{1,0:T(8,128)(2,1)S(1)}, bf16[136,1536]{1,0:T(8,128)(2,1)S(1)}, u32[]{:S(2)}, u32[]{:S(2)}) collective-permute-start(bf16[136,1536]{1,0:T(8,128)(2,1)S(1)} %collective-permute-done.11.refs_1_.refs_2_), channel_id=1, source_target_pairs={{0,32},{16,496},{32,64},{48,16},{64,96},{80,48},{96,128},{112,80},... | collective-permute-start | bytes 1253384 | tf_op jit(solution)/shard_map/ppermute | solution.py:290
  32.8 58.7 %copy-start.4 = (bf16[128,1536]{1,0:T(8,128)(2,1)}, bf16[128,1536]{1,0:T(8,128)(2,1)S(1)}, u32[]{:S(2)}) copy-start(bf16[128,1536]{1,0:T(8,128)(2,1)S(1)} %collective-permute-done.2.refs_0_.refs_2_) | copy-start | bytes 1179652
  32.8 9.8 %collective-permute-start.3 = (bf16[128,1536]{1,0:T(8,128)(2,1)S(1)}, bf16[128,1536]{1,0:T(8,128)(2,1)S(1)}, u32[]{:S(2)}, u32[]{:S(2)}) collective-permute-start(bf16[128,1536]{1,0:T(8,128)(2,1)S(1)} %collective-permute-done.2.refs_0_.refs_2_), channel_id=1, source_target_pairs={{0,32},{16,496},{32,64},{48,16},{64,96},{80,48},{96,128},{112,80},... | collective-permute-start | bytes 1179656 | tf_op jit(solution)/shard_map/ppermute | solution.py:290
  37.8 9.7 %collective-permute-start.13 = (bf16[136,1536]{1,0:T(8,128)(2,1)S(1)}, bf16[136,1536]{1,0:T(8,128)(2,1)S(1)}, u32[]{:S(2)}, u32[]{:S(2)}) collective-permute-start(bf16[136,1536]{1,0:T(8,128)(2,1)S(1)} %collective-permute-done.12.refs_1_.refs_2_.refs_3_), channel_id=1, source_target_pairs={{0,32},{16,496},{32,64},{48,16},{64,96},{80,48},{96,128},{112,80},... | collective-permute-start | bytes 1253384 | tf_op jit(solution)/shard_map/ppermute | solution.py:290
  42.5 50.0 %copy-start.6 = (bf16[128,1536]{1,0:T(8,128)(2,1)}, bf16[128,1536]{1,0:T(8,128)(2,1)S(1)}, u32[]{:S(2)}) copy-start(bf16[128,1536]{1,0:T(8,128)(2,1)S(1)} %collective-permute-done.3.refs_0_.refs_4_) | copy-start | bytes 1179652
  42.6 10.0 %collective-permute-start.4 = (bf16[128,1536]{1,0:T(8,128)(2,1)S(1)}, bf16[128,1536]{1,0:T(8,128)(2,1)S(1)}, u32[]{:S(2)}, u32[]{:S(2)}) collective-permute-start(bf16[128,1536]{1,0:T(8,128)(2,1)S(1)} %collective-permute-done.3.refs_0_.refs_4_), channel_id=1, source_target_pairs={{0,32},{16,496},{32,64},{48,16},{64,96},{80,48},{96,128},{112,80},... | collective-permute-start | bytes 1179656 | tf_op jit(solution)/shard_map/ppermute | solution.py:290
  47.5 9.9 %collective-permute-start.14 = (bf16[136,1536]{1,0:T(8,128)(2,1)S(1)}, bf16[136,1536]{1,0:T(8,128)(2,1)S(1)}, u32[]{:S(2)}, u32[]{:S(2)}) collective-permute-start(bf16[136,1536]{1,0:T(8,128)(2,1)S(1)} %collective-permute-done.13.refs_1_.refs_2_.refs_5_), channel_id=1, source_target_pairs={{0,32},{16,496},{32,64},{48,16},{64,96},{80,48},{96,128},{112,80},... | collective-permute-start | bytes 1253384 | tf_op jit(solution)/shard_map/ppermute | solution.py:290
  52.5 41.2 %copy-start.8 = (bf16[128,1536]{1,0:T(8,128)(2,1)}, bf16[128,1536]{1,0:T(8,128)(2,1)S(1)}, u32[]{:S(2)}) copy-start(bf16[128,1536]{1,0:T(8,128)(2,1)S(1)} %collective-permute-done.4.refs_0_.refs_6_) | copy-start | bytes 1179652
  52.5 10.0 %collective-permute-start.5 = (bf16[128,1536]{1,0:T(8,128)(2,1)S(1)}, bf16[128,1536]{1,0:T(8,128)(2,1)S(1)}, u32[]{:S(2)}, u32[]{:S(2)}) collective-permute-start(bf16[128,1536]{1,0:T(8,128)(2,1)S(1)} %collective-permute-done.4.refs_0_.refs_6_), channel_id=1, source_target_pairs={{0,32},{16,496},{32,64},{48,16},{64,96},{80,48},{96,128},{112,80},... | collective-permute-start | bytes 1179656 | tf_op jit(solution)/shard_map/ppermute | solution.py:290
  57.5 10.0 %collective-permute-start.15 = (bf16[136,1536]{1,0:T(8,128)(2,1)S(1)}, bf16[136,1536]{1,0:T(8,128)(2,1)S(1)}, u32[]{:S(2)}, u32[]{:S(2)}) collective-permute-start(bf16[136,1536]{1,0:T(8,128)(2,1)S(1)} %collective-permute-done.14.refs_1_.refs_2_.refs_7_), channel_id=1, source_target_pairs={{0,32},{16,496},{32,64},{48,16},{64,96},{80,48},{96,128},{112,80},... | collective-permute-start | bytes 1253384 | tf_op jit(solution)/shard_map/ppermute | solution.py:290
  62.5 32.4 %copy-start.10 = (bf16[128,1536]{1,0:T(8,128)(2,1)}, bf16[128,1536]{1,0:T(8,128)(2,1)S(1)}, u32[]{:S(2)}) copy-start(bf16[128,1536]{1,0:T(8,128)(2,1)S(1)} %collective-permute-done.5.refs_0_.refs_8_) | copy-start | bytes 1179652
  62.5 10.0 %collective-permute-start.6 = (bf16[128,1536]{1,0:T(8,128)(2,1)S(1)}, bf16[128,1536]{1,0:T(8,128)(2,1)S(1)}, u32[]{:S(2)}, u32[]{:S(2)}) collective-permute-start(bf16[128,1536]{1,0:T(8,128)(2,1)S(1)} %collective-permute-done.5.refs_0_.refs_8_), channel_id=1, source_target_pairs={{0,32},{16,496},{32,64},{48,16},{64,96},{80,48},{96,128},{112,80},... | collective-permute-start | bytes 1179656 | tf_op jit(solution)/shard_map/ppermute | solution.py:290
  67.5 15.6 %collective-permute-start.16 = (bf16[136,1536]{1,0:T(8,128)(2,1)S(1)}, bf16[136,1536]{1,0:T(8,128)(2,1)S(1)}, u32[]{:S(2)}, u32[]{:S(2)}) collective-permute-start(bf16[136,1536]{1,0:T(8,128)(2,1)S(1)} %collective-permute-done.15.refs_1_.refs_2_.refs_9_), channel_id=1, source_target_pairs={{0,32},{16,496},{32,64},{48,16},{64,96},{80,48},{96,128},{112,80},... | collective-permute-start | bytes 1253384 | tf_op jit(solution)/shard_map/ppermute | solution.py:290
  72.5 23.5 %copy-start.12 = (bf16[128,1536]{1,0:T(8,128)(2,1)}, bf16[128,1536]{1,0:T(8,128)(2,1)S(1)}, u32[]{:S(2)}) copy-start(bf16[128,1536]{1,0:T(8,128)(2,1)S(1)} %collective-permute-done.6.refs_0_.refs_10_) | copy-start | bytes 1179652
  72.5 15.5 %collective-permute-start.7 = (bf16[128,1536]{1,0:T(8,128)(2,1)S(1)}, bf16[128,1536]{1,0:T(8,128)(2,1)S(1)}, u32[]{:S(2)}, u32[]{:S(2)}) collective-permute-start(bf16[128,1536]{1,0:T(8,128)(2,1)S(1)} %collective-permute-done.6.refs_0_.refs_10_), channel_id=1, source_target_pairs={{0,32},{16,496},{32,64},{48,16},{64,96},{80,48},{96,128},{112,80},... | collective-permute-start | bytes 1179656 | tf_op jit(solution)/shard_map/ppermute | solution.py:290
  76.7 13.2 %collective-permute-start = (bf16[90,1536]{1,0:T(8,128)(2,1)}, bf16[90,1536]{1,0:T(8,128)(2,1)S(1)}, u32[]{:S(2)}, u32[]{:S(2)}) collective-permute-start(bf16[90,1536]{1,0:T(8,128)(2,1)} %bitcast.6), channel_id=1, source_target_pairs={{0,16},{16,0},{32,48},{48,32},{64,80},{80,64},{96,112},{112,96},{1... | collective-permute-start | bytes 829448 | tf_op jit(solution)/shard_map/ppermute | solution.py:293
  83.1 12.9 %copy-start = (bf16[136,1536]{1,0:T(8,128)(2,1)}, bf16[136,1536]{1,0:T(8,128)(2,1)S(1)}, u32[]{:S(2)}) copy-start(bf16[136,1536]{1,0:T(8,128)(2,1)S(1)} %collective-permute-done.16.refs_1_.refs_2_.refs_11_) | copy-start | bytes 1253380
  83.1 14.0 %collective-permute-start.17 = (bf16[136,1536]{1,0:T(8,128)(2,1)S(1)}, bf16[136,1536]{1,0:T(8,128)(2,1)S(1)}, u32[]{:S(2)}, u32[]{:S(2)}) collective-permute-start(bf16[136,1536]{1,0:T(8,128)(2,1)S(1)} %collective-permute-done.16.refs_1_.refs_2_.refs_11_), channel_id=1, source_target_pairs={{0,32},{16,496},{32,64},{48,16},{64,96},{80,48},{96,128},{112,80},... | collective-permute-start | bytes 1253384 | tf_op jit(solution)/shard_map/ppermute | solution.py:290
  88.0 9.2 %copy-start.14 = (bf16[128,1536]{1,0:T(8,128)(2,1)}, bf16[128,1536]{1,0:T(8,128)(2,1)S(1)}, u32[]{:S(2)}) copy-start(bf16[128,1536]{1,0:T(8,128)(2,1)S(1)} %collective-permute-done.7.refs_0_.refs_12_) | copy-start | bytes 1179652
  88.0 10.2 %collective-permute-start.8 = (bf16[128,1536]{1,0:T(8,128)(2,1)S(1)}, bf16[128,1536]{1,0:T(8,128)(2,1)S(1)}, u32[]{:S(2)}, u32[]{:S(2)}) collective-permute-start(bf16[128,1536]{1,0:T(8,128)(2,1)S(1)} %collective-permute-done.7.refs_0_.refs_12_), channel_id=1, source_target_pairs={{0,32},{16,496},{32,64},{48,16},{64,96},{80,48},{96,128},{112,80},... | collective-permute-start | bytes 1179656 | tf_op jit(solution)/shard_map/ppermute | solution.py:290
  99.3 0.8 copy-start.18
  100.0 17.8 %all-to-all-start = ((bf16[16,24,8,128]{3,2,1,0:T(8,128)(2,1)}), bf16[16,24,8,128]{3,2,1,0:T(8,128)(2,1)}, u32[]{:S(2)}, u32[]{:S(2)}) async-start(bf16[16,24,8,128]{3,2,1,0:T(8,128)(2,1)} %last_tangents.1), calls=%async_computation | async-start | bytes 1572864 | tf_op jit(solution)/shard_map/all_to_all | solution.py:323
  106.9 4.7 %collective-permute-start.18 = (bf16[8,128]{1,0:T(8,128)(2,1)S(1)}, bf16[8,128]{1,0:T(8,128)(2,1)S(1)}, u32[]{:S(2)}, u32[]{:S(2)}) collective-permute-start(bf16[8,128]{1,0:T(8,128)(2,1)S(1)} %slice.4), channel_id=1, source_target_pairs={{0,32},{16,496},{32,64},{48,16},{64,96},{80,48},{96,128},{112,80},... | collective-permute-start | bytes 6152 | tf_op jit(solution)/shard_map/ppermute | solution.py:290
  117.8 15.8 %copy-start.7 = (bf16[128,1536]{1,0:T(8,128)(2,1)S(1)}, bf16[128,1536]{1,0:T(8,128)(2,1)}, u32[]{:S(2)}) copy-start(bf16[128,1536]{1,0:T(8,128)(2,1)} %copy-done.6) | copy-start | bytes 1179652
  117.8 15.8 %copy-start.9 = (bf16[128,1536]{1,0:T(8,128)(2,1)S(1)}, bf16[128,1536]{1,0:T(8,128)(2,1)}, u32[]{:S(2)}) copy-start(bf16[128,1536]{1,0:T(8,128)(2,1)} %copy-done.8) | copy-start | bytes 1179652
  117.8 15.8 %copy-start.11 = (bf16[128,1536]{1,0:T(8,128)(2,1)S(1)}, bf16[128,1536]{1,0:T(8,128)(2,1)}, u32[]{:S(2)}) copy-start(bf16[128,1536]{1,0:T(8,128)(2,1)} %copy-done.10) | copy-start | bytes 1179652
  117.8 15.8 %copy-start.13 = (bf16[128,1536]{1,0:T(8,128)(2,1)S(1)}, bf16[128,1536]{1,0:T(8,128)(2,1)}, u32[]{:S(2)}) copy-start(bf16[128,1536]{1,0:T(8,128)(2,1)} %copy-done.12) | copy-start | bytes 1179652
  117.8 15.8 %copy-start.15 = (bf16[128,1536]{1,0:T(8,128)(2,1)S(1)}, bf16[128,1536]{1,0:T(8,128)(2,1)}, u32[]{:S(2)}) copy-start(bf16[128,1536]{1,0:T(8,128)(2,1)} %copy-done.14) | copy-start | bytes 1179652
  117.8 15.8 %copy-start.17 = (bf16[128,1536]{1,0:T(8,128)(2,1)S(1)}, bf16[128,1536]{1,0:T(8,128)(2,1)}, u32[]{:S(2)}) copy-start(bf16[128,1536]{1,0:T(8,128)(2,1)} %refs_14_.1) | copy-start | bytes 1179652
  117.8 15.8 %copy-start.19 = (bf16[128,1536]{1,0:T(8,128)(2,1)S(1)}, bf16[128,1536]{1,0:T(8,128)(2,1)}, u32[]{:S(2)}) copy-start(bf16[128,1536]{1,0:T(8,128)(2,1)} %copy-done.18) | copy-start | bytes 1179652
  119.6 14.0 %copy-start.1 = (bf16[136,1536]{1,0:T(8,128)(2,1)S(1)}, bf16[136,1536]{1,0:T(8,128)(2,1)}, u32[]{:S(2)}) copy-start(bf16[136,1536]{1,0:T(8,128)(2,1)} %copy-done) | copy-start | bytes 1253380
  119.6 14.0 %copy-start.3 = (bf16[128,1536]{1,0:T(8,128)(2,1)S(1)}, bf16[128,1536]{1,0:T(8,128)(2,1)}, u32[]{:S(2)}) copy-start(bf16[128,1536]{1,0:T(8,128)(2,1)} %copy-done.2) | copy-start | bytes 1179652
  119.6 14.0 %copy-start.5 = (bf16[128,1536]{1,0:T(8,128)(2,1)S(1)}, bf16[128,1536]{1,0:T(8,128)(2,1)}, u32[]{:S(2)}) copy-start(bf16[128,1536]{1,0:T(8,128)(2,1)} %copy-done.4) | copy-start | bytes 1179652
  137.3 8.7 %collective-permute-start.19 = (f32[1080,128]{1,0:T(8,128)S(1)}, f32[1080,128]{1,0:T(8,128)S(1)}, u32[]{:S(2)}, u32[]{:S(2)}) collective-permute-start(f32[1080,128]{1,0:T(8,128)S(1)} %get-tuple-element.36), channel_id=1, source_target_pairs={{0,16},{16,0},{32,48},{48,32},{64,80},{80,64},{96,112},{112,96},{1... | collective-permute-start | bytes 1658888 | tf_op jit(solution)/shard_map/ppermute | solution.py:293
where the time goes:
time: 149 us; the launch traced here: 147 us
  starting transfers between devices  103 us (69%)
  Pallas kernels  14.9 us (10%)
  blocking collectives  13.9 us (9%)
  waiting for transfers between devices  11.7 us (8%)
  local copies, waits for them, and re-layouts  2.21 us (1%)
    ppermute x16, starting transfers between devices, shift(): return lax.ppermute(x, 'dp', ring)  71.6 us
    ppermute x4, starting transfers between devices, swap(): return lax.ppermute(x, 'dp', partner)  24.2 us
    all_to_all x1, blocking collectives, body(): lax.all_to_all(adjoint, 'expert', split_axis=0, concat_axis=0, tiled=True)  13.9 us
    pallas_call x7, Pallas kernels, tangents(): pl.pallas_call(kernel, grid=(1,), out_shape=[jax.ShapeDtypeStruct(shape,...  7.85 us
    all_to_all x1, starting transfers between devices, body(): lax.all_to_all(packed, 'expert', split_axis=0, concat_axis=0, tiled=True)  6.81 us
    all_to_all x1, waiting for transfers between devices, body(): lax.all_to_all(packed, 'expert', split_axis=0, concat_axis=0, tiled=True)  6.28 us
    ppermute x16, waiting for transfers between devices, shift(): return lax.ppermute(x, 'dp', ring)  3.86 us
    pallas_call x1, Pallas kernels, gradients(): pl.pallas_call(kernel, grid=(width // step,), out_shape=[shape, shape], i...  3.64 us
  transfers between devices with their start and end apart: 21, of which 7 were waited for; matrix products, arithmetic and copies ran while one was open for 0% of the time, Pallas kernels for 6%

commit v1 on v0

--- a/solution.py
+++ b/solution.py
@@ -32,9 +32,19 @@
     return pl.CostEstimate(flops=flops, bytes_accessed=nbytes, transcendentals=0)
 
 
-def table_kernel(capacity, experts, ids_ref, gates_ref, out_ref):
+def message_kernel(capacity, experts, rows_hbm, ids_hbm, gates_hbm, out_ref, ids_ref, gates_ref, sems):
     topk, tokens = ids_ref.shape
     slots = experts * capacity
+    span, width = rows_hbm.shape
+    copies = [
+        pltpu.make_async_copy(rows_hbm, out_ref.at[:span], sems.at[0]),
+        pltpu.make_async_copy(ids_hbm, ids_ref, sems.at[1]),
+        pltpu.make_async_copy(gates_hbm, gates_ref, sems.at[2]),
+    ]
+    for copy in copies:
+        copy.start()
+    for copy in copies[1:]:
+        copy.wait()
     slot = lax.broadcasted_iota(jnp.int32, (slots, tokens), 0)
     expert = slot // capacity
     place = (slot % capacity).astype(jnp.float32)
@@ -63,19 +73,32 @@
         total += lax.dot_general(
             rows, holds, (((1,), (1,)), ((), ())), preferred_element_type=jnp.float32
         )
-    out_ref[...] = total.astype(out_ref.dtype)
-
-
-def slot_table(ids, gates, experts, capacity):
-    return pl.pallas_call(
-        functools.partial(table_kernel, capacity, experts),
-        out_shape=jax.ShapeDtypeStruct((TAB, experts * capacity), jnp.bfloat16),
-        in_specs=[whole(), whole()],
+    out_ref[span:] = jnp.concatenate(
+        [total, jnp.zeros((TAB, width - slots), jnp.float32)], axis=1
+    ).astype(out_ref.dtype)
+    copies[0].wait()
+
+
+def message(rows, ids, gates, experts, capacity):
+    args = (rows, ids.T, gates.T)
+    shape = (rows.shape[0] + TAB, rows.shape[1])
+    return pl.pallas_call(
+        functools.partial(message_kernel, capacity, experts),
+        out_shape=jax.ShapeDtypeStruct(shape, jnp.bfloat16),
+        in_specs=[pl.BlockSpec(memory_space=pltpu.HBM)] * 3,
         out_specs=whole(),
-        compiler_params=params(),
-        cost_estimate=cost(10**7, 10**5),
-        name="slot_table",
-    )(ids.T, gates.T)
+        scratch_shapes=[
+            pltpu.VMEM(args[1].shape, args[1].dtype),
+            pltpu.VMEM(args[2].shape, args[2].dtype),
+            pltpu.SemaphoreType.DMA((3,)),
+        ],
+        cost_estimate=cost(10**7, 10**6),
+        name="message",
+    )(*args)
+
+
+def table_of(rows):
+    return pl.BlockSpec((TAB, LANES), lambda i: (rows.shape[0] // TAB - 1, 0))
 
 
 def mix_of(table, scale):
@@ -106,18 +129,15 @@
 def tangents(pair, pieces, dirs, kept, shape, mix_shape, scale):
     sources, _, capacity, _ = shape
     span = sources * capacity
-    spare = pieces[-1].shape[0] - TAB
-    n = len(pieces)
-    args = list(pieces) + [pieces[-1], dirs] + list(kept)
+    args = list(pieces) + list(pieces) + [dirs] + list(kept)
 
     def kernel(*refs):
-        table_ref, dir_ref = refs[n], refs[n + 1]
-        out_ref, mix_ref = refs[-2], refs[-1]
-        parts = [refs[i][...] for i in range(n - 1)] + [refs[n - 1][:spare, :]]
-        value = project(jnp.concatenate(parts, axis=0), dir_ref[...])
+        dir_ref, out_ref, mix_ref = refs[4], refs[-2], refs[-1]
+        rows = jnp.concatenate([refs[i][:span, :] for i in range(2)], axis=0)
+        value = project(rows, dir_ref[...])
         pack(out_ref, [value[:span], value[span:]])
         for i in range(2):
-            mix_ref[i] = mix_of(table_ref[:, i * LANES : (i + 1) * LANES], scale)
+            mix_ref[i] = mix_of(refs[2 + i][...], scale)
 
     return pl.pallas_call(
         kernel,
@@ -127,13 +147,14 @@
             jax.ShapeDtypeStruct(mix_shape, jnp.bfloat16),
         ],
         in_specs=[full(x) for x in pieces]
-        + [pl.BlockSpec((TAB, 2 * LANES), lambda i: (spare // TAB, 0)), full(dirs)]
+        + [table_of(x) for x in pieces]
+        + [full(dirs)]
         + [pl.BlockSpec(memory_space=pl.ANY)] * len(kept),
         out_specs=[
             pl.BlockSpec((sources, 3, capacity, LANES), lambda i: (0, pair, 0, 0)),
             pl.BlockSpec((2,) + mix_shape[1:], lambda i: (pair, 0, 0)),
         ],
-        input_output_aliases={n + 2 + i: i for i in range(len(kept))},
+        input_output_aliases={5 + i: i for i in range(len(kept))},
         compiler_params=params(),
         cost_estimate=cost(4 * span * dirs.size, 2 * 2 * span * dirs.shape[1] + 2 * dirs.size),
         name="tangents",
@@ -157,16 +178,22 @@
 
 def last_tangents(pair, own, rows, dirs, packed):
     sources, _, capacity, _ = packed.shape
-
-    def kernel(own_ref, rows_ref, dir_ref, _, out_ref):
-        pack(out_ref, [own_ref[...], project(rows_ref[...], dir_ref[...])])
+    span = sources * capacity
+
+    def kernel(own_ref, rows_ref, dir_ref, _, out_ref, held_ref, sem):
+        copy = pltpu.make_async_copy(rows_ref, held_ref, sem)
+        copy.start()
+        copy.wait()
+        pack(out_ref, [own_ref[...], project(held_ref[:span, :], dir_ref[...])])
 
     return pl.pallas_call(
         kernel,
         grid=(1,),
         out_shape=jax.ShapeDtypeStruct(packed.shape, packed.dtype),
-        in_specs=[full(x) for x in (own, rows, dirs)] + [pl.BlockSpec(memory_space=pl.ANY)],
+        in_specs=[full(own), pl.BlockSpec(memory_space=pltpu.HBM), full(dirs)]
+        + [pl.BlockSpec(memory_space=pl.ANY)],
         out_specs=pl.BlockSpec((sources, 3, capacity, LANES), lambda i: (0, pair, 0, 0)),
+        scratch_shapes=[pltpu.VMEM(rows.shape, rows.dtype), pltpu.SemaphoreType.DMA],
         input_output_aliases={3: 0},
         compiler_params=params(),
         cost_estimate=cost(2 * own.shape[0] * dirs.size, 2 * dirs.size),
@@ -207,9 +234,10 @@
 
     return pl.pallas_call(
         kernel,
+        grid=(1,),
         out_shape=jax.ShapeDtypeStruct(packed.shape, packed.dtype),
-        in_specs=[whole()] * (2 + len(tables)),
-        out_specs=whole(),
+        in_specs=[full(packed), full(mixes)] + [table_of(x) for x in tables],
+        out_specs=full(packed),
         compiler_params=params(),
         cost_estimate=cost(10**9, 4 * packed.size),
         name="combine",
@@ -241,18 +269,9 @@
                 lhs_ref[pair] = jnp.concatenate([main, tail], axis=0).astype(jnp.bfloat16)
 
         total = None
-        at = 0
-        for pair, group in enumerate(groups):
-            parts = []
-            left = 2 * span
-            for piece in group:
-                rows = min(left, piece.shape[0])
-                parts.append(refs[at][:rows, :])
-                left -= rows
-                at += 1
-            term = jnp.dot(
-                lhs_ref[pair], jnp.concatenate(parts, axis=0), preferred_element_type=jnp.float32
-            )
+        for pair in range(pairs):
+            rows = jnp.concatenate([refs[2 * pair + i][:span, :] for i in range(2)], axis=0)
+            term = jnp.dot(lhs_ref[pair], rows, preferred_element_type=jnp.float32)
             total = term if total is None else total + term
         for i in range(2):
             lanes = slice(i * LANES, (i + 1) * LANES)
@@ -292,14 +311,10 @@
     def swap(x):
         return lax.ppermute(x, "dp", partner)
 
-    chain_a = [shift(cached_hidden)]
-    other = swap(cached_hidden)
-    table = slot_table(expert_ids, gate_weights, experts, capacity)
-    other_table = swap(table)
-    chip_table = jnp.concatenate(
-        [table, other_table, jnp.zeros((TAB, width - 2 * span), jnp.bfloat16)], axis=1
-    )
-    chain_b = [shift(jnp.concatenate([other, chip_table], axis=0))]
+    sent = message(cached_hidden, expert_ids, gate_weights, experts, capacity)
+    other = swap(sent)
+    chain_a = [shift(sent)]
+    chain_b = [shift(other)]
     other_dir = swap(direction[0])
     pad = jnp.zeros((FEATS - feats, width), jnp.bfloat16)
     dirs = jnp.concatenate([direction[0], pad, other_dir, pad], axis=0)
@@ -307,7 +322,6 @@
         chain_a.append(shift(chain_a[-1]))
         chain_b.append(shift(chain_b[-1]))
     last = shift(chain_a[-1])
-    last_table = shift(chain_b[-1][span:, :LANES])
     shape = (experts, 3 * steps, capacity, LANES)
     mix_shape = (2 * (steps - 1), span, 2 * span)
     kept = ()
@@ -321,7 +335,7 @@
     packed = last_tangents(steps - 1, own, last, dirs, packed)
     groups.append([cached_hidden, last])
     arrived = lax.all_to_all(packed, "expert", split_axis=0, concat_axis=0, tiled=True)
-    adjoint = combine(arrived, mixes, [table, last_table], scale)
+    adjoint = combine(arrived, mixes, [sent, last], scale)
     back = lax.all_to_all(adjoint, "expert", split_axis=0, concat_axis=0, tiled=True)
     mine, theirs = gradients(back, groups, feats)
     theirs = swap(theirs)

time: 149 us -> 144 us (0.966)
  blocking collectives: 13.9 us -> 30.5 us
  starting transfers between devices: 103 us -> 90.7 us
  Pallas kernels: 14.9 us -> 10.4 us
  local copies, waits for them, and re-layouts: 2.21 us -> 0.02 us
    all_to_all x0 -> x1, blocking collectives: none -> 16.9 us  [body(): lax.all_to_all(packed, 'expert', split_axis=0, concat_axis=0, tiled=True)]
    all_to_all x1 -> x0, starting transfers between devices: 6.81 us -> none  [body(): lax.all_to_all(packed, 'expert', split_axis=0, concat_axis=0, tiled=True)]
    all_to_all x1 -> x0, waiting for transfers between devices: 6.28 us -> none  [body(): lax.all_to_all(packed, 'expert', split_axis=0, concat_axis=0, tiled=True)]
    ppermute x16 -> x15, waiting for transfers between devices: 3.86 us -> 8.72 us  [shift(): return lax.ppermute(x, 'dp', ring)]
    pallas_call x7, Pallas kernels: 7.85 us -> 3.38 us  [tangents(): pl.pallas_call(kernel, grid=(1,), out_shape=[jax.ShapeDtypeStruct(shape,...]
    ppermute x16 -> x15, starting transfers between devices: 71.6 us -> 67.4 us  [shift(): return lax.ppermute(x, 'dp', ring)]
    unnamed x46 -> x6, local copies, waits for them, and re-layouts: 2.2 us -> 0.01 us
    ppermute x4 -> x3, starting transfers between devices: 24.2 us -> 23.2 us  [swap(): return lax.ppermute(x, 'dp', partner)]
  transfers between devices with their start and end apart: 21 -> 18, of which waited for: 7 -> 8; matrix products, arithmetic and copies ran while one was open for 0% -> 0% of each run, Pallas kernels for 6% -> 3%
where the time goes in v1:
time: 144 us; the launch traced here: 143 us
  starting transfers between devices  90.7 us (63%)
  blocking collectives  30.5 us (21%)
  Pallas kernels  10.4 us (7%)
  waiting for transfers between devices  10.3 us (7%)
    ppermute x15, starting transfers between devices, shift(): return lax.ppermute(x, 'dp', ring)  67.4 us
    ppermute x3, starting transfers between devices, swap(): return lax.ppermute(x, 'dp', partner)  23.2 us
    all_to_all x1, blocking collectives, body(): lax.all_to_all(packed, 'expert', split_axis=0, concat_axis=0, tiled=True)  16.9 us
    all_to_all x1, blocking collectives, body(): lax.all_to_all(adjoint, 'expert', split_axis=0, concat_axis=0, tiled=True)  13.6 us
    ppermute x15, waiting for transfers between devices, shift(): return lax.ppermute(x, 'dp', ring)  8.72 us
    pallas_call x1, Pallas kernels, gradients(): pl.pallas_call(kernel, grid=(width // step,), out_shape=[shape, shape], i...  3.62 us
    pallas_call x7, Pallas kernels, tangents(): pl.pallas_call(kernel, grid=(1,), out_shape=[jax.ShapeDtypeStruct(shape,...  3.38 us
  transfers between devices with their start and end apart: 18, of which 8 were waited for; matrix products, arithmetic and copies ran while one was open for 0% of the time, Pallas kernels for 3%

profile of v1, /device:TPU:1, one launch (start us, length us, event | category | flops | bytes accessed | tf_op | source)
XLA Modules:
  0.0 143.2 jit_solution(16560912700964153330)
XLA Ops:
  0.0 2.0 %message.1.refs_0_ = bf16[136,1536]{1,0:T(8,128)(2,1)} custom-call(bf16[128,1536]{1,0:T(8,128)(2,1)} %refs_14_.1, s32[4,128]{1,0:T(4,128)} %bitcast.6, f32[4,128]{1,0:T(4,128)} %bitcast.7), custom_call_target="tpu_custom_call" | custom-call | flops 10000000 | bytes 1000000 | tf_op jit(solution)/shard_map/message/pallas_call | solution.py:85
  2.0 8.7 %collective-permute-start.9 = (bf16[136,1536]{1,0:T(8,128)(2,1)}, bf16[136,1536]{1,0:T(8,128)(2,1)S(1)}, u32[]{:S(2)}, u32[]{:S(2)}) collective-permute-start(bf16[136,1536]{1,0:T(8,128)(2,1)} %message.1.refs_0_), channel_id=1, source_target_pairs={{0,16},{16,0},{32,48},{48,32},{64,80},{80,64},{96,112},{112,96},{1... | collective-permute-start | bytes 1253384 | tf_op jit(solution)/shard_map/ppermute | solution.py:312
  10.8 5.8 %collective-permute-start.1 = (bf16[136,1536]{1,0:T(8,128)(2,1)}, bf16[136,1536]{1,0:T(8,128)(2,1)S(1)}, u32[]{:S(2)}, u32[]{:S(2)}) collective-permute-start(bf16[136,1536]{1,0:T(8,128)(2,1)} %message.1.refs_0_), channel_id=1, source_target_pairs={{0,32},{16,496},{32,64},{48,16},{64,96},{80,48},{96,128},{112,80},... | collective-permute-start | bytes 1253384 | tf_op jit(solution)/shard_map/ppermute | solution.py:309
  16.5 0.0 collective-permute-done.9
  16.5 2.6 %collective-permute-start.10 = (bf16[136,1536]{1,0:T(8,128)(2,1)S(1)}, bf16[136,1536]{1,0:T(8,128)(2,1)S(1)}, u32[]{:S(2)}, u32[]{:S(2)}) collective-permute-start(bf16[136,1536]{1,0:T(8,128)(2,1)S(1)} %collective-permute-done.9), channel_id=1, source_target_pairs={{0,32},{16,496},{32,64},{48,16},{64,96},{80,48},{96,128},{112,80},... | collective-permute-start | bytes 1253384 | tf_op jit(solution)/shard_map/ppermute | solution.py:309
  19.2 2.6 %collective-permute-done.1.refs_0_.refs_2_ = bf16[136,1536]{1,0:T(8,128)(2,1)S(1)} collective-permute-done((bf16[136,1536]{1,0:T(8,128)(2,1)}, bf16[136,1536]{1,0:T(8,128)(2,1)S(1)}, u32[]{:S(2)}, u32[]{:S(2)}) %collective-permute-start.1) | collective-permute-done | bytes 417824 | tf_op jit(solution)/shard_map/ppermute | solution.py:309
  21.8 4.9 %collective-permute-start.2 = (bf16[136,1536]{1,0:T(8,128)(2,1)S(1)}, bf16[136,1536]{1,0:T(8,128)(2,1)S(1)}, u32[]{:S(2)}, u32[]{:S(2)}) collective-permute-start(bf16[136,1536]{1,0:T(8,128)(2,1)S(1)} %collective-permute-done.1.refs_0_.refs_2_), channel_id=1, source_target_pairs={{0,32},{16,496},{32,64},{48,16},{64,96},{80,48},{96,128},{112,80},... | collective-permute-start | bytes 1253384 | tf_op jit(solution)/shard_map/ppermute | solution.py:309
  26.7 0.0 collective-permute-done.10.refs_1_.refs_3_
  26.7 4.5 %collective-permute-start.11 = (bf16[136,1536]{1,0:T(8,128)(2,1)S(1)}, bf16[136,1536]{1,0:T(8,128)(2,1)S(1)}, u32[]{:S(2)}, u32[]{:S(2)}) collective-permute-start(bf16[136,1536]{1,0:T(8,128)(2,1)S(1)} %collective-permute-done.10.refs_1_.refs_3_), channel_id=1, source_target_pairs={{0,32},{16,496},{32,64},{48,16},{64,96},{80,48},{96,128},{112,80},... | collective-permute-start | bytes 1253384 | tf_op jit(solution)/shard_map/ppermute | solution.py:309
  31.2 0.5 collective-permute-done.2.refs_0_.refs_2_
  31.7 5.0 %collective-permute-start.3 = (bf16[136,1536]{1,0:T(8,128)(2,1)S(1)}, bf16[136,1536]{1,0:T(8,128)(2,1)S(1)}, u32[]{:S(2)}, u32[]{:S(2)}) collective-permute-start(bf16[136,1536]{1,0:T(8,128)(2,1)S(1)} %collective-permute-done.2.refs_0_.refs_2_), channel_id=1, source_target_pairs={{0,32},{16,496},{32,64},{48,16},{64,96},{80,48},{96,128},{112,80},... | collective-permute-start | bytes 1253384 | tf_op jit(solution)/shard_map/ppermute | solution.py:309
  36.7 0.0 collective-permute-done.11.refs_1_.refs_3_
  36.7 4.5 %collective-permute-start.12 = (bf16[136,1536]{1,0:T(8,128)(2,1)S(1)}, bf16[136,1536]{1,0:T(8,128)(2,1)S(1)}, u32[]{:S(2)}, u32[]{:S(2)}) collective-permute-start(bf16[136,1536]{1,0:T(8,128)(2,1)S(1)} %collective-permute-done.11.refs_1_.refs_3_), channel_id=1, source_target_pairs={{0,32},{16,496},{32,64},{48,16},{64,96},{80,48},{96,128},{112,80},... | collective-permute-start | bytes 1253384 | tf_op jit(solution)/shard_map/ppermute | solution.py:309
  41.2 0.5 collective-permute-done.3.refs_0_.refs_2_.refs_4_
  41.7 5.0 %collective-permute-start.4 = (bf16[136,1536]{1,0:T(8,128)(2,1)S(1)}, bf16[136,1536]{1,0:T(8,128)(2,1)S(1)}, u32[]{:S(2)}, u32[]{:S(2)}) collective-permute-start(bf16[136,1536]{1,0:T(8,128)(2,1)S(1)} %collective-permute-done.3.refs_0_.refs_2_.refs_4_), channel_id=1, source_target_pairs={{0,32},{16,496},{32,64},{48,16},{64,96},{80,48},{96,128},{112,80},... | collective-permute-start | bytes 1253384 | tf_op jit(solution)/shard_map/ppermute | solution.py:309
  46.7 0.0 collective-permute-done.12.refs_1_.refs_3_.refs_5_
  46.7 4.5 %collective-permute-start.13 = (bf16[136,1536]{1,0:T(8,128)(2,1)S(1)}, bf16[136,1536]{1,0:T(8,128)(2,1)S(1)}, u32[]{:S(2)}, u32[]{:S(2)}) collective-permute-start(bf16[136,1536]{1,0:T(8,128)(2,1)S(1)} %collective-permute-done.12.refs_1_.refs_3_.refs_5_), channel_id=1, source_target_pairs={{0,32},{16,496},{32,64},{48,16},{64,96},{80,48},{96,128},{112,80},... | collective-permute-start | bytes 1253384 | tf_op jit(solution)/shard_map/ppermute | solution.py:309
  51.2 0.5 collective-permute-done.4.refs_0_.refs_2_.refs_6_
  51.7 5.0 %collective-permute-start.5 = (bf16[136,1536]{1,0:T(8,128)(2,1)S(1)}, bf16[136,1536]{1,0:T(8,128)(2,1)S(1)}, u32[]{:S(2)}, u32[]{:S(2)}) collective-permute-start(bf16[136,1536]{1,0:T(8,128)(2,1)S(1)} %collective-permute-done.4.refs_0_.refs_2_.refs_6_), channel_id=1, source_target_pairs={{0,32},{16,496},{32,64},{48,16},{64,96},{80,48},{96,128},{112,80},... | collective-permute-start | bytes 1253384 | tf_op jit(solution)/shard_map/ppermute | solution.py:309
  56.7 4.5 %collective-permute-start.14 = (bf16[136,1536]{1,0:T(8,128)(2,1)S(1)}, bf16[136,1536]{1,0:T(8,128)(2,1)S(1)}, u32[]{:S(2)}, u32[]{:S(2)}) collective-permute-start(bf16[136,1536]{1,0:T(8,128)(2,1)S(1)} %collective-permute-done.13.refs_1_.refs_3_.refs_7_), channel_id=1, source_target_pairs={{0,32},{16,496},{32,64},{48,16},{64,96},{80,48},{96,128},{112,80},... | collective-permute-start | bytes 1253384 | tf_op jit(solution)/shard_map/ppermute | solution.py:309
  61.2 0.5 collective-permute-done.5.refs_0_.refs_2_.refs_8_
  61.6 5.0 %collective-permute-start.6 = (bf16[136,1536]{1,0:T(8,128)(2,1)S(1)}, bf16[136,1536]{1,0:T(8,128)(2,1)S(1)}, u32[]{:S(2)}, u32[]{:S(2)}) collective-permute-start(bf16[136,1536]{1,0:T(8,128)(2,1)S(1)} %collective-permute-done.5.refs_0_.refs_2_.refs_8_), channel_id=1, source_target_pairs={{0,32},{16,496},{32,64},{48,16},{64,96},{80,48},{96,128},{112,80},... | collective-permute-start | bytes 1253384 | tf_op jit(solution)/shard_map/ppermute | solution.py:309
  66.7 4.5 %collective-permute-start.15 = (bf16[136,1536]{1,0:T(8,128)(2,1)S(1)}, bf16[136,1536]{1,0:T(8,128)(2,1)S(1)}, u32[]{:S(2)}, u32[]{:S(2)}) collective-permute-start(bf16[136,1536]{1,0:T(8,128)(2,1)S(1)} %collective-permute-done.14.refs_1_.refs_3_.refs_9_), channel_id=1, source_target_pairs={{0,32},{16,496},{32,64},{48,16},{64,96},{80,48},{96,128},{112,80},... | collective-permute-start | bytes 1253384 | tf_op jit(solution)/shard_map/ppermute | solution.py:309
  71.1 0.5 collective-permute-done.6.refs_0_.refs_2_.refs_10_
  71.6 5.0 %collective-permute-start.7 = (bf16[136,1536]{1,0:T(8,128)(2,1)S(1)}, bf16[136,1536]{1,0:T(8,128)(2,1)S(1)}, u32[]{:S(2)}, u32[]{:S(2)}) collective-permute-start(bf16[136,1536]{1,0:T(8,128)(2,1)S(1)} %collective-permute-done.6.refs_0_.refs_2_.refs_10_), channel_id=1, source_target_pairs={{0,32},{16,496},{32,64},{48,16},{64,96},{80,48},{96,128},{112,80},... | collective-permute-start | bytes 1253384 | tf_op jit(solution)/shard_map/ppermute | solution.py:309
  76.7 5.9 %collective-permute-start = (bf16[90,1536]{1,0:T(8,128)(2,1)}, bf16[90,1536]{1,0:T(8,128)(2,1)S(1)}, u32[]{:S(2)}, u32[]{:S(2)}) collective-permute-start(bf16[90,1536]{1,0:T(8,128)(2,1)} %bitcast.4), channel_id=1, source_target_pairs={{0,16},{16,0},{32,48},{48,32},{64,80},{80,64},{96,112},{112,96},{1... | collective-permute-start | bytes 829448 | tf_op jit(solution)/shard_map/ppermute | solution.py:312
  82.5 0.0 collective-permute-done.15.refs_1_.refs_3_.refs_11_
  82.6 4.9 %collective-permute-start.16 = (bf16[136,1536]{1,0:T(8,128)(2,1)S(1)}, bf16[136,1536]{1,0:T(8,128)(2,1)S(1)}, u32[]{:S(2)}, u32[]{:S(2)}) collective-permute-start(bf16[136,1536]{1,0:T(8,128)(2,1)S(1)} %collective-permute-done.15.refs_1_.refs_3_.refs_11_), channel_id=1, source_target_pairs={{0,32},{16,496},{32,64},{48,16},{64,96},{80,48},{96,128},{112,80},... | collective-permute-start | bytes 1253384 | tf_op jit(solution)/shard_map/ppermute | solution.py:309
  87.4 1.9 %collective-permute-start.8 = (bf16[136,1536]{1,0:T(8,128)(2,1)S(1)}, bf16[136,1536]{1,0:T(8,128)(2,1)S(1)}, u32[]{:S(2)}, u32[]{:S(2)}) collective-permute-start(bf16[136,1536]{1,0:T(8,128)(2,1)S(1)} %collective-permute-done.7.refs_0_.refs_2_.refs_12_), channel_id=1, source_target_pairs={{0,32},{16,496},{32,64},{48,16},{64,96},{80,48},{96,128},{112,80},... | collective-permute-start | bytes 1253384 | tf_op jit(solution)/shard_map/ppermute | solution.py:309
  89.4 0.0 collective-permute-done
  89.5 0.3 own_tangents.1.own_ref
  89.8 0.5 tangents.7
  90.3 0.5 tangents.8
  90.8 0.5 tangents.9
  91.2 0.5 tangents.10
  91.7 0.5 tangents.11
  92.2 0.5 tangents.12
  92.7 0.5 tangents.13
  93.2 3.6 %collective-permute-done.8.rows_ref.refs_1_.refs_15_ = bf16[136,1536]{1,0:T(8,128)(2,1)S(1)} collective-permute-done((bf16[136,1536]{1,0:T(8,128)(2,1)S(1)}, bf16[136,1536]{1,0:T(8,128)(2,1)S(1)}, u32[]{:S(2)}, u32[]{:S(2)}) %collective-permute-start.8) | collective-permute-done | bytes 417824 | tf_op jit(solution)/shard_map/ppermute | solution.py:309
  96.9 0.6 last_tangents.1
  97.5 0.0 copy-start.1
  97.5 16.9 %all_to_all.10.in_ref = bf16[16,24,8,128]{3,2,1,0:T(8,128)(2,1)S(1)} all-to-all(bf16[16,24,8,128]{3,2,1,0:T(8,128)(2,1)S(1)} %last_tangents.1), channel_id=1, replica_groups=mesh['dp'=32,'expert'=16] {'expert'}, dimensions={0} | all-to-all | bytes 1572864 | tf_op jit(solution)/shard_map/all_to_all | solution.py:337
  114.4 0.5 combine.1
  114.9 13.6 %all_to_all.11.in_ref = bf16[16,24,8,128]{3,2,1,0:T(8,128)(2,1)S(1)} all-to-all(bf16[16,24,8,128]{3,2,1,0:T(8,128)(2,1)S(1)} %combine.1), channel_id=1, replica_groups=mesh['dp'=32,'expert'=16] {'expert'}, dimensions={0} | all-to-all | bytes 1572864 | tf_op jit(solution)/shard_map/all_to_all | solution.py:339
  128.5 3.6 %gradients.1 = (f32[1080,128]{1,0:T(8,128)S(1)}, f32[1080,128]{1,0:T(8,128)S(1)}) custom-call(bf16[16,24,8,128]{3,2,1,0:T(8,128)(2,1)S(1)} %all_to_all.11.in_ref, bf16[136,1536]{1,0:T(8,128)(2,1)S(1)} %collective-permute-done.1.refs_0_.refs_2_, bf16[136,1536]{1,0:T(8,128)(2,1)S(1)} %collective-permute-done.10.refs_1_.refs_3_, ...), custom_call_target="tpu_custom_call" | custom-call | flops 1207959552 | bytes 6291456 | tf_op jit(solution)/shard_map/gradients/pallas_call | solution.py:283
  132.1 8.6 %collective-permute-start.17 = (f32[1080,128]{1,0:T(8,128)S(1)}, f32[1080,128]{1,0:T(8,128)S(1)}, u32[]{:S(2)}, u32[]{:S(2)}) collective-permute-start(f32[1080,128]{1,0:T(8,128)S(1)} %get-tuple-element.36), channel_id=1, source_target_pairs={{0,16},{16,0},{32,48},{48,32},{64,80},{80,64},{96,112},{112,96},{1... | collective-permute-start | bytes 1658888 | tf_op jit(solution)/shard_map/ppermute | solution.py:312
  140.7 1.6 %collective-permute-done.17 = f32[1080,128]{1,0:T(8,128)S(1)} collective-permute-done((f32[1080,128]{1,0:T(8,128)S(1)}, f32[1080,128]{1,0:T(8,128)S(1)}, u32[]{:S(2)}, u32[]{:S(2)}) %collective-permute-start.17) | collective-permute-done | bytes 552992 | tf_op jit(solution)/shard_map/ppermute | solution.py:312
  142.3 0.9 add.3
  (11 shorter events, 0.1 us)
Async XLA Ops:
  0.0 89.4 %copy-start.2 = (bf16[1,90,1536]{2,1,0:T(8,128)(2,1)S(1)}, bf16[1,90,1536]{2,1,0:T(8,128)(2,1)}, u32[]{:S(2)}) copy-start(bf16[1,90,1536]{2,1,0:T(8,128)(2,1)} %param.5) | copy-start | bytes 829444
  0.0 89.4 %copy-start = (bf16[128,1536]{1,0:T(8,128)(2,1)S(1)}, bf16[128,1536]{1,0:T(8,128)(2,1)}, u32[]{:S(2)}) copy-start(bf16[128,1536]{1,0:T(8,128)(2,1)} %refs_14_.1) | copy-start | bytes 1179652
  2.0 14.5 %collective-permute-start.9 = (bf16[136,1536]{1,0:T(8,128)(2,1)}, bf16[136,1536]{1,0:T(8,128)(2,1)S(1)}, u32[]{:S(2)}, u32[]{:S(2)}) collective-permute-start(bf16[136,1536]{1,0:T(8,128)(2,1)} %message.1.refs_0_), channel_id=1, source_target_pairs={{0,16},{16,0},{32,48},{48,32},{64,80},{80,64},{96,112},{112,96},{1... | collective-permute-start | bytes 1253384 | tf_op jit(solution)/shard_map/ppermute | solution.py:312
  10.8 11.1 %collective-permute-start.1 = (bf16[136,1536]{1,0:T(8,128)(2,1)}, bf16[136,1536]{1,0:T(8,128)(2,1)S(1)}, u32[]{:S(2)}, u32[]{:S(2)}) collective-permute-start(bf16[136,1536]{1,0:T(8,128)(2,1)} %message.1.refs_0_), channel_id=1, source_target_pairs={{0,32},{16,496},{32,64},{48,16},{64,96},{80,48},{96,128},{112,80},... | collective-permute-start | bytes 1253384 | tf_op jit(solution)/shard_map/ppermute | solution.py:309
  16.5 10.2 %collective-permute-start.10 = (bf16[136,1536]{1,0:T(8,128)(2,1)S(1)}, bf16[136,1536]{1,0:T(8,128)(2,1)S(1)}, u32[]{:S(2)}, u32[]{:S(2)}) collective-permute-start(bf16[136,1536]{1,0:T(8,128)(2,1)S(1)} %collective-permute-done.9), channel_id=1, source_target_pairs={{0,32},{16,496},{32,64},{48,16},{64,96},{80,48},{96,128},{112,80},... | collective-permute-start | bytes 1253384 | tf_op jit(solution)/shard_map/ppermute | solution.py:309
  21.8 9.9 %collective-permute-start.2 = (bf16[136,1536]{1,0:T(8,128)(2,1)S(1)}, bf16[136,1536]{1,0:T(8,128)(2,1)S(1)}, u32[]{:S(2)}, u32[]{:S(2)}) collective-permute-start(bf16[136,1536]{1,0:T(8,128)(2,1)S(1)} %collective-permute-done.1.refs_0_.refs_2_), channel_id=1, source_target_pairs={{0,32},{16,496},{32,64},{48,16},{64,96},{80,48},{96,128},{112,80},... | collective-permute-start | bytes 1253384 | tf_op jit(solution)/shard_map/ppermute | solution.py:309
  26.7 10.0 %collective-permute-start.11 = (bf16[136,1536]{1,0:T(8,128)(2,1)S(1)}, bf16[136,1536]{1,0:T(8,128)(2,1)S(1)}, u32[]{:S(2)}, u32[]{:S(2)}) collective-permute-start(bf16[136,1536]{1,0:T(8,128)(2,1)S(1)} %collective-permute-done.10.refs_1_.refs_3_), channel_id=1, source_target_pairs={{0,32},{16,496},{32,64},{48,16},{64,96},{80,48},{96,128},{112,80},... | collective-permute-start | bytes 1253384 | tf_op jit(solution)/shard_map/ppermute | solution.py:309
  31.7 10.0 %collective-permute-start.3 = (bf16[136,1536]{1,0:T(8,128)(2,1)S(1)}, bf16[136,1536]{1,0:T(8,128)(2,1)S(1)}, u32[]{:S(2)}, u32[]{:S(2)}) collective-permute-start(bf16[136,1536]{1,0:T(8,128)(2,1)S(1)} %collective-permute-done.2.refs_0_.refs_2_), channel_id=1, source_target_pairs={{0,32},{16,496},{32,64},{48,16},{64,96},{80,48},{96,128},{112,80},... | collective-permute-start | bytes 1253384 | tf_op jit(solution)/shard_map/ppermute | solution.py:309
  36.7 10.0 %collective-permute-start.12 = (bf16[136,1536]{1,0:T(8,128)(2,1)S(1)}, bf16[136,1536]{1,0:T(8,128)(2,1)S(1)}, u32[]{:S(2)}, u32[]{:S(2)}) collective-permute-start(bf16[136,1536]{1,0:T(8,128)(2,1)S(1)} %collective-permute-done.11.refs_1_.refs_3_), channel_id=1, source_target_pairs={{0,32},{16,496},{32,64},{48,16},{64,96},{80,48},{96,128},{112,80},... | collective-permute-start | bytes 1253384 | tf_op jit(solution)/shard_map/ppermute | solution.py:309
  41.7 10.0 %collective-permute-start.4 = (bf16[136,1536]{1,0:T(8,128)(2,1)S(1)}, bf16[136,1536]{1,0:T(8,128)(2,1)S(1)}, u32[]{:S(2)}, u32[]{:S(2)}) collective-permute-start(bf16[136,1536]{1,0:T(8,128)(2,1)S(1)} %collective-permute-done.3.refs_0_.refs_2_.refs_4_), channel_id=1, source_target_pairs={{0,32},{16,496},{32,64},{48,16},{64,96},{80,48},{96,128},{112,80},... | collective-permute-start | bytes 1253384 | tf_op jit(solution)/shard_map/ppermute | solution.py:309
  46.7 10.0 %collective-permute-start.13 = (bf16[136,1536]{1,0:T(8,128)(2,1)S(1)}, bf16[136,1536]{1,0:T(8,128)(2,1)S(1)}, u32[]{:S(2)}, u32[]{:S(2)}) collective-permute-start(bf16[136,1536]{1,0:T(8,128)(2,1)S(1)} %collective-permute-done.12.refs_1_.refs_3_.refs_5_), channel_id=1, source_target_pairs={{0,32},{16,496},{32,64},{48,16},{64,96},{80,48},{96,128},{112,80},... | collective-permute-start | bytes 1253384 | tf_op jit(solution)/shard_map/ppermute | solution.py:309
  51.7 10.0 %collective-permute-start.5 = (bf16[136,1536]{1,0:T(8,128)(2,1)S(1)}, bf16[136,1536]{1,0:T(8,128)(2,1)S(1)}, u32[]{:S(2)}, u32[]{:S(2)}) collective-permute-start(bf16[136,1536]{1,0:T(8,128)(2,1)S(1)} %collective-permute-done.4.refs_0_.refs_2_.refs_6_), channel_id=1, source_target_pairs={{0,32},{16,496},{32,64},{48,16},{64,96},{80,48},{96,128},{112,80},... | collective-permute-start | bytes 1253384 | tf_op jit(solution)/shard_map/ppermute | solution.py:309
  56.7 10.0 %collective-permute-start.14 = (bf16[136,1536]{1,0:T(8,128)(2,1)S(1)}, bf16[136,1536]{1,0:T(8,128)(2,1)S(1)}, u32[]{:S(2)}, u32[]{:S(2)}) collective-permute-start(bf16[136,1536]{1,0:T(8,128)(2,1)S(1)} %collective-permute-done.13.refs_1_.refs_3_.refs_7_), channel_id=1, source_target_pairs={{0,32},{16,496},{32,64},{48,16},{64,96},{80,48},{96,128},{112,80},... | collective-permute-start | bytes 1253384 | tf_op jit(solution)/shard_map/ppermute | solution.py:309
  61.6 10.0 %collective-permute-start.6 = (bf16[136,1536]{1,0:T(8,128)(2,1)S(1)}, bf16[136,1536]{1,0:T(8,128)(2,1)S(1)}, u32[]{:S(2)}, u32[]{:S(2)}) collective-permute-start(bf16[136,1536]{1,0:T(8,128)(2,1)S(1)} %collective-permute-done.5.refs_0_.refs_2_.refs_8_), channel_id=1, source_target_pairs={{0,32},{16,496},{32,64},{48,16},{64,96},{80,48},{96,128},{112,80},... | collective-permute-start | bytes 1253384 | tf_op jit(solution)/shard_map/ppermute | solution.py:309
  66.7 15.9 %collective-permute-start.15 = (bf16[136,1536]{1,0:T(8,128)(2,1)S(1)}, bf16[136,1536]{1,0:T(8,128)(2,1)S(1)}, u32[]{:S(2)}, u32[]{:S(2)}) collective-permute-start(bf16[136,1536]{1,0:T(8,128)(2,1)S(1)} %collective-permute-done.14.refs_1_.refs_3_.refs_9_), channel_id=1, source_target_pairs={{0,32},{16,496},{32,64},{48,16},{64,96},{80,48},{96,128},{112,80},... | collective-permute-start | bytes 1253384 | tf_op jit(solution)/shard_map/ppermute | solution.py:309
  71.6 15.8 %collective-permute-start.7 = (bf16[136,1536]{1,0:T(8,128)(2,1)S(1)}, bf16[136,1536]{1,0:T(8,128)(2,1)S(1)}, u32[]{:S(2)}, u32[]{:S(2)}) collective-permute-start(bf16[136,1536]{1,0:T(8,128)(2,1)S(1)} %collective-permute-done.6.refs_0_.refs_2_.refs_10_), channel_id=1, source_target_pairs={{0,32},{16,496},{32,64},{48,16},{64,96},{80,48},{96,128},{112,80},... | collective-permute-start | bytes 1253384 | tf_op jit(solution)/shard_map/ppermute | solution.py:309
  76.7 12.7 %collective-permute-start = (bf16[90,1536]{1,0:T(8,128)(2,1)}, bf16[90,1536]{1,0:T(8,128)(2,1)S(1)}, u32[]{:S(2)}, u32[]{:S(2)}) collective-permute-start(bf16[90,1536]{1,0:T(8,128)(2,1)} %bitcast.4), channel_id=1, source_target_pairs={{0,16},{16,0},{32,48},{48,32},{64,80},{80,64},{96,112},{112,96},{1... | collective-permute-start | bytes 829448 | tf_op jit(solution)/shard_map/ppermute | solution.py:312
  82.6 10.2 %collective-permute-start.16 = (bf16[136,1536]{1,0:T(8,128)(2,1)S(1)}, bf16[136,1536]{1,0:T(8,128)(2,1)S(1)}, u32[]{:S(2)}, u32[]{:S(2)}) collective-permute-start(bf16[136,1536]{1,0:T(8,128)(2,1)S(1)} %collective-permute-done.15.refs_1_.refs_3_.refs_11_), channel_id=1, source_target_pairs={{0,32},{16,496},{32,64},{48,16},{64,96},{80,48},{96,128},{112,80},... | collective-permute-start | bytes 1253384 | tf_op jit(solution)/shard_map/ppermute | solution.py:309
  87.4 9.4 %collective-permute-start.8 = (bf16[136,1536]{1,0:T(8,128)(2,1)S(1)}, bf16[136,1536]{1,0:T(8,128)(2,1)S(1)}, u32[]{:S(2)}, u32[]{:S(2)}) collective-permute-start(bf16[136,1536]{1,0:T(8,128)(2,1)S(1)} %collective-permute-done.7.refs_0_.refs_2_.refs_12_), channel_id=1, source_target_pairs={{0,32},{16,496},{32,64},{48,16},{64,96},{80,48},{96,128},{112,80},... | collective-permute-start | bytes 1253384 | tf_op jit(solution)/shard_map/ppermute | solution.py:309
  97.5 16.9 %copy-start.1 = (bf16[136,1536]{1,0:T(8,128)(2,1)S(1)}, bf16[136,1536]{1,0:T(8,128)(2,1)}, u32[]{:S(2)}) copy-start(bf16[136,1536]{1,0:T(8,128)(2,1)} %message.1.refs_0_) | copy-start | bytes 1253380
  132.1 10.2 %collective-permute-start.17 = (f32[1080,128]{1,0:T(8,128)S(1)}, f32[1080,128]{1,0:T(8,128)S(1)}, u32[]{:S(2)}, u32[]{:S(2)}) collective-permute-start(f32[1080,128]{1,0:T(8,128)S(1)} %get-tuple-element.36), channel_id=1, source_target_pairs={{0,16},{16,0},{32,48},{48,32},{64,80},{80,64},{96,112},{112,96},{1... | collective-permute-start | bytes 1658888 | tf_op jit(solution)/shard_map/ppermute | solution.py:312

commit v2 on v1

--- a/solution.py
+++ b/solution.py
@@ -32,7 +32,8 @@
     return pl.CostEstimate(flops=flops, bytes_accessed=nbytes, transcendentals=0)
 
 
-def message_kernel(capacity, experts, rows_hbm, ids_hbm, gates_hbm, out_ref, ids_ref, gates_ref, sems):
+def message_kernel(capacity, experts, *refs):
+    rows_hbm, ids_hbm, gates_hbm, dir_hbm, out_ref, head_ref, ids_ref, gates_ref, dir_ref, sems = refs
     topk, tokens = ids_ref.shape
     slots = experts * capacity
     span, width = rows_hbm.shape
@@ -40,10 +41,12 @@
         pltpu.make_async_copy(rows_hbm, out_ref.at[:span], sems.at[0]),
         pltpu.make_async_copy(ids_hbm, ids_ref, sems.at[1]),
         pltpu.make_async_copy(gates_hbm, gates_ref, sems.at[2]),
+        pltpu.make_async_copy(rows_hbm.at[: head_ref.shape[0]], head_ref, sems.at[3]),
+        pltpu.make_async_copy(dir_hbm, dir_ref, sems.at[4]),
     ]
     for copy in copies:
         copy.start()
-    for copy in copies[1:]:
+    for copy in copies[1:3]:
         copy.wait()
     slot = lax.broadcasted_iota(jnp.int32, (slots, tokens), 0)
     expert = slot // capacity
@@ -73,28 +76,58 @@
         total += lax.dot_general(
             rows, holds, (((1,), (1,)), ((), ())), preferred_element_type=jnp.float32
         )
-    out_ref[span:] = jnp.concatenate(
+    out_ref[span + FEATS :] = jnp.concatenate(
         [total, jnp.zeros((TAB, width - slots), jnp.float32)], axis=1
     ).astype(out_ref.dtype)
+    feats = dir_ref.shape[0]
+    copies[4].wait()
+    out_ref[span : span + feats] = dir_ref[...]
+    out_ref[span + feats : span + FEATS] = jnp.zeros((FEATS - feats, width), out_ref.dtype)
     copies[0].wait()
-
-
-def message(rows, ids, gates, experts, capacity):
-    args = (rows, ids.T, gates.T)
-    shape = (rows.shape[0] + TAB, rows.shape[1])
+    copies[3].wait()
+
+
+def message(rows, ids, gates, dirs, experts, capacity, cut):
+    args = (rows, ids.T, gates.T, dirs)
+    span, width = rows.shape
     return pl.pallas_call(
         functools.partial(message_kernel, capacity, experts),
-        out_shape=jax.ShapeDtypeStruct(shape, jnp.bfloat16),
-        in_specs=[pl.BlockSpec(memory_space=pltpu.HBM)] * 3,
-        out_specs=whole(),
-        scratch_shapes=[
-            pltpu.VMEM(args[1].shape, args[1].dtype),
-            pltpu.VMEM(args[2].shape, args[2].dtype),
-            pltpu.SemaphoreType.DMA((3,)),
+        out_shape=[
+            jax.ShapeDtypeStruct((span + TAB + FEATS, width), jnp.bfloat16),
+            jax.ShapeDtypeStruct((cut, width), jnp.bfloat16),
         ],
+        in_specs=[pl.BlockSpec(memory_space=pltpu.HBM)] * 4,
+        out_specs=[whole(), whole()],
+        scratch_shapes=[pltpu.VMEM(x.shape, x.dtype) for x in args[1:]]
+        + [pltpu.SemaphoreType.DMA((5,))],
         cost_estimate=cost(10**7, 10**6),
         name="message",
     )(*args)
+
+
+def split(sent, other, span, cut, join):
+    width = sent.shape[1]
+    left = span - cut
+    sizes = (join + left + TAB, span - join + TAB, 2 * FEATS)
+
+    def kernel(sent_ref, other_ref, first_ref, second_ref, dir_ref):
+        first_ref[:join] = other_ref[:join]
+        first_ref[join : join + left] = sent_ref[cut:span]
+        first_ref[join + left :] = sent_ref[span + FEATS :]
+        second_ref[: span - join] = other_ref[join:span]
+        second_ref[span - join :] = other_ref[span + FEATS :]
+        dir_ref[:FEATS] = sent_ref[span : span + FEATS]
+        dir_ref[FEATS:] = other_ref[span : span + FEATS]
+
+    return pl.pallas_call(
+        kernel,
+        out_shape=[jax.ShapeDtypeStruct((size, width), sent.dtype) for size in sizes],
+        in_specs=[whole()] * 2,
+        out_specs=[whole()] * 3,
+        compiler_params=params(),
+        cost_estimate=cost(0, 4 * sent.size),
+        name="split",
+    )(sent, other)
 
 
 def table_of(rows):
@@ -126,18 +159,23 @@
         out_ref[:, i] = value.reshape(sources, -1, LANES).astype(jnp.bfloat16)
 
 
-def tangents(pair, pieces, dirs, kept, shape, mix_shape, scale):
+def parts_of(span, cut, join):
+    left = span - cut
+    return ((0, 0, cut), (1, join, join + left), (1, 0, join), (2, 0, span - join))
+
+
+def tangents(pair, pieces, parts, dirs, kept, shape, mix_shape, scale):
     sources, _, capacity, _ = shape
     span = sources * capacity
-    args = list(pieces) + list(pieces) + [dirs] + list(kept)
+    args = list(pieces) + list(pieces[1:]) + [dirs] + list(kept)
 
     def kernel(*refs):
-        dir_ref, out_ref, mix_ref = refs[4], refs[-2], refs[-1]
-        rows = jnp.concatenate([refs[i][:span, :] for i in range(2)], axis=0)
+        dir_ref, out_ref, mix_ref = refs[5], refs[-2], refs[-1]
+        rows = jnp.concatenate([refs[i][a:b, :] for i, a, b in parts], axis=0)
         value = project(rows, dir_ref[...])
         pack(out_ref, [value[:span], value[span:]])
         for i in range(2):
-            mix_ref[i] = mix_of(refs[2 + i][...], scale)
+            mix_ref[i] = mix_of(refs[3 + i][...], scale)
 
     return pl.pallas_call(
         kernel,
@@ -147,14 +185,14 @@
             jax.ShapeDtypeStruct(mix_shape, jnp.bfloat16),
         ],
         in_specs=[full(x) for x in pieces]
-        + [table_of(x) for x in pieces]
+        + [table_of(x) for x in pieces[1:]]
         + [full(dirs)]
         + [pl.BlockSpec(memory_space=pl.ANY)] * len(kept),
         out_specs=[
             pl.BlockSpec((sources, 3, capacity, LANES), lambda i: (0, pair, 0, 0)),
             pl.BlockSpec((2,) + mix_shape[1:], lambda i: (pair, 0, 0)),
         ],
-        input_output_aliases={5 + i: i for i in range(len(kept))},
+        input_output_aliases={6 + i: i for i in range(len(kept))},
         compiler_params=params(),
         cost_estimate=cost(4 * span * dirs.size, 2 * 2 * span * dirs.shape[1] + 2 * dirs.size),
         name="tangents",
@@ -176,29 +214,26 @@
     )(rows, dirs)
 
 
-def last_tangents(pair, own, rows, dirs, packed):
+def last_tangents(pair, own, first, second, dirs, packed):
     sources, _, capacity, _ = packed.shape
-    span = sources * capacity
-
-    def kernel(own_ref, rows_ref, dir_ref, _, out_ref, held_ref, sem):
-        copy = pltpu.make_async_copy(rows_ref, held_ref, sem)
-        copy.start()
-        copy.wait()
-        pack(out_ref, [own_ref[...], project(held_ref[:span, :], dir_ref[...])])
+    left = sources * capacity - first.shape[0]
+
+    def kernel(own_ref, first_ref, second_ref, dir_ref, _, out_ref):
+        rows = jnp.concatenate([first_ref[...], second_ref[:left, :]], axis=0)
+        pack(out_ref, [own_ref[...], project(rows, dir_ref[...])])
 
     return pl.pallas_call(
         kernel,
         grid=(1,),
         out_shape=jax.ShapeDtypeStruct(packed.shape, packed.dtype),
-        in_specs=[full(own), pl.BlockSpec(memory_space=pltpu.HBM), full(dirs)]
+        in_specs=[full(x) for x in (own, first, second, dirs)]
         + [pl.BlockSpec(memory_space=pl.ANY)],
         out_specs=pl.BlockSpec((sources, 3, capacity, LANES), lambda i: (0, pair, 0, 0)),
-        scratch_shapes=[pltpu.VMEM(rows.shape, rows.dtype), pltpu.SemaphoreType.DMA],
-        input_output_aliases={3: 0},
+        input_output_aliases={4: 0},
         compiler_params=params(),
         cost_estimate=cost(2 * own.shape[0] * dirs.size, 2 * dirs.size),
         name="last_tangents",
-    )(own, rows, dirs, packed)
+    )(own, first, second, dirs, packed)
 
 
 def combine(packed, mixes, tables, scale):
@@ -244,7 +279,7 @@
     )(packed, mixes, *tables)
 
 
-def gradients(packed, groups, feats):
+def gradients(packed, groups, parts, feats):
     sources, slabs, capacity, _ = packed.shape
     span = sources * capacity
     pairs = slabs // 3
@@ -259,19 +294,25 @@
 
         @pl.when(column == 0)
         def _():
-            def load(slab):
-                return in_ref[:, slab].astype(jnp.float32).reshape(span, LANES)
+            def turned(slab):
+                rows = in_ref[:, slab].astype(jnp.float32).reshape(span, LANES)
+                return rows.astype(jnp.bfloat16).T
 
             for pair in range(pairs):
-                main = jnp.concatenate([load(3 * pair).T, load(3 * pair + 1).T], axis=1)
-                tail = load(3 * pair + 2).T
-                tail = jnp.concatenate([tail[: LANES // 2], tail[LANES // 2 :]], axis=1)
-                lhs_ref[pair] = jnp.concatenate([main, tail], axis=0).astype(jnp.bfloat16)
+                lhs_ref[pair, :LANES, :span] = turned(3 * pair)
+                lhs_ref[pair, :LANES, span:] = turned(3 * pair + 1)
+                tail = turned(3 * pair + 2)
+                lhs_ref[pair, LANES:, :span] = tail[: LANES // 2]
+                lhs_ref[pair, LANES:, span:] = tail[LANES // 2 :]
 
         total = None
+        at = 0
         for pair in range(pairs):
-            rows = jnp.concatenate([refs[2 * pair + i][:span, :] for i in range(2)], axis=0)
-            term = jnp.dot(lhs_ref[pair], rows, preferred_element_type=jnp.float32)
+            rows = [refs[at + i][a:b, :] for i, a, b in parts[pair]]
+            at += len(groups[pair])
+            term = jnp.dot(
+                lhs_ref[pair], jnp.concatenate(rows, axis=0), preferred_element_type=jnp.float32
+            )
             total = term if total is None else total + term
         for i in range(2):
             lanes = slice(i * LANES, (i + 1) * LANES)
@@ -311,33 +352,37 @@
     def swap(x):
         return lax.ppermute(x, "dp", partner)
 
-    sent = message(cached_hidden, expert_ids, gate_weights, experts, capacity)
+    cut = span * 3 // 4
+    join = span * 3 // 8
+    parts = parts_of(span, cut, join)
+    sent, head = message(
+        cached_hidden, expert_ids, gate_weights, direction[0], experts, capacity, cut
+    )
     other = swap(sent)
-    chain_a = [shift(sent)]
-    chain_b = [shift(other)]
-    other_dir = swap(direction[0])
-    pad = jnp.zeros((FEATS - feats, width), jnp.bfloat16)
-    dirs = jnp.concatenate([direction[0], pad, other_dir, pad], axis=0)
-    for _ in range(2, steps):
-        chain_a.append(shift(chain_a[-1]))
-        chain_b.append(shift(chain_b[-1]))
-    last = shift(chain_a[-1])
+    middle, final, dirs = split(sent, other, span, cut, join)
+    chain = [[shift(x)] for x in (head, middle, final)]
+    for s in range(2, steps + 1):
+        for k in range(3 if s < steps else 2):
+            x = chain[k][-1]
+            chain[k].append(shift(x[join:] if k == 1 and s == steps else x))
+    last = [chain[0][-1], chain[1][-1]]
     shape = (experts, 3 * steps, capacity, LANES)
     mix_shape = (2 * (steps - 1), span, 2 * span)
     kept = ()
     groups = []
     for s in range(1, steps):
-        pieces = [chain_a[s - 1], chain_b[s - 1]]
-        kept = tangents(s - 1, pieces, dirs, kept, shape, mix_shape, scale)
+        pieces = [chain[k][s - 1] for k in range(3)]
+        kept = tangents(s - 1, pieces, parts, dirs, kept, shape, mix_shape, scale)
         groups.append(pieces)
     packed, mixes = kept
     own = own_tangents(cached_hidden, dirs)
-    packed = last_tangents(steps - 1, own, last, dirs, packed)
-    groups.append([cached_hidden, last])
+    packed = last_tangents(steps - 1, own, last[0], last[1], dirs, packed)
+    groups.append([cached_hidden] + last)
+    places = [parts] * (steps - 1) + [((0, 0, span), (1, 0, cut), (2, 0, span - cut))]
     arrived = lax.all_to_all(packed, "expert", split_axis=0, concat_axis=0, tiled=True)
-    adjoint = combine(arrived, mixes, [sent, last], scale)
+    adjoint = combine(arrived, mixes, [middle, last[1]], scale)
     back = lax.all_to_all(adjoint, "expert", split_axis=0, concat_axis=0, tiled=True)
-    mine, theirs = gradients(back, groups, feats)
+    mine, theirs = gradients(back, groups, places, feats)
     theirs = swap(theirs)
     return (mine + theirs).reshape(1, feats, width)
 

time: 144 us -> 146 us (1.014)
  starting transfers between devices: 90.7 us -> 93.5 us
  waiting for transfers between devices: 10.3 us -> 8.44 us
    ppermute x15 -> x23, starting transfers between devices: 67.4 us -> 72 us  [shift(): return lax.ppermute(x, 'dp', ring)]
    ppermute x15 -> x23, waiting for transfers between devices: 8.72 us -> 6.88 us  [shift(): return lax.ppermute(x, 'dp', ring)]
    ppermute x3 -> x2, starting transfers between devices: 23.2 us -> 21.5 us  [swap(): return lax.ppermute(x, 'dp', partner)]
  transfers between devices with their start and end apart: 18 -> 25, of which waited for: 8 -> 4; matrix products, arithmetic and copies ran while one was open for 0% -> 0% of each run, Pallas kernels for 3% -> 3%
where the time goes in v2:
time: 146 us; the launch traced here: 145 us
  starting transfers between devices  93.5 us (64%)
  blocking collectives  30 us (21%)
  Pallas kernels  10.8 us (7%)
  waiting for transfers between devices  8.44 us (6%)
    ppermute x23, starting transfers between devices, shift(): return lax.ppermute(x, 'dp', ring)  72 us
    ppermute x2, starting transfers between devices, swap(): return lax.ppermute(x, 'dp', partner)  21.5 us
    all_to_all x1, blocking collectives, body(): lax.all_to_all(packed, 'expert', split_axis=0, concat_axis=0, tiled=True)  16.7 us
    all_to_all x1, blocking collectives, body(): lax.all_to_all(adjoint, 'expert', split_axis=0, concat_axis=0, tiled=True)  13.3 us
    ppermute x23, waiting for transfers between devices, shift(): return lax.ppermute(x, 'dp', ring)  6.88 us
    pallas_call x1, Pallas kernels, gradients(): pl.pallas_call(kernel, grid=(width // step,), out_shape=[shape, shape], i...  3.93 us
    pallas_call x7, Pallas kernels, tangents(): pl.pallas_call(kernel, grid=(1,), out_shape=[jax.ShapeDtypeStruct(shape,...  3.38 us
  transfers between devices with their start and end apart: 25, of which 4 were waited for; matrix products, arithmetic and copies ran while one was open for 0% of the time, Pallas kernels for 3%

profile of v2, /device:TPU:1, one launch (start us, length us, event | category | flops | bytes accessed | tf_op | source)
XLA Modules:
  0.0 145.3 jit_solution(16664009759305156591)
XLA Ops:
  0.0 2.2 %message.1 = (bf16[232,1536]{1,0:T(8,128)(2,1)}, bf16[96,1536]{1,0:T(8,128)(2,1)}) custom-call(bf16[128,1536]{1,0:T(8,128)(2,1)} %refs_21_.1, s32[4,128]{1,0:T(4,128)} %bitcast.5, f32[4,128]{1,0:T(4,128)} %bitcast.6, bf16[90,1536]{1,0:T(8,128)(2,1)} %bitcast.4), custom_call_target="tpu_custom_call" | custom-call | flops 10000000 | bytes 1000000 | tf_op jit(solution)/shard_map/message/pallas_call | solution.py:93
  2.2 8.7 %collective-permute-start = (bf16[232,1536]{1,0:T(8,128)(2,1)}, bf16[232,1536]{1,0:T(8,128)(2,1)S(1)}, u32[]{:S(2)}, u32[]{:S(2)}) collective-permute-start(bf16[232,1536]{1,0:T(8,128)(2,1)} %get-tuple-element.26.sent_ref), channel_id=1, source_target_pairs={{0,16},{16,0},{32,48},{48,32},{64,80},{80,64},{96,112},{112,96},{1... | collective-permute-start | bytes 2138120 | tf_op jit(solution)/shard_map/ppermute | solution.py:353
  11.0 5.8 %collective-permute-start.1 = (bf16[96,1536]{1,0:T(8,128)(2,1)}, bf16[96,1536]{1,0:T(8,128)(2,1)S(1)}, u32[]{:S(2)}, u32[]{:S(2)}) collective-permute-start(bf16[96,1536]{1,0:T(8,128)(2,1)} %get-tuple-element.28), channel_id=1, source_target_pairs={{0,32},{16,496},{32,64},{48,16},{64,96},{80,48},{96,128},{112,80},... | collective-permute-start | bytes 884744 | tf_op jit(solution)/shard_map/ppermute | solution.py:350
  16.8 4.0 %collective-permute-done.1.refs_0_ = bf16[96,1536]{1,0:T(8,128)(2,1)S(1)} collective-permute-done((bf16[96,1536]{1,0:T(8,128)(2,1)}, bf16[96,1536]{1,0:T(8,128)(2,1)S(1)}, u32[]{:S(2)}, u32[]{:S(2)}) %collective-permute-start.1) | collective-permute-done | bytes 294944 | tf_op jit(solution)/shard_map/ppermute | solution.py:350
  20.7 4.9 %collective-permute-start.2 = (bf16[96,1536]{1,0:T(8,128)(2,1)S(1)}, bf16[96,1536]{1,0:T(8,128)(2,1)S(1)}, u32[]{:S(2)}, u32[]{:S(2)}) collective-permute-start(bf16[96,1536]{1,0:T(8,128)(2,1)S(1)} %collective-permute-done.1.refs_0_), channel_id=1, source_target_pairs={{0,32},{16,496},{32,64},{48,16},{64,96},{80,48},{96,128},{112,80},... | collective-permute-start | bytes 884744 | tf_op jit(solution)/shard_map/ppermute | solution.py:350
  25.6 0.0 collective-permute-done.other_ref
  25.7 1.1 copy-done.1
  26.8 0.1 split.1
  26.8 2.1 %collective-permute-start.9 = (bf16[88,1536]{1,0:T(8,128)(2,1)S(1)}, bf16[88,1536]{1,0:T(8,128)(2,1)S(1)}, u32[]{:S(2)}, u32[]{:S(2)}) collective-permute-start(bf16[88,1536]{1,0:T(8,128)(2,1)S(1)} %get-tuple-element.29.refs_0_), channel_id=1, source_target_pairs={{0,32},{16,496},{32,64},{48,16},{64,96},{80,48},{96,128},{112,80},... | collective-permute-start | bytes 811016 | tf_op jit(solution)/shard_map/ppermute | solution.py:350
  28.9 2.4 %collective-permute-start.17 = (bf16[88,1536]{1,0:T(8,128)(2,1)S(1)}, bf16[88,1536]{1,0:T(8,128)(2,1)S(1)}, u32[]{:S(2)}, u32[]{:S(2)}) collective-permute-start(bf16[88,1536]{1,0:T(8,128)(2,1)S(1)} %get-tuple-element.30), channel_id=1, source_target_pairs={{0,32},{16,496},{32,64},{48,16},{64,96},{80,48},{96,128},{112,80},... | collective-permute-start | bytes 811016 | tf_op jit(solution)/shard_map/ppermute | solution.py:350
  31.3 0.0 collective-permute-done.2.refs_0_.refs_3_
  31.4 2.9 %collective-permute-start.3 = (bf16[96,1536]{1,0:T(8,128)(2,1)S(1)}, bf16[96,1536]{1,0:T(8,128)(2,1)S(1)}, u32[]{:S(2)}, u32[]{:S(2)}) collective-permute-start(bf16[96,1536]{1,0:T(8,128)(2,1)S(1)} %collective-permute-done.2.refs_0_.refs_3_), channel_id=1, source_target_pairs={{0,32},{16,496},{32,64},{48,16},{64,96},{80,48},{96,128},{112,80},... | collective-permute-start | bytes 884744 | tf_op jit(solution)/shard_map/ppermute | solution.py:350
  34.3 0.2 collective-permute-done.9.refs_1_.refs_3_
  34.5 4.3 %collective-permute-start.10 = (bf16[88,1536]{1,0:T(8,128)(2,1)S(1)}, bf16[88,1536]{1,0:T(8,128)(2,1)S(1)}, u32[]{:S(2)}, u32[]{:S(2)}) collective-permute-start(bf16[88,1536]{1,0:T(8,128)(2,1)S(1)} %collective-permute-done.9.refs_1_.refs_3_), channel_id=1, source_target_pairs={{0,32},{16,496},{32,64},{48,16},{64,96},{80,48},{96,128},{112,80},... | collective-permute-start | bytes 811016 | tf_op jit(solution)/shard_map/ppermute | solution.py:350
  38.8 1.9 %collective-permute-start.18 = (bf16[88,1536]{1,0:T(8,128)(2,1)S(1)}, bf16[88,1536]{1,0:T(8,128)(2,1)S(1)}, u32[]{:S(2)}, u32[]{:S(2)}) collective-permute-start(bf16[88,1536]{1,0:T(8,128)(2,1)S(1)} %collective-permute-done.17.refs_2_.refs_4_), channel_id=1, source_target_pairs={{0,32},{16,496},{32,64},{48,16},{64,96},{80,48},{96,128},{112,80},... | collective-permute-start | bytes 811016 | tf_op jit(solution)/shard_map/ppermute | solution.py:350
  40.7 2.7 %collective-permute-done.10.refs_1_.refs_3_.refs_4_ = bf16[88,1536]{1,0:T(8,128)(2,1)S(1)} collective-permute-done((bf16[88,1536]{1,0:T(8,128)(2,1)S(1)}, bf16[88,1536]{1,0:T(8,128)(2,1)S(1)}, u32[]{:S(2)}, u32[]{:S(2)}) %collective-permute-start.10) | collective-permute-done | bytes 270368 | tf_op jit(solution)/shard_map/ppermute | solution.py:350
  43.4 3.7 %collective-permute-start.11 = (bf16[88,1536]{1,0:T(8,128)(2,1)S(1)}, bf16[88,1536]{1,0:T(8,128)(2,1)S(1)}, u32[]{:S(2)}, u32[]{:S(2)}) collective-permute-start(bf16[88,1536]{1,0:T(8,128)(2,1)S(1)} %collective-permute-done.10.refs_1_.refs_3_.refs_4_), channel_id=1, source_target_pairs={{0,32},{16,496},{32,64},{48,16},{64,96},{80,48},{96,128},{112,80},... | collective-permute-start | bytes 811016 | tf_op jit(solution)/shard_map/ppermute | solution.py:350
  47.2 2.2 %collective-permute-start.4 = (bf16[96,1536]{1,0:T(8,128)(2,1)S(1)}, bf16[96,1536]{1,0:T(8,128)(2,1)S(1)}, u32[]{:S(2)}, u32[]{:S(2)}) collective-permute-start(bf16[96,1536]{1,0:T(8,128)(2,1)S(1)} %collective-permute-done.3.refs_0_.refs_6_), channel_id=1, source_target_pairs={{0,32},{16,496},{32,64},{48,16},{64,96},{80,48},{96,128},{112,80},... | collective-permute-start | bytes 884744 | tf_op jit(solution)/shard_map/ppermute | solution.py:350
  49.4 2.9 %collective-permute-start.19 = (bf16[88,1536]{1,0:T(8,128)(2,1)S(1)}, bf16[88,1536]{1,0:T(8,128)(2,1)S(1)}, u32[]{:S(2)}, u32[]{:S(2)}) collective-permute-start(bf16[88,1536]{1,0:T(8,128)(2,1)S(1)} %collective-permute-done.18.refs_2_.refs_4_.refs_5_), channel_id=1, source_target_pairs={{0,32},{16,496},{32,64},{48,16},{64,96},{80,48},{96,128},{112,80},... | collective-permute-start | bytes 811016 | tf_op jit(solution)/shard_map/ppermute | solution.py:350
  52.3 3.2 %collective-permute-start.12 = (bf16[88,1536]{1,0:T(8,128)(2,1)S(1)}, bf16[88,1536]{1,0:T(8,128)(2,1)S(1)}, u32[]{:S(2)}, u32[]{:S(2)}) collective-permute-start(bf16[88,1536]{1,0:T(8,128)(2,1)S(1)} %collective-permute-done.11.refs_1_.refs_3_.refs_7_), channel_id=1, source_target_pairs={{0,32},{16,496},{32,64},{48,16},{64,96},{80,48},{96,128},{112,80},... | collective-permute-start | bytes 811016 | tf_op jit(solution)/shard_map/ppermute | solution.py:350
  55.6 3.1 %collective-permute-start.5 = (bf16[96,1536]{1,0:T(8,128)(2,1)S(1)}, bf16[96,1536]{1,0:T(8,128)(2,1)S(1)}, u32[]{:S(2)}, u32[]{:S(2)}) collective-permute-start(bf16[96,1536]{1,0:T(8,128)(2,1)S(1)} %collective-permute-done.4.refs_0_.refs_9_), channel_id=1, source_target_pairs={{0,32},{16,496},{32,64},{48,16},{64,96},{80,48},{96,128},{112,80},... | collective-permute-start | bytes 884744 | tf_op jit(solution)/shard_map/ppermute | solution.py:350
  58.8 2.9 %collective-permute-start.20 = (bf16[88,1536]{1,0:T(8,128)(2,1)S(1)}, bf16[88,1536]{1,0:T(8,128)(2,1)S(1)}, u32[]{:S(2)}, u32[]{:S(2)}) collective-permute-start(bf16[88,1536]{1,0:T(8,128)(2,1)S(1)} %collective-permute-done.19.refs_2_.refs_4_.refs_8_), channel_id=1, source_target_pairs={{0,32},{16,496},{32,64},{48,16},{64,96},{80,48},{96,128},{112,80},... | collective-permute-start | bytes 811016 | tf_op jit(solution)/shard_map/ppermute | solution.py:350
  61.6 2.9 %collective-permute-start.13 = (bf16[88,1536]{1,0:T(8,128)(2,1)S(1)}, bf16[88,1536]{1,0:T(8,128)(2,1)S(1)}, u32[]{:S(2)}, u32[]{:S(2)}) collective-permute-start(bf16[88,1536]{1,0:T(8,128)(2,1)S(1)} %collective-permute-done.12.refs_1_.refs_3_.refs_10_), channel_id=1, source_target_pairs={{0,32},{16,496},{32,64},{48,16},{64,96},{80,48},{96,128},{112,80},... | collective-permute-start | bytes 811016 | tf_op jit(solution)/shard_map/ppermute | solution.py:350
  64.5 3.1 %collective-permute-start.6 = (bf16[96,1536]{1,0:T(8,128)(2,1)S(1)}, bf16[96,1536]{1,0:T(8,128)(2,1)S(1)}, u32[]{:S(2)}, u32[]{:S(2)}) collective-permute-start(bf16[96,1536]{1,0:T(8,128)(2,1)S(1)} %collective-permute-done.5.refs_0_.refs_12_), channel_id=1, source_target_pairs={{0,32},{16,496},{32,64},{48,16},{64,96},{80,48},{96,128},{112,80},... | collective-permute-start | bytes 884744 | tf_op jit(solution)/shard_map/ppermute | solution.py:350
  67.7 2.9 %collective-permute-start.21 = (bf16[88,1536]{1,0:T(8,128)(2,1)S(1)}, bf16[88,1536]{1,0:T(8,128)(2,1)S(1)}, u32[]{:S(2)}, u32[]{:S(2)}) collective-permute-start(bf16[88,1536]{1,0:T(8,128)(2,1)S(1)} %collective-permute-done.20.refs_2_.refs_4_.refs_11_), channel_id=1, source_target_pairs={{0,32},{16,496},{32,64},{48,16},{64,96},{80,48},{96,128},{112,80},... | collective-permute-start | bytes 811016 | tf_op jit(solution)/shard_map/ppermute | solution.py:350
  70.6 2.9 %collective-permute-start.14 = (bf16[88,1536]{1,0:T(8,128)(2,1)S(1)}, bf16[88,1536]{1,0:T(8,128)(2,1)S(1)}, u32[]{:S(2)}, u32[]{:S(2)}) collective-permute-start(bf16[88,1536]{1,0:T(8,128)(2,1)S(1)} %collective-permute-done.13.refs_1_.refs_3_.refs_13_), channel_id=1, source_target_pairs={{0,32},{16,496},{32,64},{48,16},{64,96},{80,48},{96,128},{112,80},... | collective-permute-start | bytes 811016 | tf_op jit(solution)/shard_map/ppermute | solution.py:350
  73.5 3.1 %collective-permute-start.7 = (bf16[96,1536]{1,0:T(8,128)(2,1)S(1)}, bf16[96,1536]{1,0:T(8,128)(2,1)S(1)}, u32[]{:S(2)}, u32[]{:S(2)}) collective-permute-start(bf16[96,1536]{1,0:T(8,128)(2,1)S(1)} %collective-permute-done.6.refs_0_.refs_15_), channel_id=1, source_target_pairs={{0,32},{16,496},{32,64},{48,16},{64,96},{80,48},{96,128},{112,80},... | collective-permute-start | bytes 884744 | tf_op jit(solution)/shard_map/ppermute | solution.py:350
  76.7 2.9 %collective-permute-start.22 = (bf16[88,1536]{1,0:T(8,128)(2,1)S(1)}, bf16[88,1536]{1,0:T(8,128)(2,1)S(1)}, u32[]{:S(2)}, u32[]{:S(2)}) collective-permute-start(bf16[88,1536]{1,0:T(8,128)(2,1)S(1)} %collective-permute-done.21.refs_2_.refs_4_.refs_14_), channel_id=1, source_target_pairs={{0,32},{16,496},{32,64},{48,16},{64,96},{80,48},{96,128},{112,80},... | collective-permute-start | bytes 811016 | tf_op jit(solution)/shard_map/ppermute | solution.py:350
  79.6 2.9 %collective-permute-start.15 = (bf16[88,1536]{1,0:T(8,128)(2,1)S(1)}, bf16[88,1536]{1,0:T(8,128)(2,1)S(1)}, u32[]{:S(2)}, u32[]{:S(2)}) collective-permute-start(bf16[88,1536]{1,0:T(8,128)(2,1)S(1)} %collective-permute-done.14.refs_1_.refs_3_.refs_16_), channel_id=1, source_target_pairs={{0,32},{16,496},{32,64},{48,16},{64,96},{80,48},{96,128},{112,80},... | collective-permute-start | bytes 811016 | tf_op jit(solution)/shard_map/ppermute | solution.py:350
  82.5 3.1 %collective-permute-start.8 = (bf16[96,1536]{1,0:T(8,128)(2,1)S(1)}, bf16[96,1536]{1,0:T(8,128)(2,1)S(1)}, u32[]{:S(2)}, u32[]{:S(2)}) collective-permute-start(bf16[96,1536]{1,0:T(8,128)(2,1)S(1)} %collective-permute-done.7.refs_0_.refs_18_), channel_id=1, source_target_pairs={{0,32},{16,496},{32,64},{48,16},{64,96},{80,48},{96,128},{112,80},... | collective-permute-start | bytes 884744 | tf_op jit(solution)/shard_map/ppermute | solution.py:350
  85.6 2.9 %collective-permute-start.23 = (bf16[88,1536]{1,0:T(8,128)(2,1)S(1)}, bf16[88,1536]{1,0:T(8,128)(2,1)S(1)}, u32[]{:S(2)}, u32[]{:S(2)}) collective-permute-start(bf16[88,1536]{1,0:T(8,128)(2,1)S(1)} %collective-permute-done.22.refs_2_.refs_4_.refs_17_), channel_id=1, source_target_pairs={{0,32},{16,496},{32,64},{48,16},{64,96},{80,48},{96,128},{112,80},... | collective-permute-start | bytes 811016 | tf_op jit(solution)/shard_map/ppermute | solution.py:350
  88.5 2.9 %collective-permute-start.16 = (bf16[40,1536]{1,0:T(8,128)(2,1)S(1)}, bf16[40,1536]{1,0:T(8,128)(2,1)S(1)}, u32[]{:S(2)}, u32[]{:S(2)}) collective-permute-start(bf16[40,1536]{1,0:T(8,128)(2,1)S(1)} %slice.4), channel_id=1, source_target_pairs={{0,32},{16,496},{32,64},{48,16},{64,96},{80,48},{96,128},{112,80},... | collective-permute-start | bytes 368648 | tf_op jit(solution)/shard_map/ppermute | solution.py:350
  91.4 0.3 own_tangents.1.own_ref
  91.8 0.5 tangents.7
  92.3 0.5 tangents.8
  92.7 0.5 tangents.9
  93.2 0.5 tangents.10
  93.7 0.5 tangents.11
  94.2 0.5 tangents.12
  94.7 0.5 tangents.13
  95.2 0.4 last_tangents.1
  95.6 16.7 %all_to_all.10.in_ref = bf16[16,24,8,128]{3,2,1,0:T(8,128)(2,1)S(1)} all-to-all(bf16[16,24,8,128]{3,2,1,0:T(8,128)(2,1)S(1)} %last_tangents.1), channel_id=1, replica_groups=mesh['dp'=32,'expert'=16] {'expert'}, dimensions={0} | all-to-all | bytes 1572864 | tf_op jit(solution)/shard_map/all_to_all | solution.py:382
  112.4 0.5 combine.1
  112.8 13.3 %all_to_all.11.in_ref = bf16[16,24,8,128]{3,2,1,0:T(8,128)(2,1)S(1)} all-to-all(bf16[16,24,8,128]{3,2,1,0:T(8,128)(2,1)S(1)} %combine.1), channel_id=1, replica_groups=mesh['dp'=32,'expert'=16] {'expert'}, dimensions={0} | all-to-all | bytes 1572864 | tf_op jit(solution)/shard_map/all_to_all | solution.py:384
  126.2 3.9 %gradients.1 = (f32[1080,128]{1,0:T(8,128)S(1)}, f32[1080,128]{1,0:T(8,128)S(1)}) custom-call(bf16[16,24,8,128]{3,2,1,0:T(8,128)(2,1)S(1)} %all_to_all.11.in_ref, bf16[96,1536]{1,0:T(8,128)(2,1)S(1)} %collective-permute-done.1.refs_0_, bf16[88,1536]{1,0:T(8,128)(2,1)S(1)} %collective-permute-done.9.refs_1_.refs_3_, ...), custom_call_target="tpu_custom_call" | custom-call | flops 1207959552 | bytes 6291456 | tf_op jit(solution)/shard_map/gradients/pallas_call | solution.py:324
  130.1 12.8 %collective-permute-start.24 = (f32[1080,128]{1,0:T(8,128)S(1)}, f32[1080,128]{1,0:T(8,128)S(1)}, u32[]{:S(2)}, u32[]{:S(2)}) collective-permute-start(f32[1080,128]{1,0:T(8,128)S(1)} %get-tuple-element.46), channel_id=1, source_target_pairs={{0,16},{16,0},{32,48},{48,32},{64,80},{80,64},{96,112},{112,96},{1... | collective-permute-start | bytes 1658888 | tf_op jit(solution)/shard_map/ppermute | solution.py:353
  142.9 1.6 %collective-permute-done.24 = f32[1080,128]{1,0:T(8,128)S(1)} collective-permute-done((f32[1080,128]{1,0:T(8,128)S(1)}, f32[1080,128]{1,0:T(8,128)S(1)}, u32[]{:S(2)}, u32[]{:S(2)}) %collective-permute-start.24) | collective-permute-done | bytes 552992 | tf_op jit(solution)/shard_map/ppermute | solution.py:353
  144.4 0.9 add.3
  (23 shorter events, 0.1 us)
Async XLA Ops:
  2.2 23.4 %collective-permute-start = (bf16[232,1536]{1,0:T(8,128)(2,1)}, bf16[232,1536]{1,0:T(8,128)(2,1)S(1)}, u32[]{:S(2)}, u32[]{:S(2)}) collective-permute-start(bf16[232,1536]{1,0:T(8,128)(2,1)} %get-tuple-element.26.sent_ref), channel_id=1, source_target_pairs={{0,16},{16,0},{32,48},{48,32},{64,80},{80,64},{96,112},{112,96},{1... | collective-permute-start | bytes 2138120 | tf_op jit(solution)/shard_map/ppermute | solution.py:353
  11.0 9.7 %collective-permute-start.1 = (bf16[96,1536]{1,0:T(8,128)(2,1)}, bf16[96,1536]{1,0:T(8,128)(2,1)S(1)}, u32[]{:S(2)}, u32[]{:S(2)}) collective-permute-start(bf16[96,1536]{1,0:T(8,128)(2,1)} %get-tuple-element.28), channel_id=1, source_target_pairs={{0,32},{16,496},{32,64},{48,16},{64,96},{80,48},{96,128},{112,80},... | collective-permute-start | bytes 884744 | tf_op jit(solution)/shard_map/ppermute | solution.py:350
  20.7 10.6 %collective-permute-start.2 = (bf16[96,1536]{1,0:T(8,128)(2,1)S(1)}, bf16[96,1536]{1,0:T(8,128)(2,1)S(1)}, u32[]{:S(2)}, u32[]{:S(2)}) collective-permute-start(bf16[96,1536]{1,0:T(8,128)(2,1)S(1)} %collective-permute-done.1.refs_0_), channel_id=1, source_target_pairs={{0,32},{16,496},{32,64},{48,16},{64,96},{80,48},{96,128},{112,80},... | collective-permute-start | bytes 884744 | tf_op jit(solution)/shard_map/ppermute | solution.py:350
  25.6 1.1 copy-start.1
  26.8 64.7 %copy-start = (bf16[128,1536]{1,0:T(8,128)(2,1)S(1)}, bf16[128,1536]{1,0:T(8,128)(2,1)}, u32[]{:S(2)}) copy-start(bf16[128,1536]{1,0:T(8,128)(2,1)} %refs_21_.1) | copy-start | bytes 1179652
  26.8 7.6 %collective-permute-start.9 = (bf16[88,1536]{1,0:T(8,128)(2,1)S(1)}, bf16[88,1536]{1,0:T(8,128)(2,1)S(1)}, u32[]{:S(2)}, u32[]{:S(2)}) collective-permute-start(bf16[88,1536]{1,0:T(8,128)(2,1)S(1)} %get-tuple-element.29.refs_0_), channel_id=1, source_target_pairs={{0,32},{16,496},{32,64},{48,16},{64,96},{80,48},{96,128},{112,80},... | collective-permute-start | bytes 811016 | tf_op jit(solution)/shard_map/ppermute | solution.py:350
  28.9 9.9 %collective-permute-start.17 = (bf16[88,1536]{1,0:T(8,128)(2,1)S(1)}, bf16[88,1536]{1,0:T(8,128)(2,1)S(1)}, u32[]{:S(2)}, u32[]{:S(2)}) collective-permute-start(bf16[88,1536]{1,0:T(8,128)(2,1)S(1)} %get-tuple-element.30), channel_id=1, source_target_pairs={{0,32},{16,496},{32,64},{48,16},{64,96},{80,48},{96,128},{112,80},... | collective-permute-start | bytes 811016 | tf_op jit(solution)/shard_map/ppermute | solution.py:350
  31.4 15.8 %collective-permute-start.3 = (bf16[96,1536]{1,0:T(8,128)(2,1)S(1)}, bf16[96,1536]{1,0:T(8,128)(2,1)S(1)}, u32[]{:S(2)}, u32[]{:S(2)}) collective-permute-start(bf16[96,1536]{1,0:T(8,128)(2,1)S(1)} %collective-permute-done.2.refs_0_.refs_3_), channel_id=1, source_target_pairs={{0,32},{16,496},{32,64},{48,16},{64,96},{80,48},{96,128},{112,80},... | collective-permute-start | bytes 884744 | tf_op jit(solution)/shard_map/ppermute | solution.py:350
  34.5 9.0 %collective-permute-start.10 = (bf16[88,1536]{1,0:T(8,128)(2,1)S(1)}, bf16[88,1536]{1,0:T(8,128)(2,1)S(1)}, u32[]{:S(2)}, u32[]{:S(2)}) collective-permute-start(bf16[88,1536]{1,0:T(8,128)(2,1)S(1)} %collective-permute-done.9.refs_1_.refs_3_), channel_id=1, source_target_pairs={{0,32},{16,496},{32,64},{48,16},{64,96},{80,48},{96,128},{112,80},... | collective-permute-start | bytes 811016 | tf_op jit(solution)/shard_map/ppermute | solution.py:350
  38.8 10.6 %collective-permute-start.18 = (bf16[88,1536]{1,0:T(8,128)(2,1)S(1)}, bf16[88,1536]{1,0:T(8,128)(2,1)S(1)}, u32[]{:S(2)}, u32[]{:S(2)}) collective-permute-start(bf16[88,1536]{1,0:T(8,128)(2,1)S(1)} %collective-permute-done.17.refs_2_.refs_4_), channel_id=1, source_target_pairs={{0,32},{16,496},{32,64},{48,16},{64,96},{80,48},{96,128},{112,80},... | collective-permute-start | bytes 811016 | tf_op jit(solution)/shard_map/ppermute | solution.py:350
  43.4 8.9 %collective-permute-start.11 = (bf16[88,1536]{1,0:T(8,128)(2,1)S(1)}, bf16[88,1536]{1,0:T(8,128)(2,1)S(1)}, u32[]{:S(2)}, u32[]{:S(2)}) collective-permute-start(bf16[88,1536]{1,0:T(8,128)(2,1)S(1)} %collective-permute-done.10.refs_1_.refs_3_.refs_4_), channel_id=1, source_target_pairs={{0,32},{16,496},{32,64},{48,16},{64,96},{80,48},{96,128},{112,80},... | collective-permute-start | bytes 811016 | tf_op jit(solution)/shard_map/ppermute | solution.py:350
  47.2 8.4 %collective-permute-start.4 = (bf16[96,1536]{1,0:T(8,128)(2,1)S(1)}, bf16[96,1536]{1,0:T(8,128)(2,1)S(1)}, u32[]{:S(2)}, u32[]{:S(2)}) collective-permute-start(bf16[96,1536]{1,0:T(8,128)(2,1)S(1)} %collective-permute-done.3.refs_0_.refs_6_), channel_id=1, source_target_pairs={{0,32},{16,496},{32,64},{48,16},{64,96},{80,48},{96,128},{112,80},... | collective-permute-start | bytes 884744 | tf_op jit(solution)/shard_map/ppermute | solution.py:350
  49.4 9.3 %collective-permute-start.19 = (bf16[88,1536]{1,0:T(8,128)(2,1)S(1)}, bf16[88,1536]{1,0:T(8,128)(2,1)S(1)}, u32[]{:S(2)}, u32[]{:S(2)}) collective-permute-start(bf16[88,1536]{1,0:T(8,128)(2,1)S(1)} %collective-permute-done.18.refs_2_.refs_4_.refs_5_), channel_id=1, source_target_pairs={{0,32},{16,496},{32,64},{48,16},{64,96},{80,48},{96,128},{112,80},... | collective-permute-start | bytes 811016 | tf_op jit(solution)/shard_map/ppermute | solution.py:350
  52.3 9.3 %collective-permute-start.12 = (bf16[88,1536]{1,0:T(8,128)(2,1)S(1)}, bf16[88,1536]{1,0:T(8,128)(2,1)S(1)}, u32[]{:S(2)}, u32[]{:S(2)}) collective-permute-start(bf16[88,1536]{1,0:T(8,128)(2,1)S(1)} %collective-permute-done.11.refs_1_.refs_3_.refs_7_), channel_id=1, source_target_pairs={{0,32},{16,496},{32,64},{48,16},{64,96},{80,48},{96,128},{112,80},... | collective-permute-start | bytes 811016 | tf_op jit(solution)/shard_map/ppermute | solution.py:350
  55.6 8.9 %collective-permute-start.5 = (bf16[96,1536]{1,0:T(8,128)(2,1)S(1)}, bf16[96,1536]{1,0:T(8,128)(2,1)S(1)}, u32[]{:S(2)}, u32[]{:S(2)}) collective-permute-start(bf16[96,1536]{1,0:T(8,128)(2,1)S(1)} %collective-permute-done.4.refs_0_.refs_9_), channel_id=1, source_target_pairs={{0,32},{16,496},{32,64},{48,16},{64,96},{80,48},{96,128},{112,80},... | collective-permute-start | bytes 884744 | tf_op jit(solution)/shard_map/ppermute | solution.py:350
  58.8 8.9 %collective-permute-start.20 = (bf16[88,1536]{1,0:T(8,128)(2,1)S(1)}, bf16[88,1536]{1,0:T(8,128)(2,1)S(1)}, u32[]{:S(2)}, u32[]{:S(2)}) collective-permute-start(bf16[88,1536]{1,0:T(8,128)(2,1)S(1)} %collective-permute-done.19.refs_2_.refs_4_.refs_8_), channel_id=1, source_target_pairs={{0,32},{16,496},{32,64},{48,16},{64,96},{80,48},{96,128},{112,80},... | collective-permute-start | bytes 811016 | tf_op jit(solution)/shard_map/ppermute | solution.py:350
  61.6 8.9 %collective-permute-start.13 = (bf16[88,1536]{1,0:T(8,128)(2,1)S(1)}, bf16[88,1536]{1,0:T(8,128)(2,1)S(1)}, u32[]{:S(2)}, u32[]{:S(2)}) collective-permute-start(bf16[88,1536]{1,0:T(8,128)(2,1)S(1)} %collective-permute-done.12.refs_1_.refs_3_.refs_10_), channel_id=1, source_target_pairs={{0,32},{16,496},{32,64},{48,16},{64,96},{80,48},{96,128},{112,80},... | collective-permute-start | bytes 811016 | tf_op jit(solution)/shard_map/ppermute | solution.py:350
  64.5 8.9 %collective-permute-start.6 = (bf16[96,1536]{1,0:T(8,128)(2,1)S(1)}, bf16[96,1536]{1,0:T(8,128)(2,1)S(1)}, u32[]{:S(2)}, u32[]{:S(2)}) collective-permute-start(bf16[96,1536]{1,0:T(8,128)(2,1)S(1)} %collective-permute-done.5.refs_0_.refs_12_), channel_id=1, source_target_pairs={{0,32},{16,496},{32,64},{48,16},{64,96},{80,48},{96,128},{112,80},... | collective-permute-start | bytes 884744 | tf_op jit(solution)/shard_map/ppermute | solution.py:350
  67.7 8.9 %collective-permute-start.21 = (bf16[88,1536]{1,0:T(8,128)(2,1)S(1)}, bf16[88,1536]{1,0:T(8,128)(2,1)S(1)}, u32[]{:S(2)}, u32[]{:S(2)}) collective-permute-start(bf16[88,1536]{1,0:T(8,128)(2,1)S(1)} %collective-permute-done.20.refs_2_.refs_4_.refs_11_), channel_id=1, source_target_pairs={{0,32},{16,496},{32,64},{48,16},{64,96},{80,48},{96,128},{112,80},... | collective-permute-start | bytes 811016 | tf_op jit(solution)/shard_map/ppermute | solution.py:350
  70.6 8.9 %collective-permute-start.14 = (bf16[88,1536]{1,0:T(8,128)(2,1)S(1)}, bf16[88,1536]{1,0:T(8,128)(2,1)S(1)}, u32[]{:S(2)}, u32[]{:S(2)}) collective-permute-start(bf16[88,1536]{1,0:T(8,128)(2,1)S(1)} %collective-permute-done.13.refs_1_.refs_3_.refs_13_), channel_id=1, source_target_pairs={{0,32},{16,496},{32,64},{48,16},{64,96},{80,48},{96,128},{112,80},... | collective-permute-start | bytes 811016 | tf_op jit(solution)/shard_map/ppermute | solution.py:350
  73.5 8.9 %collective-permute-start.7 = (bf16[96,1536]{1,0:T(8,128)(2,1)S(1)}, bf16[96,1536]{1,0:T(8,128)(2,1)S(1)}, u32[]{:S(2)}, u32[]{:S(2)}) collective-permute-start(bf16[96,1536]{1,0:T(8,128)(2,1)S(1)} %collective-permute-done.6.refs_0_.refs_15_), channel_id=1, source_target_pairs={{0,32},{16,496},{32,64},{48,16},{64,96},{80,48},{96,128},{112,80},... | collective-permute-start | bytes 884744 | tf_op jit(solution)/shard_map/ppermute | solution.py:350
  76.7 8.9 %collective-permute-start.22 = (bf16[88,1536]{1,0:T(8,128)(2,1)S(1)}, bf16[88,1536]{1,0:T(8,128)(2,1)S(1)}, u32[]{:S(2)}, u32[]{:S(2)}) collective-permute-start(bf16[88,1536]{1,0:T(8,128)(2,1)S(1)} %collective-permute-done.21.refs_2_.refs_4_.refs_14_), channel_id=1, source_target_pairs={{0,32},{16,496},{32,64},{48,16},{64,96},{80,48},{96,128},{112,80},... | collective-permute-start | bytes 811016 | tf_op jit(solution)/shard_map/ppermute | solution.py:350
  79.6 8.9 %collective-permute-start.15 = (bf16[88,1536]{1,0:T(8,128)(2,1)S(1)}, bf16[88,1536]{1,0:T(8,128)(2,1)S(1)}, u32[]{:S(2)}, u32[]{:S(2)}) collective-permute-start(bf16[88,1536]{1,0:T(8,128)(2,1)S(1)} %collective-permute-done.14.refs_1_.refs_3_.refs_16_), channel_id=1, source_target_pairs={{0,32},{16,496},{32,64},{48,16},{64,96},{80,48},{96,128},{112,80},... | collective-permute-start | bytes 811016 | tf_op jit(solution)/shard_map/ppermute | solution.py:350
  82.5 12.7 %collective-permute-start.8 = (bf16[96,1536]{1,0:T(8,128)(2,1)S(1)}, bf16[96,1536]{1,0:T(8,128)(2,1)S(1)}, u32[]{:S(2)}, u32[]{:S(2)}) collective-permute-start(bf16[96,1536]{1,0:T(8,128)(2,1)S(1)} %collective-permute-done.7.refs_0_.refs_18_), channel_id=1, source_target_pairs={{0,32},{16,496},{32,64},{48,16},{64,96},{80,48},{96,128},{112,80},... | collective-permute-start | bytes 884744 | tf_op jit(solution)/shard_map/ppermute | solution.py:350
  85.6 9.1 %collective-permute-start.23 = (bf16[88,1536]{1,0:T(8,128)(2,1)S(1)}, bf16[88,1536]{1,0:T(8,128)(2,1)S(1)}, u32[]{:S(2)}, u32[]{:S(2)}) collective-permute-start(bf16[88,1536]{1,0:T(8,128)(2,1)S(1)} %collective-permute-done.22.refs_2_.refs_4_.refs_17_), channel_id=1, source_target_pairs={{0,32},{16,496},{32,64},{48,16},{64,96},{80,48},{96,128},{112,80},... | collective-permute-start | bytes 811016 | tf_op jit(solution)/shard_map/ppermute | solution.py:350
  88.5 6.7 %collective-permute-start.16 = (bf16[40,1536]{1,0:T(8,128)(2,1)S(1)}, bf16[40,1536]{1,0:T(8,128)(2,1)S(1)}, u32[]{:S(2)}, u32[]{:S(2)}) collective-permute-start(bf16[40,1536]{1,0:T(8,128)(2,1)S(1)} %slice.4), channel_id=1, source_target_pairs={{0,32},{16,496},{32,64},{48,16},{64,96},{80,48},{96,128},{112,80},... | collective-permute-start | bytes 368648 | tf_op jit(solution)/shard_map/ppermute | solution.py:350
  130.1 14.3 %collective-permute-start.24 = (f32[1080,128]{1,0:T(8,128)S(1)}, f32[1080,128]{1,0:T(8,128)S(1)}, u32[]{:S(2)}, u32[]{:S(2)}) collective-permute-start(f32[1080,128]{1,0:T(8,128)S(1)} %get-tuple-element.46), channel_id=1, source_target_pairs={{0,16},{16,0},{32,48},{48,32},{64,80},{80,64},{96,112},{112,96},{1... | collective-permute-start | bytes 1658888 | tf_op jit(solution)/shard_map/ppermute | solution.py:353

commit v3 on v2

--- a/solution.py
+++ b/solution.py
@@ -108,14 +108,14 @@
 def split(sent, other, span, cut, join):
     width = sent.shape[1]
     left = span - cut
-    sizes = (join + left + TAB, span - join + TAB, 2 * FEATS)
+    sizes = (join + left + TAB, span - join, 2 * FEATS)
 
     def kernel(sent_ref, other_ref, first_ref, second_ref, dir_ref):
         first_ref[:join] = other_ref[:join]
         first_ref[join : join + left] = sent_ref[cut:span]
         first_ref[join + left :] = sent_ref[span + FEATS :]
-        second_ref[: span - join] = other_ref[join:span]
-        second_ref[span - join :] = other_ref[span + FEATS :]
+        first_ref[join + left :, LANES : 2 * LANES] = other_ref[span + FEATS :, :LANES]
+        second_ref[...] = other_ref[join:span]
         dir_ref[:FEATS] = sent_ref[span : span + FEATS]
         dir_ref[FEATS:] = other_ref[span : span + FEATS]
 
@@ -130,8 +130,8 @@
     )(sent, other)
 
 
-def table_of(rows):
-    return pl.BlockSpec((TAB, LANES), lambda i: (rows.shape[0] // TAB - 1, 0))
+def table_of(rows, count=1):
+    return pl.BlockSpec((TAB, count * LANES), lambda i: (rows.shape[0] // TAB - 1, 0))
 
 
 def mix_of(table, scale):
@@ -167,15 +167,15 @@
 def tangents(pair, pieces, parts, dirs, kept, shape, mix_shape, scale):
     sources, _, capacity, _ = shape
     span = sources * capacity
-    args = list(pieces) + list(pieces[1:]) + [dirs] + list(kept)
+    args = list(pieces) + [pieces[1], dirs] + list(kept)
 
     def kernel(*refs):
-        dir_ref, out_ref, mix_ref = refs[5], refs[-2], refs[-1]
+        table_ref, dir_ref, out_ref, mix_ref = refs[3], refs[4], refs[-2], refs[-1]
         rows = jnp.concatenate([refs[i][a:b, :] for i, a, b in parts], axis=0)
         value = project(rows, dir_ref[...])
         pack(out_ref, [value[:span], value[span:]])
         for i in range(2):
-            mix_ref[i] = mix_of(refs[3 + i][...], scale)
+            mix_ref[i] = mix_of(table_ref[:, i * LANES : (i + 1) * LANES], scale)
 
     return pl.pallas_call(
         kernel,
@@ -185,14 +185,13 @@
             jax.ShapeDtypeStruct(mix_shape, jnp.bfloat16),
         ],
         in_specs=[full(x) for x in pieces]
-        + [table_of(x) for x in pieces[1:]]
-        + [full(dirs)]
+        + [table_of(pieces[1], 2), full(dirs)]
         + [pl.BlockSpec(memory_space=pl.ANY)] * len(kept),
         out_specs=[
             pl.BlockSpec((sources, 3, capacity, LANES), lambda i: (0, pair, 0, 0)),
             pl.BlockSpec((2,) + mix_shape[1:], lambda i: (pair, 0, 0)),
         ],
-        input_output_aliases={6 + i: i for i in range(len(kept))},
+        input_output_aliases={5 + i: i for i in range(len(kept))},
         compiler_params=params(),
         cost_estimate=cost(4 * span * dirs.size, 2 * 2 * span * dirs.shape[1] + 2 * dirs.size),
         name="tangents",
@@ -290,44 +289,40 @@
 
     def kernel(in_ref, *refs):
         own_ref, other_ref, lhs_ref = refs[-3:]
-        column = pl.program_id(0)
-
-        @pl.when(column == 0)
-        def _():
-            def turned(slab):
-                rows = in_ref[:, slab].astype(jnp.float32).reshape(span, LANES)
-                return rows.astype(jnp.bfloat16).T
-
+
+        def turned(slab):
+            rows = in_ref[:, slab].astype(jnp.float32).reshape(span, LANES)
+            return rows.astype(jnp.bfloat16).T
+
+        for pair in range(pairs):
+            lhs_ref[pair, :LANES, :span] = turned(3 * pair)
+            lhs_ref[pair, :LANES, span:] = turned(3 * pair + 1)
+            tail = turned(3 * pair + 2)
+            lhs_ref[pair, LANES:, :span] = tail[: LANES // 2]
+            lhs_ref[pair, LANES:, span:] = tail[LANES // 2 :]
+        for column in range(width // step):
+            lanes = slice(column * step, (column + 1) * step)
+            total = None
+            at = 0
             for pair in range(pairs):
-                lhs_ref[pair, :LANES, :span] = turned(3 * pair)
-                lhs_ref[pair, :LANES, span:] = turned(3 * pair + 1)
-                tail = turned(3 * pair + 2)
-                lhs_ref[pair, LANES:, :span] = tail[: LANES // 2]
-                lhs_ref[pair, LANES:, span:] = tail[LANES // 2 :]
-
-        total = None
-        at = 0
-        for pair in range(pairs):
-            rows = [refs[at + i][a:b, :] for i, a, b in parts[pair]]
-            at += len(groups[pair])
-            term = jnp.dot(
-                lhs_ref[pair], jnp.concatenate(rows, axis=0), preferred_element_type=jnp.float32
-            )
-            total = term if total is None else total + term
-        for i in range(2):
-            lanes = slice(i * LANES, (i + 1) * LANES)
-            rows = pl.ds(2 * column + i, feats, stride=tiles)
-            own_ref[rows, :] = total[:feats, lanes]
-            other_ref[rows, :] = total[FEATS : FEATS + feats, lanes]
+                rows = [refs[at + i][a:b, lanes] for i, a, b in parts[pair]]
+                at += len(groups[pair])
+                term = jnp.dot(
+                    lhs_ref[pair], jnp.concatenate(rows, axis=0), preferred_element_type=jnp.float32
+                )
+                total = term if total is None else total + term
+            for i in range(2):
+                half = total[:, i * LANES : (i + 1) * LANES]
+                rows = pl.ds(2 * column + i, feats, stride=tiles)
+                own_ref[rows, :] = half[:feats]
+                other_ref[rows, :] = half[FEATS : FEATS + feats]
 
     shape = jax.ShapeDtypeStruct((feats * tiles, LANES), jnp.float32)
     return pl.pallas_call(
         kernel,
-        grid=(width // step,),
         out_shape=[shape, shape],
-        in_specs=[full(packed)]
-        + [pl.BlockSpec((x.shape[0], step), lambda i: (0, i)) for x in pieces],
-        out_specs=[pl.BlockSpec(shape.shape, lambda i: (0, 0))] * 2,
+        in_specs=[whole()] * (1 + len(pieces)),
+        out_specs=[whole()] * 2,
         scratch_shapes=[pltpu.VMEM((pairs, 2 * FEATS, 2 * span), jnp.bfloat16)],
         compiler_params=params(),
         cost_estimate=cost(4 * FEATS * 2 * span * pairs * width, 2 * 2 * span * pairs * width),

time: 146 us -> 148 us (1.014)
  waiting for transfers between devices: 8.44 us -> 11.3 us
  Pallas kernels: 10.8 us -> 8.33 us
  starting transfers between devices: 93.5 us -> 95 us
    ppermute x23, waiting for transfers between devices: 6.88 us -> 9.77 us  [shift(): return lax.ppermute(x, 'dp', ring)]
    pallas_call x1, Pallas kernels: 3.93 us -> 1.41 us  [gradients(): pl.pallas_call(kernel, out_shape=[shape, shape], in_specs=[whole()] * (1...]
  transfers between devices with their start and end apart: 25 -> 25, of which waited for: 4 -> 5; matrix products, arithmetic and copies ran while one was open for 0% -> 0% of each run, Pallas kernels for 3% -> 3%
where the time goes in v3:
time: 148 us; the launch traced here: 147 us
  starting transfers between devices  95 us (64%)
  blocking collectives  30 us (20%)
  waiting for transfers between devices  11.3 us (8%)
  Pallas kernels  8.33 us (6%)
    ppermute x23, starting transfers between devices, shift(): return lax.ppermute(x, 'dp', ring)  72.6 us
    ppermute x2, starting transfers between devices, swap(): return lax.ppermute(x, 'dp', partner)  22.4 us
    all_to_all x1, blocking collectives, body(): lax.all_to_all(packed, 'expert', split_axis=0, concat_axis=0, tiled=True)  16.7 us
    all_to_all x1, blocking collectives, body(): lax.all_to_all(adjoint, 'expert', split_axis=0, concat_axis=0, tiled=True)  13.3 us
    ppermute x23, waiting for transfers between devices, shift(): return lax.ppermute(x, 'dp', ring)  9.77 us
    pallas_call x7, Pallas kernels, tangents(): pl.pallas_call(kernel, grid=(1,), out_shape=[jax.ShapeDtypeStruct(shape,...  3.4 us
  transfers between devices with their start and end apart: 25, of which 5 were waited for; matrix products, arithmetic and copies ran while one was open for 0% of the time, Pallas kernels for 3%

profile of v3, /device:TPU:1, one launch (start us, length us, event | category | flops | bytes accessed | tf_op | source)
XLA Modules:
  0.0 147.1 jit_solution(816468277610921213)
XLA Ops:
  0.0 2.2 %message.1 = (bf16[232,1536]{1,0:T(8,128)(2,1)}, bf16[96,1536]{1,0:T(8,128)(2,1)}) custom-call(bf16[128,1536]{1,0:T(8,128)(2,1)} %refs_21_.1, s32[4,128]{1,0:T(4,128)} %bitcast.5, f32[4,128]{1,0:T(4,128)} %bitcast.6, bf16[90,1536]{1,0:T(8,128)(2,1)} %bitcast.4), custom_call_target="tpu_custom_call" | custom-call | flops 10000000 | bytes 1000000 | tf_op jit(solution)/shard_map/message/pallas_call | solution.py:93
  2.2 8.7 %collective-permute-start = (bf16[232,1536]{1,0:T(8,128)(2,1)}, bf16[232,1536]{1,0:T(8,128)(2,1)S(1)}, u32[]{:S(2)}, u32[]{:S(2)}) collective-permute-start(bf16[232,1536]{1,0:T(8,128)(2,1)} %get-tuple-element.26.sent_ref), channel_id=1, source_target_pairs={{0,16},{16,0},{32,48},{48,32},{64,80},{80,64},{96,112},{112,96},{1... | collective-permute-start | bytes 2138120 | tf_op jit(solution)/shard_map/ppermute | solution.py:348
  11.0 5.8 %collective-permute-start.1 = (bf16[96,1536]{1,0:T(8,128)(2,1)}, bf16[96,1536]{1,0:T(8,128)(2,1)S(1)}, u32[]{:S(2)}, u32[]{:S(2)}) collective-permute-start(bf16[96,1536]{1,0:T(8,128)(2,1)} %get-tuple-element.28), channel_id=1, source_target_pairs={{0,32},{16,496},{32,64},{48,16},{64,96},{80,48},{96,128},{112,80},... | collective-permute-start | bytes 884744 | tf_op jit(solution)/shard_map/ppermute | solution.py:345
  16.8 4.0 %collective-permute-done.1.refs_0_ = bf16[96,1536]{1,0:T(8,128)(2,1)S(1)} collective-permute-done((bf16[96,1536]{1,0:T(8,128)(2,1)}, bf16[96,1536]{1,0:T(8,128)(2,1)S(1)}, u32[]{:S(2)}, u32[]{:S(2)}) %collective-permute-start.1) | collective-permute-done | bytes 294944 | tf_op jit(solution)/shard_map/ppermute | solution.py:345
  20.7 4.9 %collective-permute-start.2 = (bf16[96,1536]{1,0:T(8,128)(2,1)S(1)}, bf16[96,1536]{1,0:T(8,128)(2,1)S(1)}, u32[]{:S(2)}, u32[]{:S(2)}) collective-permute-start(bf16[96,1536]{1,0:T(8,128)(2,1)S(1)} %collective-permute-done.1.refs_0_), channel_id=1, source_target_pairs={{0,32},{16,496},{32,64},{48,16},{64,96},{80,48},{96,128},{112,80},... | collective-permute-start | bytes 884744 | tf_op jit(solution)/shard_map/ppermute | solution.py:345
  25.6 0.0 collective-permute-done.other_ref
  25.7 1.1 copy-done.1
  26.8 0.1 split.1
  26.8 2.1 %collective-permute-start.9 = (bf16[88,1536]{1,0:T(8,128)(2,1)S(1)}, bf16[88,1536]{1,0:T(8,128)(2,1)S(1)}, u32[]{:S(2)}, u32[]{:S(2)}) collective-permute-start(bf16[88,1536]{1,0:T(8,128)(2,1)S(1)} %get-tuple-element.29.refs_0_), channel_id=1, source_target_pairs={{0,32},{16,496},{32,64},{48,16},{64,96},{80,48},{96,128},{112,80},... | collective-permute-start | bytes 811016 | tf_op jit(solution)/shard_map/ppermute | solution.py:345
  28.9 0.4 collective-permute-done.2.refs_0_.refs_3_
  29.3 5.0 %collective-permute-start.3 = (bf16[96,1536]{1,0:T(8,128)(2,1)S(1)}, bf16[96,1536]{1,0:T(8,128)(2,1)S(1)}, u32[]{:S(2)}, u32[]{:S(2)}) collective-permute-start(bf16[96,1536]{1,0:T(8,128)(2,1)S(1)} %collective-permute-done.2.refs_0_.refs_3_), channel_id=1, source_target_pairs={{0,32},{16,496},{32,64},{48,16},{64,96},{80,48},{96,128},{112,80},... | collective-permute-start | bytes 884744 | tf_op jit(solution)/shard_map/ppermute | solution.py:345
  34.3 0.1 collective-permute-done.9.refs_1_.refs_3_
  34.4 2.9 %collective-permute-start.10 = (bf16[88,1536]{1,0:T(8,128)(2,1)S(1)}, bf16[88,1536]{1,0:T(8,128)(2,1)S(1)}, u32[]{:S(2)}, u32[]{:S(2)}) collective-permute-start(bf16[88,1536]{1,0:T(8,128)(2,1)S(1)} %collective-permute-done.9.refs_1_.refs_3_), channel_id=1, source_target_pairs={{0,32},{16,496},{32,64},{48,16},{64,96},{80,48},{96,128},{112,80},... | collective-permute-start | bytes 811016 | tf_op jit(solution)/shard_map/ppermute | solution.py:345
  37.3 1.9 %collective-permute-start.17 = (bf16[80,1536]{1,0:T(8,128)(2,1)S(1)}, bf16[80,1536]{1,0:T(8,128)(2,1)S(1)}, u32[]{:S(2)}, u32[]{:S(2)}) collective-permute-start(bf16[80,1536]{1,0:T(8,128)(2,1)S(1)} %get-tuple-element.30), channel_id=1, source_target_pairs={{0,32},{16,496},{32,64},{48,16},{64,96},{80,48},{96,128},{112,80},... | collective-permute-start | bytes 737288 | tf_op jit(solution)/shard_map/ppermute | solution.py:345
  39.2 5.3 %collective-permute-done.17.refs_2_ = bf16[80,1536]{1,0:T(8,128)(2,1)S(1)} collective-permute-done((bf16[80,1536]{1,0:T(8,128)(2,1)S(1)}, bf16[80,1536]{1,0:T(8,128)(2,1)S(1)}, u32[]{:S(2)}, u32[]{:S(2)}) %collective-permute-start.17) | collective-permute-done | bytes 245792 | tf_op jit(solution)/shard_map/ppermute | solution.py:345
  44.5 4.0 %collective-permute-start.18 = (bf16[80,1536]{1,0:T(8,128)(2,1)S(1)}, bf16[80,1536]{1,0:T(8,128)(2,1)S(1)}, u32[]{:S(2)}, u32[]{:S(2)}) collective-permute-start(bf16[80,1536]{1,0:T(8,128)(2,1)S(1)} %collective-permute-done.17.refs_2_), channel_id=1, source_target_pairs={{0,32},{16,496},{32,64},{48,16},{64,96},{80,48},{96,128},{112,80},... | collective-permute-start | bytes 737288 | tf_op jit(solution)/shard_map/ppermute | solution.py:345
  48.5 1.9 %collective-permute-start.11 = (bf16[88,1536]{1,0:T(8,128)(2,1)S(1)}, bf16[88,1536]{1,0:T(8,128)(2,1)S(1)}, u32[]{:S(2)}, u32[]{:S(2)}) collective-permute-start(bf16[88,1536]{1,0:T(8,128)(2,1)S(1)} %collective-permute-done.10.refs_1_.refs_3_.refs_4_), channel_id=1, source_target_pairs={{0,32},{16,496},{32,64},{48,16},{64,96},{80,48},{96,128},{112,80},... | collective-permute-start | bytes 811016 | tf_op jit(solution)/shard_map/ppermute | solution.py:345
  50.5 3.0 %collective-permute-start.4 = (bf16[96,1536]{1,0:T(8,128)(2,1)S(1)}, bf16[96,1536]{1,0:T(8,128)(2,1)S(1)}, u32[]{:S(2)}, u32[]{:S(2)}) collective-permute-start(bf16[96,1536]{1,0:T(8,128)(2,1)S(1)} %collective-permute-done.3.refs_0_.refs_6_), channel_id=1, source_target_pairs={{0,32},{16,496},{32,64},{48,16},{64,96},{80,48},{96,128},{112,80},... | collective-permute-start | bytes 884744 | tf_op jit(solution)/shard_map/ppermute | solution.py:345
  53.5 3.1 %collective-permute-start.19 = (bf16[80,1536]{1,0:T(8,128)(2,1)S(1)}, bf16[80,1536]{1,0:T(8,128)(2,1)S(1)}, u32[]{:S(2)}, u32[]{:S(2)}) collective-permute-start(bf16[80,1536]{1,0:T(8,128)(2,1)S(1)} %collective-permute-done.18.refs_2_.refs_5_), channel_id=1, source_target_pairs={{0,32},{16,496},{32,64},{48,16},{64,96},{80,48},{96,128},{112,80},... | collective-permute-start | bytes 737288 | tf_op jit(solution)/shard_map/ppermute | solution.py:345
  56.7 3.7 %collective-permute-start.12 = (bf16[88,1536]{1,0:T(8,128)(2,1)S(1)}, bf16[88,1536]{1,0:T(8,128)(2,1)S(1)}, u32[]{:S(2)}, u32[]{:S(2)}) collective-permute-start(bf16[88,1536]{1,0:T(8,128)(2,1)S(1)} %collective-permute-done.11.refs_1_.refs_3_.refs_7_), channel_id=1, source_target_pairs={{0,32},{16,496},{32,64},{48,16},{64,96},{80,48},{96,128},{112,80},... | collective-permute-start | bytes 811016 | tf_op jit(solution)/shard_map/ppermute | solution.py:345
  60.3 2.4 %collective-permute-start.5 = (bf16[96,1536]{1,0:T(8,128)(2,1)S(1)}, bf16[96,1536]{1,0:T(8,128)(2,1)S(1)}, u32[]{:S(2)}, u32[]{:S(2)}) collective-permute-start(bf16[96,1536]{1,0:T(8,128)(2,1)S(1)} %collective-permute-done.4.refs_0_.refs_9_), channel_id=1, source_target_pairs={{0,32},{16,496},{32,64},{48,16},{64,96},{80,48},{96,128},{112,80},... | collective-permute-start | bytes 884744 | tf_op jit(solution)/shard_map/ppermute | solution.py:345
  62.7 2.6 %collective-permute-start.20 = (bf16[80,1536]{1,0:T(8,128)(2,1)S(1)}, bf16[80,1536]{1,0:T(8,128)(2,1)S(1)}, u32[]{:S(2)}, u32[]{:S(2)}) collective-permute-start(bf16[80,1536]{1,0:T(8,128)(2,1)S(1)} %collective-permute-done.19.refs_2_.refs_8_), channel_id=1, source_target_pairs={{0,32},{16,496},{32,64},{48,16},{64,96},{80,48},{96,128},{112,80},... | collective-permute-start | bytes 737288 | tf_op jit(solution)/shard_map/ppermute | solution.py:345
  65.3 3.4 %collective-permute-start.13 = (bf16[88,1536]{1,0:T(8,128)(2,1)S(1)}, bf16[88,1536]{1,0:T(8,128)(2,1)S(1)}, u32[]{:S(2)}, u32[]{:S(2)}) collective-permute-start(bf16[88,1536]{1,0:T(8,128)(2,1)S(1)} %collective-permute-done.12.refs_1_.refs_3_.refs_10_), channel_id=1, source_target_pairs={{0,32},{16,496},{32,64},{48,16},{64,96},{80,48},{96,128},{112,80},... | collective-permute-start | bytes 811016 | tf_op jit(solution)/shard_map/ppermute | solution.py:345
  68.7 3.1 %collective-permute-start.6 = (bf16[96,1536]{1,0:T(8,128)(2,1)S(1)}, bf16[96,1536]{1,0:T(8,128)(2,1)S(1)}, u32[]{:S(2)}, u32[]{:S(2)}) collective-permute-start(bf16[96,1536]{1,0:T(8,128)(2,1)S(1)} %collective-permute-done.5.refs_0_.refs_12_), channel_id=1, source_target_pairs={{0,32},{16,496},{32,64},{48,16},{64,96},{80,48},{96,128},{112,80},... | collective-permute-start | bytes 884744 | tf_op jit(solution)/shard_map/ppermute | solution.py:345
  71.9 2.6 %collective-permute-start.21 = (bf16[80,1536]{1,0:T(8,128)(2,1)S(1)}, bf16[80,1536]{1,0:T(8,128)(2,1)S(1)}, u32[]{:S(2)}, u32[]{:S(2)}) collective-permute-start(bf16[80,1536]{1,0:T(8,128)(2,1)S(1)} %collective-permute-done.20.refs_2_.refs_11_), channel_id=1, source_target_pairs={{0,32},{16,496},{32,64},{48,16},{64,96},{80,48},{96,128},{112,80},... | collective-permute-start | bytes 737288 | tf_op jit(solution)/shard_map/ppermute | solution.py:345
  74.5 2.9 %collective-permute-start.14 = (bf16[88,1536]{1,0:T(8,128)(2,1)S(1)}, bf16[88,1536]{1,0:T(8,128)(2,1)S(1)}, u32[]{:S(2)}, u32[]{:S(2)}) collective-permute-start(bf16[88,1536]{1,0:T(8,128)(2,1)S(1)} %collective-permute-done.13.refs_1_.refs_3_.refs_13_), channel_id=1, source_target_pairs={{0,32},{16,496},{32,64},{48,16},{64,96},{80,48},{96,128},{112,80},... | collective-permute-start | bytes 811016 | tf_op jit(solution)/shard_map/ppermute | solution.py:345
  77.4 3.1 %collective-permute-start.7 = (bf16[96,1536]{1,0:T(8,128)(2,1)S(1)}, bf16[96,1536]{1,0:T(8,128)(2,1)S(1)}, u32[]{:S(2)}, u32[]{:S(2)}) collective-permute-start(bf16[96,1536]{1,0:T(8,128)(2,1)S(1)} %collective-permute-done.6.refs_0_.refs_15_), channel_id=1, source_target_pairs={{0,32},{16,496},{32,64},{48,16},{64,96},{80,48},{96,128},{112,80},... | collective-permute-start | bytes 884744 | tf_op jit(solution)/shard_map/ppermute | solution.py:345
  80.6 2.6 %collective-permute-start.22 = (bf16[80,1536]{1,0:T(8,128)(2,1)S(1)}, bf16[80,1536]{1,0:T(8,128)(2,1)S(1)}, u32[]{:S(2)}, u32[]{:S(2)}) collective-permute-start(bf16[80,1536]{1,0:T(8,128)(2,1)S(1)} %collective-permute-done.21.refs_2_.refs_14_), channel_id=1, source_target_pairs={{0,32},{16,496},{32,64},{48,16},{64,96},{80,48},{96,128},{112,80},... | collective-permute-start | bytes 737288 | tf_op jit(solution)/shard_map/ppermute | solution.py:345
  83.2 2.9 %collective-permute-start.15 = (bf16[88,1536]{1,0:T(8,128)(2,1)S(1)}, bf16[88,1536]{1,0:T(8,128)(2,1)S(1)}, u32[]{:S(2)}, u32[]{:S(2)}) collective-permute-start(bf16[88,1536]{1,0:T(8,128)(2,1)S(1)} %collective-permute-done.14.refs_1_.refs_3_.refs_16_), channel_id=1, source_target_pairs={{0,32},{16,496},{32,64},{48,16},{64,96},{80,48},{96,128},{112,80},... | collective-permute-start | bytes 811016 | tf_op jit(solution)/shard_map/ppermute | solution.py:345
  86.1 3.1 %collective-permute-start.8 = (bf16[96,1536]{1,0:T(8,128)(2,1)S(1)}, bf16[96,1536]{1,0:T(8,128)(2,1)S(1)}, u32[]{:S(2)}, u32[]{:S(2)}) collective-permute-start(bf16[96,1536]{1,0:T(8,128)(2,1)S(1)} %collective-permute-done.7.refs_0_.refs_18_), channel_id=1, source_target_pairs={{0,32},{16,496},{32,64},{48,16},{64,96},{80,48},{96,128},{112,80},... | collective-permute-start | bytes 884744 | tf_op jit(solution)/shard_map/ppermute | solution.py:345
  89.3 2.6 %collective-permute-start.23 = (bf16[80,1536]{1,0:T(8,128)(2,1)S(1)}, bf16[80,1536]{1,0:T(8,128)(2,1)S(1)}, u32[]{:S(2)}, u32[]{:S(2)}) collective-permute-start(bf16[80,1536]{1,0:T(8,128)(2,1)S(1)} %collective-permute-done.22.refs_2_.refs_17_), channel_id=1, source_target_pairs={{0,32},{16,496},{32,64},{48,16},{64,96},{80,48},{96,128},{112,80},... | collective-permute-start | bytes 737288 | tf_op jit(solution)/shard_map/ppermute | solution.py:345
  91.9 2.9 %collective-permute-start.16 = (bf16[40,1536]{1,0:T(8,128)(2,1)S(1)}, bf16[40,1536]{1,0:T(8,128)(2,1)S(1)}, u32[]{:S(2)}, u32[]{:S(2)}) collective-permute-start(bf16[40,1536]{1,0:T(8,128)(2,1)S(1)} %slice.4), channel_id=1, source_target_pairs={{0,32},{16,496},{32,64},{48,16},{64,96},{80,48},{96,128},{112,80},... | collective-permute-start | bytes 368648 | tf_op jit(solution)/shard_map/ppermute | solution.py:345
  94.8 0.3 own_tangents.1.own_ref
  95.2 0.5 tangents.7
  95.7 0.5 tangents.8
  96.1 0.5 tangents.9
  96.6 0.5 tangents.10
  97.1 0.5 tangents.11
  97.6 0.5 tangents.12
  98.1 0.5 tangents.13
  98.6 0.4 last_tangents.1
  99.0 16.7 %all_to_all.10.in_ref = bf16[16,24,8,128]{3,2,1,0:T(8,128)(2,1)S(1)} all-to-all(bf16[16,24,8,128]{3,2,1,0:T(8,128)(2,1)S(1)} %last_tangents.1), channel_id=1, replica_groups=mesh['dp'=32,'expert'=16] {'expert'}, dimensions={0} | all-to-all | bytes 1572864 | tf_op jit(solution)/shard_map/all_to_all | solution.py:377
  115.8 0.5 combine.1
  116.3 13.3 %all_to_all.11.in_ref = bf16[16,24,8,128]{3,2,1,0:T(8,128)(2,1)S(1)} all-to-all(bf16[16,24,8,128]{3,2,1,0:T(8,128)(2,1)S(1)} %combine.1), channel_id=1, replica_groups=mesh['dp'=32,'expert'=16] {'expert'}, dimensions={0} | all-to-all | bytes 1572864 | tf_op jit(solution)/shard_map/all_to_all | solution.py:379
  129.6 1.4 gradients.1
  131.0 13.7 %collective-permute-start.24 = (f32[1080,128]{1,0:T(8,128)S(1)}, f32[1080,128]{1,0:T(8,128)S(1)}, u32[]{:S(2)}, u32[]{:S(2)}) collective-permute-start(f32[1080,128]{1,0:T(8,128)S(1)} %get-tuple-element.46), channel_id=1, source_target_pairs={{0,16},{16,0},{32,48},{48,32},{64,80},{80,64},{96,112},{112,96},{1... | collective-permute-start | bytes 1658888 | tf_op jit(solution)/shard_map/ppermute | solution.py:348
  144.7 1.6 %collective-permute-done.24 = f32[1080,128]{1,0:T(8,128)S(1)} collective-permute-done((f32[1080,128]{1,0:T(8,128)S(1)}, f32[1080,128]{1,0:T(8,128)S(1)}, u32[]{:S(2)}, u32[]{:S(2)}) %collective-permute-start.24) | collective-permute-done | bytes 552992 | tf_op jit(solution)/shard_map/ppermute | solution.py:348
  146.3 0.9 add.3
  (23 shorter events, 0.1 us)
Async XLA Ops:
  2.2 23.4 %collective-permute-start = (bf16[232,1536]{1,0:T(8,128)(2,1)}, bf16[232,1536]{1,0:T(8,128)(2,1)S(1)}, u32[]{:S(2)}, u32[]{:S(2)}) collective-permute-start(bf16[232,1536]{1,0:T(8,128)(2,1)} %get-tuple-element.26.sent_ref), channel_id=1, source_target_pairs={{0,16},{16,0},{32,48},{48,32},{64,80},{80,64},{96,112},{112,96},{1... | collective-permute-start | bytes 2138120 | tf_op jit(solution)/shard_map/ppermute | solution.py:348
  11.0 9.7 %collective-permute-start.1 = (bf16[96,1536]{1,0:T(8,128)(2,1)}, bf16[96,1536]{1,0:T(8,128)(2,1)S(1)}, u32[]{:S(2)}, u32[]{:S(2)}) collective-permute-start(bf16[96,1536]{1,0:T(8,128)(2,1)} %get-tuple-element.28), channel_id=1, source_target_pairs={{0,32},{16,496},{32,64},{48,16},{64,96},{80,48},{96,128},{112,80},... | collective-permute-start | bytes 884744 | tf_op jit(solution)/shard_map/ppermute | solution.py:345
  20.7 8.6 %collective-permute-start.2 = (bf16[96,1536]{1,0:T(8,128)(2,1)S(1)}, bf16[96,1536]{1,0:T(8,128)(2,1)S(1)}, u32[]{:S(2)}, u32[]{:S(2)}) collective-permute-start(bf16[96,1536]{1,0:T(8,128)(2,1)S(1)} %collective-permute-done.1.refs_0_), channel_id=1, source_target_pairs={{0,32},{16,496},{32,64},{48,16},{64,96},{80,48},{96,128},{112,80},... | collective-permute-start | bytes 884744 | tf_op jit(solution)/shard_map/ppermute | solution.py:345
  25.6 1.1 copy-start.1
  26.8 68.1 %copy-start = (bf16[128,1536]{1,0:T(8,128)(2,1)S(1)}, bf16[128,1536]{1,0:T(8,128)(2,1)}, u32[]{:S(2)}) copy-start(bf16[128,1536]{1,0:T(8,128)(2,1)} %refs_21_.1) | copy-start | bytes 1179652
  26.8 7.5 %collective-permute-start.9 = (bf16[88,1536]{1,0:T(8,128)(2,1)S(1)}, bf16[88,1536]{1,0:T(8,128)(2,1)S(1)}, u32[]{:S(2)}, u32[]{:S(2)}) collective-permute-start(bf16[88,1536]{1,0:T(8,128)(2,1)S(1)} %get-tuple-element.29.refs_0_), channel_id=1, source_target_pairs={{0,32},{16,496},{32,64},{48,16},{64,96},{80,48},{96,128},{112,80},... | collective-permute-start | bytes 811016 | tf_op jit(solution)/shard_map/ppermute | solution.py:345
  29.3 21.2 %collective-permute-start.3 = (bf16[96,1536]{1,0:T(8,128)(2,1)S(1)}, bf16[96,1536]{1,0:T(8,128)(2,1)S(1)}, u32[]{:S(2)}, u32[]{:S(2)}) collective-permute-start(bf16[96,1536]{1,0:T(8,128)(2,1)S(1)} %collective-permute-done.2.refs_0_.refs_3_), channel_id=1, source_target_pairs={{0,32},{16,496},{32,64},{48,16},{64,96},{80,48},{96,128},{112,80},... | collective-permute-start | bytes 884744 | tf_op jit(solution)/shard_map/ppermute | solution.py:345
  34.4 14.1 %collective-permute-start.10 = (bf16[88,1536]{1,0:T(8,128)(2,1)S(1)}, bf16[88,1536]{1,0:T(8,128)(2,1)S(1)}, u32[]{:S(2)}, u32[]{:S(2)}) collective-permute-start(bf16[88,1536]{1,0:T(8,128)(2,1)S(1)} %collective-permute-done.9.refs_1_.refs_3_), channel_id=1, source_target_pairs={{0,32},{16,496},{32,64},{48,16},{64,96},{80,48},{96,128},{112,80},... | collective-permute-start | bytes 811016 | tf_op jit(solution)/shard_map/ppermute | solution.py:345
  37.3 7.2 %collective-permute-start.17 = (bf16[80,1536]{1,0:T(8,128)(2,1)S(1)}, bf16[80,1536]{1,0:T(8,128)(2,1)S(1)}, u32[]{:S(2)}, u32[]{:S(2)}) collective-permute-start(bf16[80,1536]{1,0:T(8,128)(2,1)S(1)} %get-tuple-element.30), channel_id=1, source_target_pairs={{0,32},{16,496},{32,64},{48,16},{64,96},{80,48},{96,128},{112,80},... | collective-permute-start | bytes 737288 | tf_op jit(solution)/shard_map/ppermute | solution.py:345
  44.5 9.0 %collective-permute-start.18 = (bf16[80,1536]{1,0:T(8,128)(2,1)S(1)}, bf16[80,1536]{1,0:T(8,128)(2,1)S(1)}, u32[]{:S(2)}, u32[]{:S(2)}) collective-permute-start(bf16[80,1536]{1,0:T(8,128)(2,1)S(1)} %collective-permute-done.17.refs_2_), channel_id=1, source_target_pairs={{0,32},{16,496},{32,64},{48,16},{64,96},{80,48},{96,128},{112,80},... | collective-permute-start | bytes 737288 | tf_op jit(solution)/shard_map/ppermute | solution.py:345
  48.5 8.1 %collective-permute-start.11 = (bf16[88,1536]{1,0:T(8,128)(2,1)S(1)}, bf16[88,1536]{1,0:T(8,128)(2,1)S(1)}, u32[]{:S(2)}, u32[]{:S(2)}) collective-permute-start(bf16[88,1536]{1,0:T(8,128)(2,1)S(1)} %collective-permute-done.10.refs_1_.refs_3_.refs_4_), channel_id=1, source_target_pairs={{0,32},{16,496},{32,64},{48,16},{64,96},{80,48},{96,128},{112,80},... | collective-permute-start | bytes 811016 | tf_op jit(solution)/shard_map/ppermute | solution.py:345
  50.5 9.9 %collective-permute-start.4 = (bf16[96,1536]{1,0:T(8,128)(2,1)S(1)}, bf16[96,1536]{1,0:T(8,128)(2,1)S(1)}, u32[]{:S(2)}, u32[]{:S(2)}) collective-permute-start(bf16[96,1536]{1,0:T(8,128)(2,1)S(1)} %collective-permute-done.3.refs_0_.refs_6_), channel_id=1, source_target_pairs={{0,32},{16,496},{32,64},{48,16},{64,96},{80,48},{96,128},{112,80},... | collective-permute-start | bytes 884744 | tf_op jit(solution)/shard_map/ppermute | solution.py:345
  53.5 9.2 %collective-permute-start.19 = (bf16[80,1536]{1,0:T(8,128)(2,1)S(1)}, bf16[80,1536]{1,0:T(8,128)(2,1)S(1)}, u32[]{:S(2)}, u32[]{:S(2)}) collective-permute-start(bf16[80,1536]{1,0:T(8,128)(2,1)S(1)} %collective-permute-done.18.refs_2_.refs_5_), channel_id=1, source_target_pairs={{0,32},{16,496},{32,64},{48,16},{64,96},{80,48},{96,128},{112,80},... | collective-permute-start | bytes 737288 | tf_op jit(solution)/shard_map/ppermute | solution.py:345
  56.7 8.7 %collective-permute-start.12 = (bf16[88,1536]{1,0:T(8,128)(2,1)S(1)}, bf16[88,1536]{1,0:T(8,128)(2,1)S(1)}, u32[]{:S(2)}, u32[]{:S(2)}) collective-permute-start(bf16[88,1536]{1,0:T(8,128)(2,1)S(1)} %collective-permute-done.11.refs_1_.refs_3_.refs_7_), channel_id=1, source_target_pairs={{0,32},{16,496},{32,64},{48,16},{64,96},{80,48},{96,128},{112,80},... | collective-permute-start | bytes 811016 | tf_op jit(solution)/shard_map/ppermute | solution.py:345
  60.3 8.4 %collective-permute-start.5 = (bf16[96,1536]{1,0:T(8,128)(2,1)S(1)}, bf16[96,1536]{1,0:T(8,128)(2,1)S(1)}, u32[]{:S(2)}, u32[]{:S(2)}) collective-permute-start(bf16[96,1536]{1,0:T(8,128)(2,1)S(1)} %collective-permute-done.4.refs_0_.refs_9_), channel_id=1, source_target_pairs={{0,32},{16,496},{32,64},{48,16},{64,96},{80,48},{96,128},{112,80},... | collective-permute-start | bytes 884744 | tf_op jit(solution)/shard_map/ppermute | solution.py:345
  62.7 9.2 %collective-permute-start.20 = (bf16[80,1536]{1,0:T(8,128)(2,1)S(1)}, bf16[80,1536]{1,0:T(8,128)(2,1)S(1)}, u32[]{:S(2)}, u32[]{:S(2)}) collective-permute-start(bf16[80,1536]{1,0:T(8,128)(2,1)S(1)} %collective-permute-done.19.refs_2_.refs_8_), channel_id=1, source_target_pairs={{0,32},{16,496},{32,64},{48,16},{64,96},{80,48},{96,128},{112,80},... | collective-permute-start | bytes 737288 | tf_op jit(solution)/shard_map/ppermute | solution.py:345
  65.3 9.2 %collective-permute-start.13 = (bf16[88,1536]{1,0:T(8,128)(2,1)S(1)}, bf16[88,1536]{1,0:T(8,128)(2,1)S(1)}, u32[]{:S(2)}, u32[]{:S(2)}) collective-permute-start(bf16[88,1536]{1,0:T(8,128)(2,1)S(1)} %collective-permute-done.12.refs_1_.refs_3_.refs_10_), channel_id=1, source_target_pairs={{0,32},{16,496},{32,64},{48,16},{64,96},{80,48},{96,128},{112,80},... | collective-permute-start | bytes 811016 | tf_op jit(solution)/shard_map/ppermute | solution.py:345
  68.7 8.7 %collective-permute-start.6 = (bf16[96,1536]{1,0:T(8,128)(2,1)S(1)}, bf16[96,1536]{1,0:T(8,128)(2,1)S(1)}, u32[]{:S(2)}, u32[]{:S(2)}) collective-permute-start(bf16[96,1536]{1,0:T(8,128)(2,1)S(1)} %collective-permute-done.5.refs_0_.refs_12_), channel_id=1, source_target_pairs={{0,32},{16,496},{32,64},{48,16},{64,96},{80,48},{96,128},{112,80},... | collective-permute-start | bytes 884744 | tf_op jit(solution)/shard_map/ppermute | solution.py:345
  71.9 8.7 %collective-permute-start.21 = (bf16[80,1536]{1,0:T(8,128)(2,1)S(1)}, bf16[80,1536]{1,0:T(8,128)(2,1)S(1)}, u32[]{:S(2)}, u32[]{:S(2)}) collective-permute-start(bf16[80,1536]{1,0:T(8,128)(2,1)S(1)} %collective-permute-done.20.refs_2_.refs_11_), channel_id=1, source_target_pairs={{0,32},{16,496},{32,64},{48,16},{64,96},{80,48},{96,128},{112,80},... | collective-permute-start | bytes 737288 | tf_op jit(solution)/shard_map/ppermute | solution.py:345
  74.5 8.7 %collective-permute-start.14 = (bf16[88,1536]{1,0:T(8,128)(2,1)S(1)}, bf16[88,1536]{1,0:T(8,128)(2,1)S(1)}, u32[]{:S(2)}, u32[]{:S(2)}) collective-permute-start(bf16[88,1536]{1,0:T(8,128)(2,1)S(1)} %collective-permute-done.13.refs_1_.refs_3_.refs_13_), channel_id=1, source_target_pairs={{0,32},{16,496},{32,64},{48,16},{64,96},{80,48},{96,128},{112,80},... | collective-permute-start | bytes 811016 | tf_op jit(solution)/shard_map/ppermute | solution.py:345
  77.4 8.7 %collective-permute-start.7 = (bf16[96,1536]{1,0:T(8,128)(2,1)S(1)}, bf16[96,1536]{1,0:T(8,128)(2,1)S(1)}, u32[]{:S(2)}, u32[]{:S(2)}) collective-permute-start(bf16[96,1536]{1,0:T(8,128)(2,1)S(1)} %collective-permute-done.6.refs_0_.refs_15_), channel_id=1, source_target_pairs={{0,32},{16,496},{32,64},{48,16},{64,96},{80,48},{96,128},{112,80},... | collective-permute-start | bytes 884744 | tf_op jit(solution)/shard_map/ppermute | solution.py:345
  80.6 8.7 %collective-permute-start.22 = (bf16[80,1536]{1,0:T(8,128)(2,1)S(1)}, bf16[80,1536]{1,0:T(8,128)(2,1)S(1)}, u32[]{:S(2)}, u32[]{:S(2)}) collective-permute-start(bf16[80,1536]{1,0:T(8,128)(2,1)S(1)} %collective-permute-done.21.refs_2_.refs_14_), channel_id=1, source_target_pairs={{0,32},{16,496},{32,64},{48,16},{64,96},{80,48},{96,128},{112,80},... | collective-permute-start | bytes 737288 | tf_op jit(solution)/shard_map/ppermute | solution.py:345
  83.2 8.7 %collective-permute-start.15 = (bf16[88,1536]{1,0:T(8,128)(2,1)S(1)}, bf16[88,1536]{1,0:T(8,128)(2,1)S(1)}, u32[]{:S(2)}, u32[]{:S(2)}) collective-permute-start(bf16[88,1536]{1,0:T(8,128)(2,1)S(1)} %collective-permute-done.14.refs_1_.refs_3_.refs_16_), channel_id=1, source_target_pairs={{0,32},{16,496},{32,64},{48,16},{64,96},{80,48},{96,128},{112,80},... | collective-permute-start | bytes 811016 | tf_op jit(solution)/shard_map/ppermute | solution.py:345
  86.1 12.5 %collective-permute-start.8 = (bf16[96,1536]{1,0:T(8,128)(2,1)S(1)}, bf16[96,1536]{1,0:T(8,128)(2,1)S(1)}, u32[]{:S(2)}, u32[]{:S(2)}) collective-permute-start(bf16[96,1536]{1,0:T(8,128)(2,1)S(1)} %collective-permute-done.7.refs_0_.refs_18_), channel_id=1, source_target_pairs={{0,32},{16,496},{32,64},{48,16},{64,96},{80,48},{96,128},{112,80},... | collective-permute-start | bytes 884744 | tf_op jit(solution)/shard_map/ppermute | solution.py:345
  89.3 8.8 %collective-permute-start.23 = (bf16[80,1536]{1,0:T(8,128)(2,1)S(1)}, bf16[80,1536]{1,0:T(8,128)(2,1)S(1)}, u32[]{:S(2)}, u32[]{:S(2)}) collective-permute-start(bf16[80,1536]{1,0:T(8,128)(2,1)S(1)} %collective-permute-done.22.refs_2_.refs_17_), channel_id=1, source_target_pairs={{0,32},{16,496},{32,64},{48,16},{64,96},{80,48},{96,128},{112,80},... | collective-permute-start | bytes 737288 | tf_op jit(solution)/shard_map/ppermute | solution.py:345
  91.9 6.7 %collective-permute-start.16 = (bf16[40,1536]{1,0:T(8,128)(2,1)S(1)}, bf16[40,1536]{1,0:T(8,128)(2,1)S(1)}, u32[]{:S(2)}, u32[]{:S(2)}) collective-permute-start(bf16[40,1536]{1,0:T(8,128)(2,1)S(1)} %slice.4), channel_id=1, source_target_pairs={{0,32},{16,496},{32,64},{48,16},{64,96},{80,48},{96,128},{112,80},... | collective-permute-start | bytes 368648 | tf_op jit(solution)/shard_map/ppermute | solution.py:345
  131.0 15.2 %collective-permute-start.24 = (f32[1080,128]{1,0:T(8,128)S(1)}, f32[1080,128]{1,0:T(8,128)S(1)}, u32[]{:S(2)}, u32[]{:S(2)}) collective-permute-start(f32[1080,128]{1,0:T(8,128)S(1)} %get-tuple-element.46), channel_id=1, source_target_pairs={{0,16},{16,0},{32,48},{48,32},{64,80},{80,64},{96,112},{112,96},{1... | collective-permute-start | bytes 1658888 | tf_op jit(solution)/shard_map/ppermute | solution.py:348

commit v4 on v3

--- a/solution.py
+++ b/solution.py
@@ -33,7 +33,9 @@
 
 
 def message_kernel(capacity, experts, *refs):
-    rows_hbm, ids_hbm, gates_hbm, dir_hbm, out_ref, head_ref, ids_ref, gates_ref, dir_ref, sems = refs
+    rows_hbm, ids_hbm, gates_hbm, dir_hbm = refs[:4]
+    out_ref, head_ref, keep_ref = refs[4:7]
+    ids_ref, gates_ref, dir_ref, sems = refs[7:]
     topk, tokens = ids_ref.shape
     slots = experts * capacity
     span, width = rows_hbm.shape
@@ -84,6 +86,8 @@
     out_ref[span : span + feats] = dir_ref[...]
     out_ref[span + feats : span + FEATS] = jnp.zeros((FEATS - feats, width), out_ref.dtype)
     copies[0].wait()
+    cut = head_ref.shape[0]
+    keep_ref[...] = out_ref[cut:]
     copies[3].wait()
 
 
@@ -95,9 +99,10 @@
         out_shape=[
             jax.ShapeDtypeStruct((span + TAB + FEATS, width), jnp.bfloat16),
             jax.ShapeDtypeStruct((cut, width), jnp.bfloat16),
+            pltpu.VMEM((span - cut + FEATS + TAB, width), jnp.bfloat16),
         ],
         in_specs=[pl.BlockSpec(memory_space=pltpu.HBM)] * 4,
-        out_specs=[whole(), whole()],
+        out_specs=[whole()] * 3,
         scratch_shapes=[pltpu.VMEM(x.shape, x.dtype) for x in args[1:]]
         + [pltpu.SemaphoreType.DMA((5,))],
         cost_estimate=cost(10**7, 10**6),
@@ -105,29 +110,29 @@
     )(*args)
 
 
-def split(sent, other, span, cut, join):
-    width = sent.shape[1]
+def split(keep, other, span, cut, join):
+    width = keep.shape[1]
     left = span - cut
     sizes = (join + left + TAB, span - join, 2 * FEATS)
 
-    def kernel(sent_ref, other_ref, first_ref, second_ref, dir_ref):
+    def kernel(keep_ref, other_ref, first_ref, second_ref, dir_ref):
         first_ref[:join] = other_ref[:join]
-        first_ref[join : join + left] = sent_ref[cut:span]
-        first_ref[join + left :] = sent_ref[span + FEATS :]
+        first_ref[join : join + left] = keep_ref[:left]
+        first_ref[join + left :] = keep_ref[left + FEATS :]
         first_ref[join + left :, LANES : 2 * LANES] = other_ref[span + FEATS :, :LANES]
         second_ref[...] = other_ref[join:span]
-        dir_ref[:FEATS] = sent_ref[span : span + FEATS]
+        dir_ref[:FEATS] = keep_ref[left : left + FEATS]
         dir_ref[FEATS:] = other_ref[span : span + FEATS]
 
     return pl.pallas_call(
         kernel,
-        out_shape=[jax.ShapeDtypeStruct((size, width), sent.dtype) for size in sizes],
+        out_shape=[jax.ShapeDtypeStruct((size, width), keep.dtype) for size in sizes],
         in_specs=[whole()] * 2,
         out_specs=[whole()] * 3,
         compiler_params=params(),
-        cost_estimate=cost(0, 4 * sent.size),
+        cost_estimate=cost(0, 4 * other.size),
         name="split",
-    )(sent, other)
+    )(keep, other)
 
 
 def table_of(rows, count=1):
@@ -278,28 +283,35 @@
     )(packed, mixes, *tables)
 
 
-def gradients(packed, groups, parts, feats):
+def gradients(packed, groups, parts, feats, first):
     sources, slabs, capacity, _ = packed.shape
     span = sources * capacity
     pairs = slabs // 3
     width = groups[0][0].shape[1]
     tiles = width // LANES
     step = 2 * LANES
+    half = LANES // 2
     pieces = [x for group in groups for x in group]
 
     def kernel(in_ref, *refs):
-        own_ref, other_ref, lhs_ref = refs[-3:]
+        out_ref, lhs_ref = refs[-2:]
 
         def turned(slab):
             rows = in_ref[:, slab].astype(jnp.float32).reshape(span, LANES)
             return rows.astype(jnp.bfloat16).T
 
         for pair in range(pairs):
-            lhs_ref[pair, :LANES, :span] = turned(3 * pair)
-            lhs_ref[pair, :LANES, span:] = turned(3 * pair + 1)
-            tail = turned(3 * pair + 2)
-            lhs_ref[pair, LANES:, :span] = tail[: LANES // 2]
-            lhs_ref[pair, LANES:, span:] = tail[LANES // 2 :]
+            for i in range(2):
+                columns = slice(i * span, (i + 1) * span)
+                main = turned(3 * pair + i)
+                if first:
+                    lhs_ref[pair, :, columns] = main[:FEATS]
+                else:
+                    lhs_ref[pair, : LANES - FEATS, columns] = main[FEATS:]
+            if not first:
+                tail = turned(3 * pair + 2)
+                lhs_ref[pair, LANES - FEATS :, :span] = tail[:half]
+                lhs_ref[pair, LANES - FEATS :, span:] = tail[half:]
         for column in range(width // step):
             lanes = slice(column * step, (column + 1) * step)
             total = None
@@ -312,20 +324,17 @@
                 )
                 total = term if total is None else total + term
             for i in range(2):
-                half = total[:, i * LANES : (i + 1) * LANES]
                 rows = pl.ds(2 * column + i, feats, stride=tiles)
-                own_ref[rows, :] = half[:feats]
-                other_ref[rows, :] = half[FEATS : FEATS + feats]
-
-    shape = jax.ShapeDtypeStruct((feats * tiles, LANES), jnp.float32)
-    return pl.pallas_call(
-        kernel,
-        out_shape=[shape, shape],
+                out_ref[rows, :] = total[:feats, i * LANES : (i + 1) * LANES]
+
+    return pl.pallas_call(
+        kernel,
+        out_shape=jax.ShapeDtypeStruct((feats * tiles, LANES), jnp.float32),
         in_specs=[whole()] * (1 + len(pieces)),
-        out_specs=[whole()] * 2,
-        scratch_shapes=[pltpu.VMEM((pairs, 2 * FEATS, 2 * span), jnp.bfloat16)],
-        compiler_params=params(),
-        cost_estimate=cost(4 * FEATS * 2 * span * pairs * width, 2 * 2 * span * pairs * width),
+        out_specs=whole(),
+        scratch_shapes=[pltpu.VMEM((pairs, FEATS, 2 * span), jnp.bfloat16)],
+        compiler_params=params(),
+        cost_estimate=cost(2 * FEATS * 2 * span * pairs * width, 2 * 2 * span * pairs * width),
         name="gradients",
     )(packed, *pieces)
 
@@ -350,11 +359,11 @@
     cut = span * 3 // 4
     join = span * 3 // 8
     parts = parts_of(span, cut, join)
-    sent, head = message(
+    sent, head, keep = message(
         cached_hidden, expert_ids, gate_weights, direction[0], experts, capacity, cut
     )
     other = swap(sent)
-    middle, final, dirs = split(sent, other, span, cut, join)
+    middle, final, dirs = split(keep, other, span, cut, join)
     chain = [[shift(x)] for x in (head, middle, final)]
     for s in range(2, steps + 1):
         for k in range(3 if s < steps else 2):
@@ -377,7 +386,8 @@
     arrived = lax.all_to_all(packed, "expert", split_axis=0, concat_axis=0, tiled=True)
     adjoint = combine(arrived, mixes, [middle, last[1]], scale)
     back = lax.all_to_all(adjoint, "expert", split_axis=0, concat_axis=0, tiled=True)
-    mine, theirs = gradients(back, groups, places, feats)
+    theirs = gradients(back, groups, places, feats, False)
+    mine = gradients(back, groups, places, feats, True)
     theirs = swap(theirs)
     return (mine + theirs).reshape(1, feats, width)
 

time: 148 us -> 148 us (level)
  transfers between devices with their start and end apart: 25 -> 25, of which waited for: 5 -> 4; matrix products, arithmetic and copies ran while one was open for 0% -> 0% of each run, Pallas kernels for 3% -> 3%
where the time goes in v4:
time: 148 us; the launch traced here: 147 us
  starting transfers between devices  95 us (64%)
  blocking collectives  30 us (20%)
  waiting for transfers between devices  11.2 us (8%)
  Pallas kernels  9.44 us (6%)
    ppermute x23, starting transfers between devices, shift(): return lax.ppermute(x, 'dp', ring)  72.6 us
    ppermute x2, starting transfers between devices, swap(): return lax.ppermute(x, 'dp', partner)  22.4 us
    all_to_all x1, blocking collectives, body(): lax.all_to_all(packed, 'expert', split_axis=0, concat_axis=0, tiled=True)  16.7 us
    all_to_all x1, blocking collectives, body(): lax.all_to_all(adjoint, 'expert', split_axis=0, concat_axis=0, tiled=True)  13.3 us
    ppermute x23, waiting for transfers between devices, shift(): return lax.ppermute(x, 'dp', ring)  10.8 us
    pallas_call x7, Pallas kernels, tangents(): pl.pallas_call(kernel, grid=(1,), out_shape=[jax.ShapeDtypeStruct(shape,...  3.44 us
  transfers between devices with their start and end apart: 25, of which 4 were waited for; matrix products, arithmetic and copies ran while one was open for 0% of the time, Pallas kernels for 3%

profile of v4, /device:TPU:1, one launch (start us, length us, event | category | flops | bytes accessed | tf_op | source)
XLA Modules:
  0.0 147.0 jit_solution(1132971647752058010)
XLA Ops:
  0.0 2.2 %message.1 = (bf16[232,1536]{1,0:T(8,128)(2,1)}, bf16[96,1536]{1,0:T(8,128)(2,1)}, bf16[136,1536]{1,0:T(8,128)(2,1)S(1)}) custom-call(bf16[128,1536]{1,0:T(8,128)(2,1)} %refs_21_.3, s32[4,128]{1,0:T(4,128)} %bitcast.5, f32[4,128]{1,0:T(4,128)} %bitcast.6, bf16[90,1536]{1,0:T(8,128)(2,1)} %bitcast.4), custom_call_target="tpu_custom_call" | custom-call | flops 10000000 | bytes 1000000 | tf_op jit(solution)/shard_map/message/pallas_call | solution.py:97
  2.2 8.7 %collective-permute-start = (bf16[232,1536]{1,0:T(8,128)(2,1)}, bf16[232,1536]{1,0:T(8,128)(2,1)S(1)}, u32[]{:S(2)}, u32[]{:S(2)}) collective-permute-start(bf16[232,1536]{1,0:T(8,128)(2,1)} %get-tuple-element.26), channel_id=1, source_target_pairs={{0,16},{16,0},{32,48},{48,32},{64,80},{80,64},{96,112},{112,96},{1... | collective-permute-start | bytes 2138120 | tf_op jit(solution)/shard_map/ppermute | solution.py:357
  11.0 5.8 %collective-permute-start.1 = (bf16[96,1536]{1,0:T(8,128)(2,1)}, bf16[96,1536]{1,0:T(8,128)(2,1)S(1)}, u32[]{:S(2)}, u32[]{:S(2)}) collective-permute-start(bf16[96,1536]{1,0:T(8,128)(2,1)} %get-tuple-element.28), channel_id=1, source_target_pairs={{0,32},{16,496},{32,64},{48,16},{64,96},{80,48},{96,128},{112,80},... | collective-permute-start | bytes 884744 | tf_op jit(solution)/shard_map/ppermute | solution.py:354
  16.8 4.0 %collective-permute-done.1.refs_0_ = bf16[96,1536]{1,0:T(8,128)(2,1)S(1)} collective-permute-done((bf16[96,1536]{1,0:T(8,128)(2,1)}, bf16[96,1536]{1,0:T(8,128)(2,1)S(1)}, u32[]{:S(2)}, u32[]{:S(2)}) %collective-permute-start.1) | collective-permute-done | bytes 294944 | tf_op jit(solution)/shard_map/ppermute | solution.py:354
  20.8 4.9 %collective-permute-start.2 = (bf16[96,1536]{1,0:T(8,128)(2,1)S(1)}, bf16[96,1536]{1,0:T(8,128)(2,1)S(1)}, u32[]{:S(2)}, u32[]{:S(2)}) collective-permute-start(bf16[96,1536]{1,0:T(8,128)(2,1)S(1)} %collective-permute-done.1.refs_0_), channel_id=1, source_target_pairs={{0,32},{16,496},{32,64},{48,16},{64,96},{80,48},{96,128},{112,80},... | collective-permute-start | bytes 884744 | tf_op jit(solution)/shard_map/ppermute | solution.py:354
  25.7 0.0 collective-permute-done.other_ref
  25.7 0.0 copy-start
  25.7 0.1 split.1
  25.8 2.1 %collective-permute-start.9 = (bf16[88,1536]{1,0:T(8,128)(2,1)S(1)}, bf16[88,1536]{1,0:T(8,128)(2,1)S(1)}, u32[]{:S(2)}, u32[]{:S(2)}) collective-permute-start(bf16[88,1536]{1,0:T(8,128)(2,1)S(1)} %get-tuple-element.29.refs_0_), channel_id=1, source_target_pairs={{0,32},{16,496},{32,64},{48,16},{64,96},{80,48},{96,128},{112,80},... | collective-permute-start | bytes 811016 | tf_op jit(solution)/shard_map/ppermute | solution.py:354
  27.8 1.5 %collective-permute-done.2.refs_0_.refs_3_ = bf16[96,1536]{1,0:T(8,128)(2,1)S(1)} collective-permute-done((bf16[96,1536]{1,0:T(8,128)(2,1)S(1)}, bf16[96,1536]{1,0:T(8,128)(2,1)S(1)}, u32[]{:S(2)}, u32[]{:S(2)}) %collective-permute-start.2) | collective-permute-done | bytes 294944 | tf_op jit(solution)/shard_map/ppermute | solution.py:354
  29.3 5.0 %collective-permute-start.3 = (bf16[96,1536]{1,0:T(8,128)(2,1)S(1)}, bf16[96,1536]{1,0:T(8,128)(2,1)S(1)}, u32[]{:S(2)}, u32[]{:S(2)}) collective-permute-start(bf16[96,1536]{1,0:T(8,128)(2,1)S(1)} %collective-permute-done.2.refs_0_.refs_3_), channel_id=1, source_target_pairs={{0,32},{16,496},{32,64},{48,16},{64,96},{80,48},{96,128},{112,80},... | collective-permute-start | bytes 884744 | tf_op jit(solution)/shard_map/ppermute | solution.py:354
  34.3 2.9 %collective-permute-start.10 = (bf16[88,1536]{1,0:T(8,128)(2,1)S(1)}, bf16[88,1536]{1,0:T(8,128)(2,1)S(1)}, u32[]{:S(2)}, u32[]{:S(2)}) collective-permute-start(bf16[88,1536]{1,0:T(8,128)(2,1)S(1)} %collective-permute-done.9.refs_1_.refs_3_), channel_id=1, source_target_pairs={{0,32},{16,496},{32,64},{48,16},{64,96},{80,48},{96,128},{112,80},... | collective-permute-start | bytes 811016 | tf_op jit(solution)/shard_map/ppermute | solution.py:354
  37.2 1.9 %collective-permute-start.17 = (bf16[80,1536]{1,0:T(8,128)(2,1)S(1)}, bf16[80,1536]{1,0:T(8,128)(2,1)S(1)}, u32[]{:S(2)}, u32[]{:S(2)}) collective-permute-start(bf16[80,1536]{1,0:T(8,128)(2,1)S(1)} %get-tuple-element.30), channel_id=1, source_target_pairs={{0,32},{16,496},{32,64},{48,16},{64,96},{80,48},{96,128},{112,80},... | collective-permute-start | bytes 737288 | tf_op jit(solution)/shard_map/ppermute | solution.py:354
  39.2 5.3 %collective-permute-done.17.refs_2_ = bf16[80,1536]{1,0:T(8,128)(2,1)S(1)} collective-permute-done((bf16[80,1536]{1,0:T(8,128)(2,1)S(1)}, bf16[80,1536]{1,0:T(8,128)(2,1)S(1)}, u32[]{:S(2)}, u32[]{:S(2)}) %collective-permute-start.17) | collective-permute-done | bytes 245792 | tf_op jit(solution)/shard_map/ppermute | solution.py:354
  44.5 4.0 %collective-permute-start.18 = (bf16[80,1536]{1,0:T(8,128)(2,1)S(1)}, bf16[80,1536]{1,0:T(8,128)(2,1)S(1)}, u32[]{:S(2)}, u32[]{:S(2)}) collective-permute-start(bf16[80,1536]{1,0:T(8,128)(2,1)S(1)} %collective-permute-done.17.refs_2_), channel_id=1, source_target_pairs={{0,32},{16,496},{32,64},{48,16},{64,96},{80,48},{96,128},{112,80},... | collective-permute-start | bytes 737288 | tf_op jit(solution)/shard_map/ppermute | solution.py:354
  48.5 1.9 %collective-permute-start.11 = (bf16[88,1536]{1,0:T(8,128)(2,1)S(1)}, bf16[88,1536]{1,0:T(8,128)(2,1)S(1)}, u32[]{:S(2)}, u32[]{:S(2)}) collective-permute-start(bf16[88,1536]{1,0:T(8,128)(2,1)S(1)} %collective-permute-done.10.refs_1_.refs_3_.refs_4_), channel_id=1, source_target_pairs={{0,32},{16,496},{32,64},{48,16},{64,96},{80,48},{96,128},{112,80},... | collective-permute-start | bytes 811016 | tf_op jit(solution)/shard_map/ppermute | solution.py:354
  50.5 2.9 %collective-permute-start.4 = (bf16[96,1536]{1,0:T(8,128)(2,1)S(1)}, bf16[96,1536]{1,0:T(8,128)(2,1)S(1)}, u32[]{:S(2)}, u32[]{:S(2)}) collective-permute-start(bf16[96,1536]{1,0:T(8,128)(2,1)S(1)} %collective-permute-done.3.refs_0_.refs_6_), channel_id=1, source_target_pairs={{0,32},{16,496},{32,64},{48,16},{64,96},{80,48},{96,128},{112,80},... | collective-permute-start | bytes 884744 | tf_op jit(solution)/shard_map/ppermute | solution.py:354
  53.4 3.3 %collective-permute-start.19 = (bf16[80,1536]{1,0:T(8,128)(2,1)S(1)}, bf16[80,1536]{1,0:T(8,128)(2,1)S(1)}, u32[]{:S(2)}, u32[]{:S(2)}) collective-permute-start(bf16[80,1536]{1,0:T(8,128)(2,1)S(1)} %collective-permute-done.18.refs_2_.refs_5_), channel_id=1, source_target_pairs={{0,32},{16,496},{32,64},{48,16},{64,96},{80,48},{96,128},{112,80},... | collective-permute-start | bytes 737288 | tf_op jit(solution)/shard_map/ppermute | solution.py:354
  56.7 3.7 %collective-permute-start.12 = (bf16[88,1536]{1,0:T(8,128)(2,1)S(1)}, bf16[88,1536]{1,0:T(8,128)(2,1)S(1)}, u32[]{:S(2)}, u32[]{:S(2)}) collective-permute-start(bf16[88,1536]{1,0:T(8,128)(2,1)S(1)} %collective-permute-done.11.refs_1_.refs_3_.refs_7_), channel_id=1, source_target_pairs={{0,32},{16,496},{32,64},{48,16},{64,96},{80,48},{96,128},{112,80},... | collective-permute-start | bytes 811016 | tf_op jit(solution)/shard_map/ppermute | solution.py:354
  60.4 2.4 %collective-permute-start.5 = (bf16[96,1536]{1,0:T(8,128)(2,1)S(1)}, bf16[96,1536]{1,0:T(8,128)(2,1)S(1)}, u32[]{:S(2)}, u32[]{:S(2)}) collective-permute-start(bf16[96,1536]{1,0:T(8,128)(2,1)S(1)} %collective-permute-done.4.refs_0_.refs_9_), channel_id=1, source_target_pairs={{0,32},{16,496},{32,64},{48,16},{64,96},{80,48},{96,128},{112,80},... | collective-permute-start | bytes 884744 | tf_op jit(solution)/shard_map/ppermute | solution.py:354
  62.7 2.6 %collective-permute-start.20 = (bf16[80,1536]{1,0:T(8,128)(2,1)S(1)}, bf16[80,1536]{1,0:T(8,128)(2,1)S(1)}, u32[]{:S(2)}, u32[]{:S(2)}) collective-permute-start(bf16[80,1536]{1,0:T(8,128)(2,1)S(1)} %collective-permute-done.19.refs_2_.refs_8_), channel_id=1, source_target_pairs={{0,32},{16,496},{32,64},{48,16},{64,96},{80,48},{96,128},{112,80},... | collective-permute-start | bytes 737288 | tf_op jit(solution)/shard_map/ppermute | solution.py:354
  65.4 3.4 %collective-permute-start.13 = (bf16[88,1536]{1,0:T(8,128)(2,1)S(1)}, bf16[88,1536]{1,0:T(8,128)(2,1)S(1)}, u32[]{:S(2)}, u32[]{:S(2)}) collective-permute-start(bf16[88,1536]{1,0:T(8,128)(2,1)S(1)} %collective-permute-done.12.refs_1_.refs_3_.refs_10_), channel_id=1, source_target_pairs={{0,32},{16,496},{32,64},{48,16},{64,96},{80,48},{96,128},{112,80},... | collective-permute-start | bytes 811016 | tf_op jit(solution)/shard_map/ppermute | solution.py:354
  68.8 3.1 %collective-permute-start.6 = (bf16[96,1536]{1,0:T(8,128)(2,1)S(1)}, bf16[96,1536]{1,0:T(8,128)(2,1)S(1)}, u32[]{:S(2)}, u32[]{:S(2)}) collective-permute-start(bf16[96,1536]{1,0:T(8,128)(2,1)S(1)} %collective-permute-done.5.refs_0_.refs_12_), channel_id=1, source_target_pairs={{0,32},{16,496},{32,64},{48,16},{64,96},{80,48},{96,128},{112,80},... | collective-permute-start | bytes 884744 | tf_op jit(solution)/shard_map/ppermute | solution.py:354
  71.9 2.6 %collective-permute-start.21 = (bf16[80,1536]{1,0:T(8,128)(2,1)S(1)}, bf16[80,1536]{1,0:T(8,128)(2,1)S(1)}, u32[]{:S(2)}, u32[]{:S(2)}) collective-permute-start(bf16[80,1536]{1,0:T(8,128)(2,1)S(1)} %collective-permute-done.20.refs_2_.refs_11_), channel_id=1, source_target_pairs={{0,32},{16,496},{32,64},{48,16},{64,96},{80,48},{96,128},{112,80},... | collective-permute-start | bytes 737288 | tf_op jit(solution)/shard_map/ppermute | solution.py:354
  74.6 2.9 %collective-permute-start.14 = (bf16[88,1536]{1,0:T(8,128)(2,1)S(1)}, bf16[88,1536]{1,0:T(8,128)(2,1)S(1)}, u32[]{:S(2)}, u32[]{:S(2)}) collective-permute-start(bf16[88,1536]{1,0:T(8,128)(2,1)S(1)} %collective-permute-done.13.refs_1_.refs_3_.refs_13_), channel_id=1, source_target_pairs={{0,32},{16,496},{32,64},{48,16},{64,96},{80,48},{96,128},{112,80},... | collective-permute-start | bytes 811016 | tf_op jit(solution)/shard_map/ppermute | solution.py:354
  77.5 3.1 %collective-permute-start.7 = (bf16[96,1536]{1,0:T(8,128)(2,1)S(1)}, bf16[96,1536]{1,0:T(8,128)(2,1)S(1)}, u32[]{:S(2)}, u32[]{:S(2)}) collective-permute-start(bf16[96,1536]{1,0:T(8,128)(2,1)S(1)} %collective-permute-done.6.refs_0_.refs_15_), channel_id=1, source_target_pairs={{0,32},{16,496},{32,64},{48,16},{64,96},{80,48},{96,128},{112,80},... | collective-permute-start | bytes 884744 | tf_op jit(solution)/shard_map/ppermute | solution.py:354
  80.6 2.6 %collective-permute-start.22 = (bf16[80,1536]{1,0:T(8,128)(2,1)S(1)}, bf16[80,1536]{1,0:T(8,128)(2,1)S(1)}, u32[]{:S(2)}, u32[]{:S(2)}) collective-permute-start(bf16[80,1536]{1,0:T(8,128)(2,1)S(1)} %collective-permute-done.21.refs_2_.refs_14_), channel_id=1, source_target_pairs={{0,32},{16,496},{32,64},{48,16},{64,96},{80,48},{96,128},{112,80},... | collective-permute-start | bytes 737288 | tf_op jit(solution)/shard_map/ppermute | solution.py:354
  83.3 2.9 %collective-permute-start.15 = (bf16[88,1536]{1,0:T(8,128)(2,1)S(1)}, bf16[88,1536]{1,0:T(8,128)(2,1)S(1)}, u32[]{:S(2)}, u32[]{:S(2)}) collective-permute-start(bf16[88,1536]{1,0:T(8,128)(2,1)S(1)} %collective-permute-done.14.refs_1_.refs_3_.refs_16_), channel_id=1, source_target_pairs={{0,32},{16,496},{32,64},{48,16},{64,96},{80,48},{96,128},{112,80},... | collective-permute-start | bytes 811016 | tf_op jit(solution)/shard_map/ppermute | solution.py:354
  86.2 3.1 %collective-permute-start.8 = (bf16[96,1536]{1,0:T(8,128)(2,1)S(1)}, bf16[96,1536]{1,0:T(8,128)(2,1)S(1)}, u32[]{:S(2)}, u32[]{:S(2)}) collective-permute-start(bf16[96,1536]{1,0:T(8,128)(2,1)S(1)} %collective-permute-done.7.refs_0_.refs_18_), channel_id=1, source_target_pairs={{0,32},{16,496},{32,64},{48,16},{64,96},{80,48},{96,128},{112,80},... | collective-permute-start | bytes 884744 | tf_op jit(solution)/shard_map/ppermute | solution.py:354
  89.3 2.6 %collective-permute-start.23 = (bf16[80,1536]{1,0:T(8,128)(2,1)S(1)}, bf16[80,1536]{1,0:T(8,128)(2,1)S(1)}, u32[]{:S(2)}, u32[]{:S(2)}) collective-permute-start(bf16[80,1536]{1,0:T(8,128)(2,1)S(1)} %collective-permute-done.22.refs_2_.refs_17_), channel_id=1, source_target_pairs={{0,32},{16,496},{32,64},{48,16},{64,96},{80,48},{96,128},{112,80},... | collective-permute-start | bytes 737288 | tf_op jit(solution)/shard_map/ppermute | solution.py:354
  92.0 2.9 %collective-permute-start.16 = (bf16[40,1536]{1,0:T(8,128)(2,1)S(1)}, bf16[40,1536]{1,0:T(8,128)(2,1)S(1)}, u32[]{:S(2)}, u32[]{:S(2)}) collective-permute-start(bf16[40,1536]{1,0:T(8,128)(2,1)S(1)} %slice.4), channel_id=1, source_target_pairs={{0,32},{16,496},{32,64},{48,16},{64,96},{80,48},{96,128},{112,80},... | collective-permute-start | bytes 368648 | tf_op jit(solution)/shard_map/ppermute | solution.py:354
  94.9 0.3 own_tangents.1.own_ref
  95.2 0.5 tangents.7
  95.7 0.5 tangents.8
  96.2 0.5 tangents.9
  96.7 0.5 tangents.10
  97.2 0.5 tangents.11
  97.7 0.5 tangents.12
  98.2 0.5 tangents.13
  98.7 0.4 last_tangents.1
  99.1 16.7 %all_to_all.10.in_ref = bf16[16,24,8,128]{3,2,1,0:T(8,128)(2,1)S(1)} all-to-all(bf16[16,24,8,128]{3,2,1,0:T(8,128)(2,1)S(1)} %last_tangents.1), channel_id=1, replica_groups=mesh['dp'=32,'expert'=16] {'expert'}, dimensions={0} | all-to-all | bytes 1572864 | tf_op jit(solution)/shard_map/all_to_all | solution.py:386
  115.8 0.5 combine.1
  116.3 13.3 %all_to_all.11.in_ref = bf16[16,24,8,128]{3,2,1,0:T(8,128)(2,1)S(1)} all-to-all(bf16[16,24,8,128]{3,2,1,0:T(8,128)(2,1)S(1)} %combine.1), channel_id=1, replica_groups=mesh['dp'=32,'expert'=16] {'expert'}, dimensions={0} | all-to-all | bytes 1572864 | tf_op jit(solution)/shard_map/all_to_all | solution.py:388
  129.6 1.3 gradients.3
  130.9 13.7 %collective-permute-start.24 = (f32[1080,128]{1,0:T(8,128)S(1)}, f32[1080,128]{1,0:T(8,128)S(1)}, u32[]{:S(2)}, u32[]{:S(2)}) collective-permute-start(f32[1080,128]{1,0:T(8,128)S(1)} %gradients.3), channel_id=1, source_target_pairs={{0,16},{16,0},{32,48},{48,32},{64,80},{80,64},{96,112},{112,96},{1... | collective-permute-start | bytes 1658888 | tf_op jit(solution)/shard_map/ppermute | solution.py:357
  144.6 1.2 gradients.2
  145.8 0.4 collective-permute-done.24
  146.1 0.9 add.3
  (22 shorter events, 0.1 us)
Async XLA Ops:
  2.2 23.4 %collective-permute-start = (bf16[232,1536]{1,0:T(8,128)(2,1)}, bf16[232,1536]{1,0:T(8,128)(2,1)S(1)}, u32[]{:S(2)}, u32[]{:S(2)}) collective-permute-start(bf16[232,1536]{1,0:T(8,128)(2,1)} %get-tuple-element.26), channel_id=1, source_target_pairs={{0,16},{16,0},{32,48},{48,32},{64,80},{80,64},{96,112},{112,96},{1... | collective-permute-start | bytes 2138120 | tf_op jit(solution)/shard_map/ppermute | solution.py:357
  11.0 9.7 %collective-permute-start.1 = (bf16[96,1536]{1,0:T(8,128)(2,1)}, bf16[96,1536]{1,0:T(8,128)(2,1)S(1)}, u32[]{:S(2)}, u32[]{:S(2)}) collective-permute-start(bf16[96,1536]{1,0:T(8,128)(2,1)} %get-tuple-element.28), channel_id=1, source_target_pairs={{0,32},{16,496},{32,64},{48,16},{64,96},{80,48},{96,128},{112,80},... | collective-permute-start | bytes 884744 | tf_op jit(solution)/shard_map/ppermute | solution.py:354
  20.8 8.6 %collective-permute-start.2 = (bf16[96,1536]{1,0:T(8,128)(2,1)S(1)}, bf16[96,1536]{1,0:T(8,128)(2,1)S(1)}, u32[]{:S(2)}, u32[]{:S(2)}) collective-permute-start(bf16[96,1536]{1,0:T(8,128)(2,1)S(1)} %collective-permute-done.1.refs_0_), channel_id=1, source_target_pairs={{0,32},{16,496},{32,64},{48,16},{64,96},{80,48},{96,128},{112,80},... | collective-permute-start | bytes 884744 | tf_op jit(solution)/shard_map/ppermute | solution.py:354
  25.7 69.2 %copy-start = (bf16[128,1536]{1,0:T(8,128)(2,1)S(1)}, bf16[128,1536]{1,0:T(8,128)(2,1)}, u32[]{:S(2)}) copy-start(bf16[128,1536]{1,0:T(8,128)(2,1)} %refs_21_.3) | copy-start | bytes 1179652
  25.8 8.6 %collective-permute-start.9 = (bf16[88,1536]{1,0:T(8,128)(2,1)S(1)}, bf16[88,1536]{1,0:T(8,128)(2,1)S(1)}, u32[]{:S(2)}, u32[]{:S(2)}) collective-permute-start(bf16[88,1536]{1,0:T(8,128)(2,1)S(1)} %get-tuple-element.29.refs_0_), channel_id=1, source_target_pairs={{0,32},{16,496},{32,64},{48,16},{64,96},{80,48},{96,128},{112,80},... | collective-permute-start | bytes 811016 | tf_op jit(solution)/shard_map/ppermute | solution.py:354
  29.3 21.2 %collective-permute-start.3 = (bf16[96,1536]{1,0:T(8,128)(2,1)S(1)}, bf16[96,1536]{1,0:T(8,128)(2,1)S(1)}, u32[]{:S(2)}, u32[]{:S(2)}) collective-permute-start(bf16[96,1536]{1,0:T(8,128)(2,1)S(1)} %collective-permute-done.2.refs_0_.refs_3_), channel_id=1, source_target_pairs={{0,32},{16,496},{32,64},{48,16},{64,96},{80,48},{96,128},{112,80},... | collective-permute-start | bytes 884744 | tf_op jit(solution)/shard_map/ppermute | solution.py:354
  34.3 14.2 %collective-permute-start.10 = (bf16[88,1536]{1,0:T(8,128)(2,1)S(1)}, bf16[88,1536]{1,0:T(8,128)(2,1)S(1)}, u32[]{:S(2)}, u32[]{:S(2)}) collective-permute-start(bf16[88,1536]{1,0:T(8,128)(2,1)S(1)} %collective-permute-done.9.refs_1_.refs_3_), channel_id=1, source_target_pairs={{0,32},{16,496},{32,64},{48,16},{64,96},{80,48},{96,128},{112,80},... | collective-permute-start | bytes 811016 | tf_op jit(solution)/shard_map/ppermute | solution.py:354
  37.2 7.2 %collective-permute-start.17 = (bf16[80,1536]{1,0:T(8,128)(2,1)S(1)}, bf16[80,1536]{1,0:T(8,128)(2,1)S(1)}, u32[]{:S(2)}, u32[]{:S(2)}) collective-permute-start(bf16[80,1536]{1,0:T(8,128)(2,1)S(1)} %get-tuple-element.30), channel_id=1, source_target_pairs={{0,32},{16,496},{32,64},{48,16},{64,96},{80,48},{96,128},{112,80},... | collective-permute-start | bytes 737288 | tf_op jit(solution)/shard_map/ppermute | solution.py:354
  44.5 8.9 %collective-permute-start.18 = (bf16[80,1536]{1,0:T(8,128)(2,1)S(1)}, bf16[80,1536]{1,0:T(8,128)(2,1)S(1)}, u32[]{:S(2)}, u32[]{:S(2)}) collective-permute-start(bf16[80,1536]{1,0:T(8,128)(2,1)S(1)} %collective-permute-done.17.refs_2_), channel_id=1, source_target_pairs={{0,32},{16,496},{32,64},{48,16},{64,96},{80,48},{96,128},{112,80},... | collective-permute-start | bytes 737288 | tf_op jit(solution)/shard_map/ppermute | solution.py:354
  48.5 8.1 %collective-permute-start.11 = (bf16[88,1536]{1,0:T(8,128)(2,1)S(1)}, bf16[88,1536]{1,0:T(8,128)(2,1)S(1)}, u32[]{:S(2)}, u32[]{:S(2)}) collective-permute-start(bf16[88,1536]{1,0:T(8,128)(2,1)S(1)} %collective-permute-done.10.refs_1_.refs_3_.refs_4_), channel_id=1, source_target_pairs={{0,32},{16,496},{32,64},{48,16},{64,96},{80,48},{96,128},{112,80},... | collective-permute-start | bytes 811016 | tf_op jit(solution)/shard_map/ppermute | solution.py:354
  50.5 9.9 %collective-permute-start.4 = (bf16[96,1536]{1,0:T(8,128)(2,1)S(1)}, bf16[96,1536]{1,0:T(8,128)(2,1)S(1)}, u32[]{:S(2)}, u32[]{:S(2)}) collective-permute-start(bf16[96,1536]{1,0:T(8,128)(2,1)S(1)} %collective-permute-done.3.refs_0_.refs_6_), channel_id=1, source_target_pairs={{0,32},{16,496},{32,64},{48,16},{64,96},{80,48},{96,128},{112,80},... | collective-permute-start | bytes 884744 | tf_op jit(solution)/shard_map/ppermute | solution.py:354
  53.4 9.3 %collective-permute-start.19 = (bf16[80,1536]{1,0:T(8,128)(2,1)S(1)}, bf16[80,1536]{1,0:T(8,128)(2,1)S(1)}, u32[]{:S(2)}, u32[]{:S(2)}) collective-permute-start(bf16[80,1536]{1,0:T(8,128)(2,1)S(1)} %collective-permute-done.18.refs_2_.refs_5_), channel_id=1, source_target_pairs={{0,32},{16,496},{32,64},{48,16},{64,96},{80,48},{96,128},{112,80},... | collective-permute-start | bytes 737288 | tf_op jit(solution)/shard_map/ppermute | solution.py:354
  56.7 8.7 %collective-permute-start.12 = (bf16[88,1536]{1,0:T(8,128)(2,1)S(1)}, bf16[88,1536]{1,0:T(8,128)(2,1)S(1)}, u32[]{:S(2)}, u32[]{:S(2)}) collective-permute-start(bf16[88,1536]{1,0:T(8,128)(2,1)S(1)} %collective-permute-done.11.refs_1_.refs_3_.refs_7_), channel_id=1, source_target_pairs={{0,32},{16,496},{32,64},{48,16},{64,96},{80,48},{96,128},{112,80},... | collective-permute-start | bytes 811016 | tf_op jit(solution)/shard_map/ppermute | solution.py:354
  60.4 8.4 %collective-permute-start.5 = (bf16[96,1536]{1,0:T(8,128)(2,1)S(1)}, bf16[96,1536]{1,0:T(8,128)(2,1)S(1)}, u32[]{:S(2)}, u32[]{:S(2)}) collective-permute-start(bf16[96,1536]{1,0:T(8,128)(2,1)S(1)} %collective-permute-done.4.refs_0_.refs_9_), channel_id=1, source_target_pairs={{0,32},{16,496},{32,64},{48,16},{64,96},{80,48},{96,128},{112,80},... | collective-permute-start | bytes 884744 | tf_op jit(solution)/shard_map/ppermute | solution.py:354
  62.7 9.2 %collective-permute-start.20 = (bf16[80,1536]{1,0:T(8,128)(2,1)S(1)}, bf16[80,1536]{1,0:T(8,128)(2,1)S(1)}, u32[]{:S(2)}, u32[]{:S(2)}) collective-permute-start(bf16[80,1536]{1,0:T(8,128)(2,1)S(1)} %collective-permute-done.19.refs_2_.refs_8_), channel_id=1, source_target_pairs={{0,32},{16,496},{32,64},{48,16},{64,96},{80,48},{96,128},{112,80},... | collective-permute-start | bytes 737288 | tf_op jit(solution)/shard_map/ppermute | solution.py:354
  65.4 9.2 %collective-permute-start.13 = (bf16[88,1536]{1,0:T(8,128)(2,1)S(1)}, bf16[88,1536]{1,0:T(8,128)(2,1)S(1)}, u32[]{:S(2)}, u32[]{:S(2)}) collective-permute-start(bf16[88,1536]{1,0:T(8,128)(2,1)S(1)} %collective-permute-done.12.refs_1_.refs_3_.refs_10_), channel_id=1, source_target_pairs={{0,32},{16,496},{32,64},{48,16},{64,96},{80,48},{96,128},{112,80},... | collective-permute-start | bytes 811016 | tf_op jit(solution)/shard_map/ppermute | solution.py:354
  68.8 8.7 %collective-permute-start.6 = (bf16[96,1536]{1,0:T(8,128)(2,1)S(1)}, bf16[96,1536]{1,0:T(8,128)(2,1)S(1)}, u32[]{:S(2)}, u32[]{:S(2)}) collective-permute-start(bf16[96,1536]{1,0:T(8,128)(2,1)S(1)} %collective-permute-done.5.refs_0_.refs_12_), channel_id=1, source_target_pairs={{0,32},{16,496},{32,64},{48,16},{64,96},{80,48},{96,128},{112,80},... | collective-permute-start | bytes 884744 | tf_op jit(solution)/shard_map/ppermute | solution.py:354
  71.9 8.7 %collective-permute-start.21 = (bf16[80,1536]{1,0:T(8,128)(2,1)S(1)}, bf16[80,1536]{1,0:T(8,128)(2,1)S(1)}, u32[]{:S(2)}, u32[]{:S(2)}) collective-permute-start(bf16[80,1536]{1,0:T(8,128)(2,1)S(1)} %collective-permute-done.20.refs_2_.refs_11_), channel_id=1, source_target_pairs={{0,32},{16,496},{32,64},{48,16},{64,96},{80,48},{96,128},{112,80},... | collective-permute-start | bytes 737288 | tf_op jit(solution)/shard_map/ppermute | solution.py:354
  74.6 8.7 %collective-permute-start.14 = (bf16[88,1536]{1,0:T(8,128)(2,1)S(1)}, bf16[88,1536]{1,0:T(8,128)(2,1)S(1)}, u32[]{:S(2)}, u32[]{:S(2)}) collective-permute-start(bf16[88,1536]{1,0:T(8,128)(2,1)S(1)} %collective-permute-done.13.refs_1_.refs_3_.refs_13_), channel_id=1, source_target_pairs={{0,32},{16,496},{32,64},{48,16},{64,96},{80,48},{96,128},{112,80},... | collective-permute-start | bytes 811016 | tf_op jit(solution)/shard_map/ppermute | solution.py:354
  77.5 8.7 %collective-permute-start.7 = (bf16[96,1536]{1,0:T(8,128)(2,1)S(1)}, bf16[96,1536]{1,0:T(8,128)(2,1)S(1)}, u32[]{:S(2)}, u32[]{:S(2)}) collective-permute-start(bf16[96,1536]{1,0:T(8,128)(2,1)S(1)} %collective-permute-done.6.refs_0_.refs_15_), channel_id=1, source_target_pairs={{0,32},{16,496},{32,64},{48,16},{64,96},{80,48},{96,128},{112,80},... | collective-permute-start | bytes 884744 | tf_op jit(solution)/shard_map/ppermute | solution.py:354
  80.6 8.7 %collective-permute-start.22 = (bf16[80,1536]{1,0:T(8,128)(2,1)S(1)}, bf16[80,1536]{1,0:T(8,128)(2,1)S(1)}, u32[]{:S(2)}, u32[]{:S(2)}) collective-permute-start(bf16[80,1536]{1,0:T(8,128)(2,1)S(1)} %collective-permute-done.21.refs_2_.refs_14_), channel_id=1, source_target_pairs={{0,32},{16,496},{32,64},{48,16},{64,96},{80,48},{96,128},{112,80},... | collective-permute-start | bytes 737288 | tf_op jit(solution)/shard_map/ppermute | solution.py:354
  83.3 8.7 %collective-permute-start.15 = (bf16[88,1536]{1,0:T(8,128)(2,1)S(1)}, bf16[88,1536]{1,0:T(8,128)(2,1)S(1)}, u32[]{:S(2)}, u32[]{:S(2)}) collective-permute-start(bf16[88,1536]{1,0:T(8,128)(2,1)S(1)} %collective-permute-done.14.refs_1_.refs_3_.refs_16_), channel_id=1, source_target_pairs={{0,32},{16,496},{32,64},{48,16},{64,96},{80,48},{96,128},{112,80},... | collective-permute-start | bytes 811016 | tf_op jit(solution)/shard_map/ppermute | solution.py:354
  86.2 12.5 %collective-permute-start.8 = (bf16[96,1536]{1,0:T(8,128)(2,1)S(1)}, bf16[96,1536]{1,0:T(8,128)(2,1)S(1)}, u32[]{:S(2)}, u32[]{:S(2)}) collective-permute-start(bf16[96,1536]{1,0:T(8,128)(2,1)S(1)} %collective-permute-done.7.refs_0_.refs_18_), channel_id=1, source_target_pairs={{0,32},{16,496},{32,64},{48,16},{64,96},{80,48},{96,128},{112,80},... | collective-permute-start | bytes 884744 | tf_op jit(solution)/shard_map/ppermute | solution.py:354
  89.3 8.9 %collective-permute-start.23 = (bf16[80,1536]{1,0:T(8,128)(2,1)S(1)}, bf16[80,1536]{1,0:T(8,128)(2,1)S(1)}, u32[]{:S(2)}, u32[]{:S(2)}) collective-permute-start(bf16[80,1536]{1,0:T(8,128)(2,1)S(1)} %collective-permute-done.22.refs_2_.refs_17_), channel_id=1, source_target_pairs={{0,32},{16,496},{32,64},{48,16},{64,96},{80,48},{96,128},{112,80},... | collective-permute-start | bytes 737288 | tf_op jit(solution)/shard_map/ppermute | solution.py:354
  92.0 6.7 %collective-permute-start.16 = (bf16[40,1536]{1,0:T(8,128)(2,1)S(1)}, bf16[40,1536]{1,0:T(8,128)(2,1)S(1)}, u32[]{:S(2)}, u32[]{:S(2)}) collective-permute-start(bf16[40,1536]{1,0:T(8,128)(2,1)S(1)} %slice.4), channel_id=1, source_target_pairs={{0,32},{16,496},{32,64},{48,16},{64,96},{80,48},{96,128},{112,80},... | collective-permute-start | bytes 368648 | tf_op jit(solution)/shard_map/ppermute | solution.py:354
  130.9 15.2 %collective-permute-start.24 = (f32[1080,128]{1,0:T(8,128)S(1)}, f32[1080,128]{1,0:T(8,128)S(1)}, u32[]{:S(2)}, u32[]{:S(2)}) collective-permute-start(f32[1080,128]{1,0:T(8,128)S(1)} %gradients.3), channel_id=1, source_target_pairs={{0,16},{16,0},{32,48},{48,32},{64,80},{80,64},{96,112},{112,96},{1... | collective-permute-start | bytes 1658888 | tf_op jit(solution)/shard_map/ppermute | solution.py:357
